TPU v7x, 32 devices: a whole 2x2x4 slice. The times are simulated.
32 devices in a mesh: dp: 16 (over z, y, x), tensor: 2 (over core).
Axes of the slice: x: 2, y: 2, z: 4, core: 2. Of those that a mesh axis runs over, the one named last changes fastest.
Arguments:
- tokens: bfloat16 [16384, 768], P('dp'), may hold values from -6 to 6
- token_slot: int32 [16, 1024], P('dp'), may hold values from 0 to 1023, each once within a row
- seq_lengths: int32 [16, 4], P('dp'), may hold values from 1 to 512, 1024 in all within a row
- query_weight: bfloat16 [768, 768], P(None, 'tensor'), may hold values from -0.3125 to 0.3125
- query_bias: float32 [768], P('tensor'), may hold values from -3 to 3
- key_weight: bfloat16 [768, 768], P(None, 'tensor'), may hold values from -0.3125 to 0.3125
- value_weight: bfloat16 [768, 768], P(None, 'tensor'), may hold values from -0.21875 to 0.21875
- value_bias: float32 [768], P('tensor'), may hold values from -3 to 3
- out_weight: bfloat16 [768, 768], P('tensor'), may hold values from -1.25 to 1.25
- out_bias: float32 [768], replicated, may hold values from -3 to 3
- first_gain: float32 [768], replicated, may hold values from 0.25 to 1.75
- first_shift: float32 [768], replicated, may hold values from -3 to 3
- up_weight: bfloat16 [768, 3072], P(None, 'tensor'), may hold values from -0.21875 to 0.21875
- up_bias: float32 [3072], P('tensor'), may hold values from -3 to 3
- down_weight: bfloat16 [3072, 768], P('tensor'), may hold values from -0.109375 to 0.109375
- down_bias: float32 [768], replicated, may hold values from -3 to 3
- second_gain: float32 [768], replicated, may hold values from 0.25 to 1.75
- second_shift: float32 [768], replicated, may hold values from -3 to 3
- cotangent: bfloat16 [16384, 768], P('dp'), may hold values from -6 to 6
Outputs:
- layer_out: bfloat16 [16384, 768], P('dp')
- input_gradient: bfloat16 [16384, 768], P('dp')
- query_weight_gradient: float32 [768, 768], P('dp', 'tensor')
- query_bias_gradient: float32 [768], P(('dp', 'tensor'))
- key_weight_gradient: float32 [768, 768], P('dp', 'tensor')
- value_weight_gradient: float32 [768, 768], P('dp', 'tensor')
- value_bias_gradient: float32 [768], P(('dp', 'tensor'))
- out_weight_gradient: float32 [768, 768], P('tensor', 'dp')
- out_bias_gradient: float32 [768], P(('dp', 'tensor'))
- first_gain_gradient: float32 [768], P(('dp', 'tensor'))
- first_shift_gradient: float32 [768], P(('dp', 'tensor'))
- up_weight_gradient: float32 [768, 3072], P('dp', 'tensor')
- up_bias_gradient: float32 [3072], P(('dp', 'tensor'))
- down_weight_gradient: float32 [3072, 768], P('tensor', 'dp')
- down_bias_gradient: float32 [768], P(('dp', 'tensor'))
- second_gain_gradient: float32 [768], P(('dp', 'tensor'))
- second_shift_gradient: float32 [768], P(('dp', 'tensor'))
Inputs may be any that keep to these rules, and one draw needn't show every extreme that they name: `token_slot`: each row orders the 1024 rows that one group receives. `seq_lengths`: each row holds one group's 4 sequence lengths in order; they sum to 1024 and the longest is 512.
All inputs are finite; a program needn't handle non-finite values.
Results may differ from a plain program's by a relative error of at most 0.015.
The roundings to bfloat16 on the way count: a program that leaves them out, or rounds other values in their place, can miss the bound.
Values may be sent and summed in bfloat16 or wider, within the bound.
No kernel may reach another device: no remote copies, remote signals or barrier semaphores. Data moves between devices by JAX's collectives and lax.ppermute only.
A program may use at most 192 MiB of HBM per device.

v0:
```python
import functools
import jax
import jax.numpy as jnp
from jax import lax
from jax.experimental import pallas as pl
from jax.experimental.pallas import tpu as pltpu
from jax.sharding import PartitionSpec as P

HD = 64
LANES = 128
SEG_MAX = 8
FORWARD_ROWS = 512
FORWARD_KEYS = 512
QB = 256
KB = 256
ROW_TILE = 64


EPSILON = 1e-12
MASKED = -1e30
F32 = jnp.float32
BF16 = jnp.bfloat16
SWAP = [(0, 1), (1, 0)]
VMEM_LIMIT = 60 << 20


def swap(values):
    return lax.ppermute(values, "tensor", SWAP)


def nt(a, b):
    return lax.dot_general(a, b, (((1,), (1,)), ((), ())), preferred_element_type=F32)


def nn(a, b):
    return jnp.dot(a, b, preferred_element_type=F32)


def segment_ends(lengths):
    ends, end = [], jnp.int32(0)
    for n in range(lengths.shape[1]):
        end = end + lengths[0, n]
        ends.append(end)
    return ends


def bounds(ends, rows, first, last):
    low, high = jnp.int32(0), jnp.int32(rows)
    for end in ends:
        low = jnp.where(end <= first, jnp.maximum(low, end), low)
        high = jnp.where(end > last, jnp.minimum(high, end), high)
    return low, high


def lane_bounds(ends, rows):
    lane = lax.broadcasted_iota(jnp.int32, (1, LANES), 1)
    start = jnp.full((1, LANES), 2 * rows, jnp.int32)
    stop = jnp.zeros((1, LANES), jnp.int32)
    begin = 0
    for n, end in enumerate(ends):
        start = jnp.where(lane == n, begin, start)
        stop = jnp.where(lane == n, end, stop)
        begin = end
    return start, stop


def key_marks(ends, rows, offset):
    start, stop = lane_bounds(ends, rows)
    pos = lax.broadcasted_iota(jnp.int32, (rows, LANES), 0) + offset
    pos = jnp.where(pos >= rows, pos - rows, pos)
    return ((pos >= start) & (pos < stop)).astype(F32).astype(BF16)


def query_marks(ends, rows, first, count):
    start, stop = lane_bounds(ends, rows)
    lane = lax.broadcasted_iota(jnp.int32, (1, LANES), 1)
    pos = lax.broadcasted_iota(jnp.int32, (count, LANES), 0) + first
    return jnp.where((lane < len(ends)) & ((pos < start) | (pos >= stop)), MASKED, 0.0)


def lane_mask(half):
    lane = lax.broadcasted_iota(jnp.int32, (1, LANES), 1)
    return ((lane // HD) == half).astype(F32).astype(BF16)


def of_pair(h):
    return slice(h // 2 * LANES, (h // 2 + 1) * LANES)


def forward_kernel(
    lengths, core, q_ref, k_ref, v_ref, o_mine, o_other, lse_ref, keys, values_t, mixed, peaks, totals
):
    rows, width = k_ref.shape
    heads = width // HD
    step = pl.program_id(0)
    ends = segment_ends(lengths)
    offset = core[0] * (rows // 2)

    @pl.when(step == 0)
    def _():
        marks = key_marks(ends, rows, offset)
        for p in range(heads // 2):
            keys[p, :, :LANES] = k_ref[:, of_pair(2 * p)]
            keys[p, :, LANES:] = marks
        for block in range(rows // FORWARD_KEYS):
            at = slice(block * FORWARD_KEYS, (block + 1) * FORWARD_KEYS)
            values_t[block] = v_ref[at, :].astype(F32).T.astype(BF16)

    first = lax.rem(step * FORWARD_ROWS + offset, rows)
    low, high = bounds(ends, rows, first, first + FORWARD_ROWS - 1)
    block_low, block_high = low // FORWARD_KEYS, (high + FORWARD_KEYS - 1) // FORWARD_KEYS
    marked = query_marks(ends, rows, first, FORWARD_ROWS).astype(BF16)
    queries = []
    for p in range(heads // 2):
        query = q_ref[:, of_pair(2 * p)] * BF16(HD**-0.5)
        both = [jnp.concatenate([query * lane_mask(n), marked], axis=1) for n in range(2)]
        queries.append(jnp.concatenate(both, axis=0))
    mixed[...] = jnp.zeros_like(mixed)
    peaks[...] = jnp.full_like(peaks, MASKED)
    totals[...] = jnp.zeros_like(totals)

    def block_step(i, carry):
        start = lax.rem(i * FORWARD_KEYS + rows - offset, rows)
        at = pl.ds(pl.multiple_of(start, FORWARD_KEYS), FORWARD_KEYS)
        block = start // FORWARD_KEYS
        made = [nt(keys[p, at, :], queries[p]) for p in range(heads // 2)]
        for p in range(heads // 2):
            scores = made[p]
            row = slice(p, p + 1)
            peak = jnp.maximum(peaks[row, :], jnp.max(scores, axis=0, keepdims=True))
            shrink = jnp.exp(peaks[row, :] - peak)
            weights = jnp.exp(scores - peak)
            peaks[row, :] = peak
            totals[row, :] = totals[row, :] * shrink + jnp.sum(weights, axis=0, keepdims=True)
            part = nn(values_t[block, of_pair(2 * p), :], weights.astype(BF16))
            for n in range(2):
                h = slice((2 * p + n) * HD, (2 * p + n + 1) * HD)
                q = slice(n * FORWARD_ROWS, (n + 1) * FORWARD_ROWS)
                mixed[h, :] = mixed[h, :] * shrink[:, q] + part[n * HD : (n + 1) * HD, q]
        return carry

    lax.fori_loop(block_low, block_high, block_step, 0)
    inverse = 1.0 / totals[...]
    lse = peaks[...] + jnp.log(totals[...])
    for h in range(heads):
        wide = slice(h * HD, (h + 1) * HD)
        p, q = h // 2, slice(h % 2 * FORWARD_ROWS, (h % 2 + 1) * FORWARD_ROWS)
        mixed[wide, :] = mixed[wide, :] * inverse[p : p + 1, q]
        lse_ref[h : h + 1, :] = lse[p : p + 1, q]
    made = mixed[...].T.astype(BF16)
    half = rows // 2
    for n in range(rows // FORWARD_ROWS):
        start = n * FORWARD_ROWS % half

        @pl.when(step == n)
        def _():
            ref = (o_mine, o_other)[n * FORWARD_ROWS // half]
            ref[start : start + FORWARD_ROWS, :] = made


def whole(shape):
    return pl.BlockSpec(shape, lambda *_: (0,) * len(shape))


def attention_forward(lengths, core, query_rows, key_rows, value_rows):
    rows, width = query_rows.shape
    heads = width // HD
    tile = pl.BlockSpec((FORWARD_ROWS, width), lambda i, *_: (i, 0))
    return pl.pallas_call(
        forward_kernel,
        grid_spec=pltpu.PrefetchScalarGridSpec(
            num_scalar_prefetch=2,
            grid=(rows // FORWARD_ROWS,),
            in_specs=[tile, whole((rows, width)), whole((rows, width))],
            out_specs=[whole((rows // 2, width))] * 2
            + [pl.BlockSpec((8, FORWARD_ROWS), lambda i, *_: (0, i))],
            scratch_shapes=[
                pltpu.VMEM((heads // 2, rows, 2 * LANES), BF16),
                pltpu.VMEM((rows // FORWARD_KEYS, width, FORWARD_KEYS), BF16),
                pltpu.VMEM((width, FORWARD_ROWS), F32),
                pltpu.VMEM((8, 2 * FORWARD_ROWS), F32),
                pltpu.VMEM((8, 2 * FORWARD_ROWS), F32),
            ],
        ),
        out_shape=[jax.ShapeDtypeStruct((rows // 2, width), BF16)] * 2
        + [jax.ShapeDtypeStruct((8, rows), F32)],
        cost_estimate=pl.CostEstimate(
            flops=8 * rows * rows * LANES * heads,
            bytes_accessed=8 * rows * width,
            transcendentals=rows * rows * heads // 2,
        ),
        compiler_params=params(),
        name="attend",
    )(lengths, core, query_rows, key_rows, value_rows)


def backward_kernel(
    lengths, core, q_ref, do_mine, do_other, o_mine, o_other, lse_ref, k_ref, v_ref,
    grad_mine, grad_other, sums_ref, keys, values, keys_t, dk_sum, dv_sum, dq_sum
):
    rows, width = k_ref.shape
    heads = width // HD
    step = pl.program_id(0)
    steps = rows // QB
    ends = segment_ends(lengths)
    offset = core[0] * (rows // 2)
    scale = HD**-0.5

    @pl.when(step == 0)
    def _():
        marks = key_marks(ends, rows, offset)
        for p in range(heads // 2):
            keys[p, :, :LANES] = k_ref[:, of_pair(2 * p)]
            keys[p, :, LANES:] = marks
            values[p] = v_ref[:, of_pair(2 * p)]
        for block in range(rows // KB):
            at = slice(block * KB, (block + 1) * KB)
            keys_t[block] = k_ref[at, :].astype(F32).T.astype(BF16)
        dk_sum[...] = jnp.zeros_like(dk_sum)
        dv_sum[...] = jnp.zeros_like(dv_sum)

    first = lax.rem(step * QB + offset, rows)
    low, high = bounds(ends, rows, first, first + QB - 1)
    block_low, block_high = low // KB, (high + KB - 1) // KB
    marked = query_marks(ends, rows, first, QB).astype(BF16)
    early = jnp.full((1, width), step, jnp.int32) < steps // 2
    use_mine = early.astype(F32).astype(BF16)
    use_other = (~early).astype(F32).astype(BF16)
    grad_rows = do_mine[...] * use_mine + do_other[...] * use_other
    mixed_rows = o_mine[...] * use_mine + o_other[...] * use_other
    lane = lax.broadcasted_iota(jnp.int32, (8, LANES), 1)
    row = lax.broadcasted_iota(jnp.int32, (8, LANES), 0)
    by_head = (lane // HD == row).astype(F32).astype(BF16)
    queries, grads, marked_queries, logsums, centres = [], [], [], [], []
    for p in range(heads // 2):
        pair = of_pair(2 * p)
        query = [q_ref[:, pair] * (lane_mask(n) * BF16(scale)) for n in range(2)]
        grad = grad_rows[:, pair]
        exact = grad.astype(F32) * mixed_rows[:, pair].astype(F32)
        high_term = exact.astype(BF16)
        low_term = (exact - high_term.astype(F32)).astype(BF16)
        centre = nt(by_head, high_term) + nt(by_head, low_term)
        centres.append(jnp.concatenate([centre[0:1, :], centre[1:2, :]], axis=1))
        logsums.append(
            jnp.concatenate([lse_ref[2 * p : 2 * p + 1, :], lse_ref[2 * p + 1 : 2 * p + 2, :]], axis=1)
        )
        queries.append(jnp.concatenate(query, axis=0))
        grads.append(jnp.concatenate([grad * lane_mask(n) for n in range(2)], axis=0))
        marked_queries.append(
            jnp.concatenate([queries[p], jnp.concatenate([marked, marked], axis=0)], axis=1)
        )
    dq_sum[...] = jnp.zeros_like(dq_sum)

    def block_step(i, carry):
        start = lax.rem(i * KB + rows - offset, rows)
        at = pl.ds(pl.multiple_of(start, KB), KB)
        block = start // KB
        scores = [nt(keys[p, at, :], marked_queries[p]) for p in range(heads // 2)]
        pulls = [nt(values[p, at, :], grads[p]) for p in range(heads // 2)]
        for p in range(heads // 2):
            weights = jnp.exp(scores[p] - logsums[p])
            pulled = pulls[p]
            dv_sum[at, of_pair(2 * p)] += nn(weights.astype(BF16), grads[p])
            slopes = (weights * (pulled - centres[p])).astype(BF16)
            dk_sum[at, of_pair(2 * p)] += nn(slopes, queries[p])
            part = nn(keys_t[block, of_pair(2 * p), :], slopes)
            for n in range(2):
                h = slice((2 * p + n) * HD, (2 * p + n + 1) * HD)
                dq_sum[h, :] += part[n * HD : (n + 1) * HD, n * QB : (n + 1) * QB]
        return carry

    lax.fori_loop(block_low, block_high, block_step, 0)
    made = (dq_sum[...] * scale).T.astype(BF16)
    half = rows // 2
    for n in range(steps):
        start = n * QB % half

        @pl.when(step == n)
        def _():
            (grad_mine, grad_other)[n * QB // half][start : start + QB, :width] = made

    total = jnp.sum(made.astype(F32), axis=0, keepdims=True)

    @pl.when(step == 0)
    def _():
        sums_ref[...] = jnp.zeros_like(sums_ref)

    sums_ref[0:1, :] += total

    @pl.when(step == steps - 1)
    def _():
        for n, ref in enumerate((grad_mine, grad_other)):
            at = slice(n * half, (n + 1) * half)
            ref[:, width : 2 * width] = dk_sum[at, :].astype(BF16)
            made = dv_sum[at, :].astype(BF16)
            ref[:, 2 * width :] = made
            sums_ref[1:2, :] += jnp.sum(made.astype(F32), axis=0, keepdims=True)


def attention_backward(
    lengths, core, query_rows, key_rows, value_rows, mixed, lse, grad_mine, grad_other
):
    rows, width = query_rows.shape
    heads = width // HD
    steps = rows // QB
    tile = pl.BlockSpec((QB, width), lambda i, *_: (i, 0))
    full = whole((rows, width))
    early = pl.BlockSpec((QB, width), lambda i, *_: (jnp.minimum(i, steps // 2 - 1), 0))
    late = pl.BlockSpec((QB, width), lambda i, *_: (jnp.maximum(i - steps // 2, 0), 0))
    outs = [jax.ShapeDtypeStruct((rows // 2, 3 * width), BF16)] * 2
    outs.append(jax.ShapeDtypeStruct((8, width), F32))
    return pl.pallas_call(
        backward_kernel,
        grid_spec=pltpu.PrefetchScalarGridSpec(
            num_scalar_prefetch=2,
            grid=(steps,),
            in_specs=[
                tile,
                early,
                late,
                early,
                late,
                pl.BlockSpec((8, QB), lambda i, *_: (0, i)),
                full,
                full,
            ],
            out_specs=[whole(o.shape) for o in outs],
            scratch_shapes=[
                pltpu.VMEM((heads // 2, rows, 2 * LANES), BF16),
                pltpu.VMEM((heads // 2, rows, LANES), BF16),
                pltpu.VMEM((rows // KB, width, KB), BF16),
                pltpu.VMEM((rows, width), F32),
                pltpu.VMEM((rows, width), F32),
                pltpu.VMEM((width, QB), F32),
            ],
        ),
        out_shape=outs,
        cost_estimate=pl.CostEstimate(
            flops=20 * rows * rows * LANES * heads,
            bytes_accessed=16 * rows * width,
            transcendentals=rows * rows * heads // 2,
        ),
        compiler_params=params(),
        name="attend_back",
    )(lengths, core, query_rows, grad_mine, grad_other, *mixed, lse, key_rows, value_rows)


def params():
    return pltpu.CompilerParams(vmem_limit_bytes=VMEM_LIMIT)


def cost(flops, moved, transcendentals=0):
    return pl.CostEstimate(flops=flops, bytes_accessed=moved, transcendentals=transcendentals)


def columns_of(slots, core, run_rows, half):
    half_run = run_rows // 2
    run, place = slots // run_rows, slots % run_rows
    held = (place // half_run + core) % 2
    return held * half + run * half_run + place % half_run


def one_hot(column, width, base):
    count = column.shape[1]
    down = jnp.broadcast_to(column, (8, count)).T[:, :1]
    lane = lax.broadcasted_iota(jnp.int32, (count, width), 1) + base
    return (down == lane).astype(F32).astype(BF16)


def intake_kernel(
    run_rows, core, slots, mine_ref, other_ref, q_weight, k_weight, v_weight, q_bias, v_bias,
    x_ref, q_ref, k_ref, v_ref
):
    half = mine_ref.shape[0]
    column = columns_of(slots[...], core[0], run_rows, half)
    rows = nn(one_hot(column, half, 0), mine_ref[...])
    rows = (rows + nn(one_hot(column, half, half), other_ref[...])).astype(BF16)
    x_ref[...] = rows
    q_ref[...] = (nn(rows, q_weight[...]) + q_bias[...]).astype(BF16)
    k_ref[...] = nn(rows, k_weight[...]).astype(BF16)
    v_ref[...] = (nn(rows, v_weight[...]) + v_bias[...]).astype(BF16)


def intake(core, slots, run_rows, mine_rows, other_rows, weights, biases):
    half, features = mine_rows.shape
    rows = 2 * half
    width = weights[0].shape[1]
    count = 512
    blocks = rows // count

    def tile(n):
        return pl.BlockSpec((count, n), lambda i, core: (i, 0))

    return pl.pallas_call(
        functools.partial(intake_kernel, run_rows),
        grid_spec=pltpu.PrefetchScalarGridSpec(
            num_scalar_prefetch=1,
            grid=(blocks,),
            in_specs=[
                pl.BlockSpec(
                    (1, count), lambda i, core: (0, (i + core[0] * (blocks // 2)) % blocks)
                ),
                whole((half, features)),
                whole((half, features)),
            ]
            + [whole((features, width))] * 3
            + [whole((1, width))] * 2,
            out_specs=[tile(features), tile(width), tile(width), tile(width)],
        ),
        out_shape=[jax.ShapeDtypeStruct((rows, features), BF16)]
        + [jax.ShapeDtypeStruct((rows, width), BF16)] * 3,
        cost_estimate=cost(2 * rows * features * (rows + 3 * width), 8 * rows * features),
        compiler_params=params(),
        name="intake",
    )(core, slots, mine_rows, other_rows, *weights, *biases)


def centred(values):
    centre = values - jnp.mean(values, axis=-1, keepdims=True)
    inverse = lax.rsqrt(jnp.mean(centre * centre, axis=-1, keepdims=True) + EPSILON)
    return centre * inverse, inverse


def norm_back(upstream, normed, inverse, gain):
    scaled = upstream * gain
    return inverse * (
        scaled
        - jnp.mean(scaled, axis=-1, keepdims=True)
        - normed * jnp.mean(scaled * normed, axis=-1, keepdims=True)
    )


def add_rows(ref, row, values):
    ref[row : row + 1, :] += jnp.sum(values, axis=0, keepdims=True)


def rows_kernel(
    run_rows, core, x_ref, mixed_mine, mixed_other, slots, cot_mine, cot_other,
    out_bias, first_gain, first_shift, down_bias, second_gain, second_shift, bias_mine, bias_other,
    out_mine, out_other, up_mine, up_other, down_mine, down_other,
    y_out, hb_out, second_out, act_out_mine, act_out_other, du_out_mine, du_out_other, first_out, low_out,
    back_out_mine, back_out_other, sums, up_sums,
    w_out, w_up, w_down, sems, out_sems, hidden, first_inv, total, slope, grad, pulled, biases,
    y_ref, hb_ref, second_ref, act, du, first_ref, low_ref, back
):
    half, features = x_ref.shape
    width = mixed_mine.shape[1]
    chunks, _, chunk = w_up.shape
    per_half = chunks // 2
    tiles = half // ROW_TILE
    copies = [
        pltpu.make_async_copy(out_mine, w_out.at[0], sems.at[0]),
        pltpu.make_async_copy(out_other, w_out.at[1], sems.at[1]),
    ]
    up_copies, down_copies = [], []
    for c in range(chunks):
        up, down = ((up_mine, down_mine), (up_other, down_other))[c // per_half]
        at = pl.ds(c % per_half * chunk, chunk)
        up_copies.append(pltpu.make_async_copy(up.at[:, at], w_up.at[c], sems.at[2 + c]))
        down_copies.append(
            pltpu.make_async_copy(down.at[at, :], w_down.at[c], sems.at[2 + chunks + c])
        )
    outgoing = []

    def send(source, target):
        copy = pltpu.make_async_copy(source, target, out_sems.at[len(outgoing)])
        copy.start()
        outgoing.append(copy)

    for copy in copies:
        copy.start()
    for up, down in zip(up_copies, down_copies):
        up.start()
        down.start()
    out_bias, first_gain, first_shift = out_bias[...], first_gain[...], first_shift[...]
    down_bias, second_gain, second_shift = down_bias[...], second_gain[...], second_shift[...]
    sums[...] = jnp.zeros_like(sums)
    up_sums[...] = jnp.zeros_like(up_sums)

    column = columns_of(slots[...], core[0], run_rows, half)
    grad[...] = nn(one_hot(column, half, 0), cot_mine[...])
    grad[...] += nn(one_hot(column, half, half), cot_other[...])

    def of_chunk(refs, c):
        return refs[c // per_half], pl.ds(c % per_half * chunk, chunk)

    for copy in copies:
        copy.wait()
    total[...] = nn(mixed_mine[...], w_out[0]) + nn(mixed_other[...], w_out[1])

    @pl.loop(0, tiles, unroll=2)
    def _(i):
        at = pl.ds(pl.multiple_of(i * ROW_TILE, ROW_TILE), ROW_TILE)
        normed, inverse = centred(x_ref[at, :].astype(F32) + total[at, :] + out_bias)
        rows = normed * first_gain + first_shift
        hidden[at, :] = rows
        hb_ref[at, :] = rows.astype(BF16)
        first_ref[at, :] = normed
        first_inv[at, :] = inverse

    send(hb_ref, hb_out)

    block = half // 2
    blocks = [slice(r * block, (r + 1) * block) for r in range(2)]
    for c in range(chunks):
        ref, wide = of_chunk((bias_mine, bias_other), c)
        biases[c : c + 1, :] = ref[:, wide]

    def inner_of(c):
        pltpu.make_async_copy(up_mine.at[:, pl.ds(0, chunk)], w_up.at[c], sems.at[2 + c]).wait()
        for at in blocks:
            slope[c, at, :] = nn(hb_ref[at, :], w_up[c]) + biases[pl.ds(c, 1), :]

    def activate(c):
        for at in blocks:
            inner = slope[c, at, :]
            share = 0.5 * (1.0 + lax.erf(inner * 0.7071067811865476))
            density = jnp.exp(-0.5 * inner * inner) * 0.3989422804014327
            act[c, at, :] = (inner * share).astype(BF16)
            slope[c, at, :] = share + inner * density
            total[at, :] += nn(act[c, at, :], w_down[c])

    def down_ready(c):
        source = down_mine.at[pl.ds(0, chunk), :]
        pltpu.make_async_copy(source, w_down.at[c], sems.at[2 + chunks + c]).wait()

    total[...] = jnp.zeros_like(total)
    inner_of(0)

    @pl.loop(0, chunks - 1)
    def _(c):
        down_ready(c)
        inner_of(c + 1)
        activate(c)

    down_ready(chunks - 1)
    activate(chunks - 1)
    for c in range(chunks):
        ref, wide = of_chunk((act_out_mine, act_out_other), c)
        send(act.at[c], ref.at[:, wide])

    @pl.loop(0, tiles, unroll=2)
    def _(i):
        at = pl.ds(pl.multiple_of(i * ROW_TILE, ROW_TILE), ROW_TILE)
        normed, inverse = centred(hidden[at, :] + total[at, :] + down_bias)
        y_ref[at, :] = (normed * second_gain + second_shift).astype(BF16)
        upstream = grad[at, :]
        add_rows(sums, 4, upstream * normed)
        add_rows(sums, 5, upstream)
        back = norm_back(upstream, normed, inverse, second_gain)
        add_rows(sums, 3, back)
        second_ref[at, :] = back.astype(BF16)
        grad[at, :] = back

    send(y_ref, y_out)
    send(second_ref, second_out)
    def pull(c):
        for at in blocks:
            pulled[c % 2, at, :] = nt(second_ref[at, :], w_down[c])

    def push(c):
        row = (c // per_half ^ core[0]) * per_half + c % per_half
        for at in blocks:
            low = (pulled[c % 2, at, :] * slope[c, at, :]).astype(BF16)
            du[c, at, :] = low
            up_sums[pl.ds(row, 1), :] += jnp.sum(low.astype(F32), axis=0, keepdims=True)
            grad[at, :] += nt(low, w_up[c])

    pull(0)

    @pl.loop(0, chunks - 1)
    def _(c):
        pull(c + 1)
        push(c)

    push(chunks - 1)
    for c in range(chunks):
        ref, wide = of_chunk((du_out_mine, du_out_other), c)
        send(du.at[c], ref.at[:, wide])

    @pl.loop(0, tiles, unroll=2)
    def _(i):
        at = pl.ds(pl.multiple_of(i * ROW_TILE, ROW_TILE), ROW_TILE)
        upstream, normed = grad[at, :], first_ref[at, :]
        add_rows(sums, 1, upstream * normed)
        add_rows(sums, 2, upstream)
        back = norm_back(upstream, normed, first_inv[at, :], first_gain)
        add_rows(sums, 0, back)
        first_ref[at, :] = back

    send(first_ref, first_out)
    low_ref[...] = first_ref[...].astype(BF16)
    send(low_ref, low_out)
    for n, out in enumerate((back_out_mine, back_out_other)):
        back[n] = nt(low_ref[...], w_out[n]).astype(BF16)
        send(back.at[n], out)
    for copy in outgoing:
        copy.wait()


def row_pass(
    core, inputs, mixed, mixed_other, slots, run_rows, cot_mine, cot_other, vectors,
    out_mine, out_other, up_mine, up_other, down_mine, down_other
):
    half, features = cot_mine.shape
    width = mixed.shape[1]
    chunk = features
    chunks = 2 * up_mine.shape[1] // chunk
    any_space = pl.BlockSpec(memory_space=pl.ANY)

    def low(*shape):
        return jax.ShapeDtypeStruct(shape, BF16)

    outs = [
        low(half, features),
        low(half, features),
        low(half, features),
        low(half, up_mine.shape[1]),
        low(half, up_mine.shape[1]),
        low(half, up_mine.shape[1]),
        low(half, up_mine.shape[1]),
        jax.ShapeDtypeStruct((half, features), F32),
        low(half, features),
        low(half, width),
        low(half, width),
        jax.ShapeDtypeStruct((8, features), F32),
        jax.ShapeDtypeStruct((chunks, chunk), F32),
    ]
    return pl.pallas_call(
        functools.partial(rows_kernel, run_rows),
        grid_spec=pltpu.PrefetchScalarGridSpec(
            num_scalar_prefetch=1,
            grid=(1,),
            in_specs=[
                whole((half, features)),
                whole((half, width)),
                whole((half, width)),
                pl.BlockSpec((1, half), lambda i, core: (0, core[0])),
                whole((half, features)),
                whole((half, features)),
            ]
            + [whole(v.shape) for v in vectors]
            + [any_space] * 6,
            out_specs=[any_space] * (len(outs) - 2) + [whole(o.shape) for o in outs[-2:]],
            scratch_shapes=[
                pltpu.VMEM((2, width, features), BF16),
                pltpu.VMEM((chunks, features, chunk), BF16),
                pltpu.VMEM((chunks, chunk, features), BF16),
                pltpu.SemaphoreType.DMA((2 + 2 * chunks,)),
                pltpu.SemaphoreType.DMA((7 + 2 * chunks,)),
                pltpu.VMEM((half, features), F32),
                pltpu.VMEM((half, 1), F32),
                pltpu.VMEM((half, features), F32),
                pltpu.VMEM((chunks, half, chunk), F32),
                pltpu.VMEM((half, features), F32),
                pltpu.VMEM((2, half, chunk), F32),
                pltpu.VMEM((chunks, chunk), F32),
                pltpu.VMEM((half, features), BF16),
                pltpu.VMEM((half, features), BF16),
                pltpu.VMEM((half, features), BF16),
                pltpu.VMEM((chunks, half, chunk), BF16),
                pltpu.VMEM((chunks, half, chunk), BF16),
                pltpu.VMEM((half, features), F32),
                pltpu.VMEM((half, features), BF16),
                pltpu.VMEM((2, half, width), BF16),
            ],
        ),
        out_shape=outs,
        cost_estimate=cost(
            8 * half * features * chunk * chunks + 10 * half * features * features,
            30 * half * features + 8 * features * chunk * chunks,
            half * chunk * chunks,
        ),
        compiler_params=params(),
        name="row_pass",
    )(
        core, inputs, mixed, mixed_other, slots, cot_mine, cot_other, *vectors,
        out_mine, out_other, up_mine, up_other, down_mine, down_other
    )


def after(values, others):
    return lax.optimization_barrier((values, others))[0]


def near_groups(groups):
    near = 4 if groups % 4 == 0 else 1
    return near, groups // near


def tn(left, right):
    return lax.dot_general(left, right, (((0,), (0,)), ((), ())), preferred_element_type=F32)


def by_place(terms, groups):
    near, far = near_groups(groups)
    place = lax.axis_index("dp") % near
    terms = terms.reshape(far, near, terms.shape[0] // groups, terms.shape[1])
    return [lax.dynamic_index_in_dim(terms, place ^ n, 1, keepdims=False) for n in range(near)]


def gradient_kernel(chunks, near, share, halving, me, *refs):
    operands, outs, acc = refs[: 4 * len(chunks)], refs[4 * len(chunks) : -1], refs[-1]
    step = pl.program_id(0)
    first, column = 0, 0
    for n, (chunk, count) in enumerate(chunks):
        left, left_more, right, right_more = operands[4 * n : 4 * n + 4]

        @pl.when((step >= first) & (step < first + count))
        def _():
            acc[:, :chunk] = tn(left[...], right[...])
            acc[:, :chunk] += tn(left_more[...], right_more[...])
            at = pl.ds(pl.multiple_of(column + (step - first) * chunk, LANES), chunk)

            def place(out, place):
                for f in range(out.shape[0]):
                    row = share * (f * near + (me[0] ^ place))
                    row = pl.ds(pl.multiple_of(row, 16), share)
                    out[f, :, at] = acc[row, :chunk].astype(out.dtype)

            if halving:
                for out, (a, b) in zip(outs, ((0, 3 - halving), (halving, 3))):
                    place(out.at[0], a)
                    place(out.at[1], b)
            else:
                for m, out in enumerate(outs):
                    place(out, m)

        first += count
        column += count * chunk


def gradients(pieces, groups, halving=0):
    near, far = near_groups(groups)
    features = pieces[0][0][0].shape[1]
    share = features // groups
    if near != 4 or share % 16 != 0:

        def rows_of(left, rows):
            return lax.slice_in_dim(left[0], left[1] * rows, (left[1] + 1) * rows, axis=0)

        terms = [
            tn(rows_of(p[0], p[2].shape[0]), p[2]) + tn(rows_of(p[1], p[3].shape[0]), p[3])
            for p in pieces
        ]
        made = [t.astype(BF16) for t in by_place(jnp.concatenate(terms, axis=1), groups)]
        if halving:
            made = [
                jnp.stack([made[0], made[3 - halving]]), jnp.stack([made[halving], made[3]])
            ]
        return made
    in_specs, operands, chunks, base, columns = [], [], [], 0, 0
    for left, left_more, right, right_more in pieces:
        rows = right.shape[0]
        chunk = min(features, right.shape[1])
        if right.shape[1] % chunk:
            chunk = right.shape[1] // 3
        count = right.shape[1] // chunk

        def at(j, me, base=base, count=count):
            return 0, jnp.clip(j - base, 0, count - 1)

        for array, block in (left, left_more):
            in_specs.append(
                pl.BlockSpec((rows, features), lambda j, me, block=block: (block, 0))
            )
            operands.append(array)
        in_specs += [pl.BlockSpec((rows, chunk), at)] * 2
        operands += [right, right_more]
        chunks.append((chunk, count))
        base += count
        columns += count * chunk
    if halving:
        outs = [jax.ShapeDtypeStruct((2, far, share, columns), BF16)] * 2
    else:
        outs = [jax.ShapeDtypeStruct((far, share, columns), BF16)] * near
    return pl.pallas_call(
        functools.partial(gradient_kernel, chunks, near, share, halving),
        grid_spec=pltpu.PrefetchScalarGridSpec(
            num_scalar_prefetch=1,
            grid=(base,),
            in_specs=in_specs,
            out_specs=[whole(o.shape) for o in outs],
            scratch_shapes=[pltpu.VMEM((features, features), F32)],
        ),
        out_shape=outs,
        cost_estimate=cost(4 * rows * features * columns, 8 * rows * features + 4 * features * columns),
        compiler_params=params(),
        name="gradients",
    )((lax.axis_index("dp") % near).reshape(1), *operands)


def pairs(groups, distance):
    return [(i, i ^ distance) for i in range(groups)]


def far_halves(total, groups, bit):
    total = total.reshape(-1, 2, *total.shape[1:])
    side = (lax.axis_index("dp") // near_groups(groups)[0] >> bit) & 1
    kept = lax.dynamic_index_in_dim(total, side, 1, keepdims=False)
    return kept, lax.dynamic_index_in_dim(total, 1 - side, 1, keepdims=False).astype(BF16)


def far_step(halves, groups, bit, first=()):
    near, far = near_groups(groups)
    kept, sent = halves
    got = after(lax.ppermute(sent, "dp", pairs(groups, near << bit)), first)
    total = kept.astype(F32) + got.astype(F32)
    return far_halves(total, groups, bit + 1) if 2 << bit < far else total[0]


def far_direct(total, groups, first=()):
    near, far = near_groups(groups)
    run = lax.axis_index("dp") // near
    kept = lax.dynamic_index_in_dim(total, run, 0, keepdims=False)
    got = []
    for step in range(1, far):
        sent = lax.dynamic_index_in_dim(total, run ^ step, 0, keepdims=False).astype(BF16)
        got.append(lax.ppermute(sent, "dp", pairs(groups, step * near)))
    return sum_of(kept, after(got, first))


def near_sends(terms, groups):
    return [lax.ppermute(t, "dp", pairs(groups, n + 1)) for n, t in enumerate(terms)]


def sum_of(kept, got):
    kept = kept.astype(F32)
    for term in got:
        kept = kept + term.astype(F32)
    return kept


def input_kernel(first_ref, mine_ref, other_ref, *refs):
    weights, out_ref = refs[:-1], refs[-1]
    total = first_ref[...]
    for n, rows in enumerate((mine_ref, other_ref)):
        wide = jnp.concatenate([weight[...] for weight in weights[3 * n : 3 * n + 3]], axis=1)
        total = total + nt(rows[...], wide)
    out_ref[...] = total.astype(BF16)


def input_rows(first_grad, mine_rows, other_rows, weights):
    half, features = first_grad.shape
    wide = other_rows.shape[1]
    count = 256

    def tile(n):
        return pl.BlockSpec((count, n), lambda i: (i, 0))

    return pl.pallas_call(
        input_kernel,
        grid=(half // count,),
        in_specs=[tile(features), tile(wide), tile(wide)] + [whole(w.shape) for w in weights],
        out_specs=tile(features),
        out_shape=jax.ShapeDtypeStruct((half, features), BF16),
        cost_estimate=cost(4 * half * features * wide, 8 * half * features + 4 * features * wide),
        compiler_params=params(),
        name="input_rows",
    )(first_grad, mine_rows, other_rows, *weights)


def route_kernel(share, has_extra, core, slots_mine, slots_other, mine_ref, other_ref, *refs):
    out_ref = refs[-1]
    groups, run = out_ref.shape[0], mine_ref.shape[0] // out_ref.shape[0]
    half = mine_ref.shape[0]
    row = lax.broadcasted_iota(jnp.int32, (half, half), 0)
    column_mine = columns_of(slots_mine[...], core[0], 2 * run, half)
    column_other = columns_of(slots_other[...], core[0], 2 * run, half)
    put_mine = (column_mine == row).astype(F32).astype(BF16)
    put_other = (column_other == row).astype(F32).astype(BF16)
    rows = (nn(put_mine, mine_ref[...]) + nn(put_other, other_ref[...])).astype(BF16)
    out_ref[:, :run, :] = rows.reshape(groups, run, rows.shape[1])
    if has_extra:
        sums, up_sums, qv_sums, wide, wide_up = refs[:5]
        features = sums.shape[1]
        width = qv_sums.shape[1]
        wide[...] = jnp.zeros_like(wide)
        wide_up[...] = jnp.zeros_like(wide_up)
        wide[:, :features] = sums[...]
        wide_up[:4, :features] = up_sums[...]
        at = pl.ds(pl.multiple_of(core[0] * width, LANES), width)
        wide[6:8, at] = qv_sums[:2, :]
        for g in range(groups):
            block = wide[:, share * g : share * g + LANES]
            start = 4 * share * g
            blocks = [block]
            parts = []
            for r in range(4):
                line = (start + share * r) // features
                lane = (start + share * r) % features
                parts.append(wide_up[line : line + 1, lane : lane + LANES])
            blocks.append(jnp.concatenate(parts + [jnp.zeros((4, LANES), F32)], axis=0))
            for b, rest in enumerate(blocks):
                for piece in range(3):
                    term = rest.astype(BF16)
                    rest = rest - term.astype(F32)
                    q = 2 * piece + b
                    out_ref[g, run : run + 8, q * LANES : (q + 1) * LANES] = term


def route(core, slots, mine_rows, other_rows, groups, extra=None):
    half, features = mine_rows.shape
    run = half // groups
    share = features // groups
    extra = extra or ()
    args = [core, slots, slots, mine_rows, other_rows, *extra]
    in_specs = [
        pl.BlockSpec((1, half), lambda i, core: (0, core[0])),
        pl.BlockSpec((1, half), lambda i, core: (0, 1 - core[0])),
    ] + [whole(a.shape) for a in args[3:]]
    scratch = [pltpu.VMEM((8, features + LANES), F32)] * 2 if extra else []
    shape = (groups, run + (8 if extra else 0), features)

    def kernel(*refs):
        ins, (out_ref, *more) = refs[: len(args)], refs[len(args) :]
        route_kernel(share, len(extra) > 0, *ins, *more, out_ref)

    return pl.pallas_call(
        kernel,
        grid_spec=pltpu.PrefetchScalarGridSpec(
            num_scalar_prefetch=1,
            grid=(1,),
            in_specs=in_specs,
            out_specs=whole(shape),
            scratch_shapes=scratch,
        ),
        out_shape=jax.ShapeDtypeStruct(shape, BF16),
        cost_estimate=cost(4 * half * half * features, 6 * half * features),
        compiler_params=params(),
        name="route",
    )(*args)


def exchange(values):
    return lax.all_to_all(values, "dp", split_axis=0, concat_axis=0, tiled=True)


def weave_kernel(core, mine_ref, other_ref, out_ref, *outs):
    run = out_ref.shape[2]
    out_ref[:, core[0]] = mine_ref[:, :run, :]
    out_ref[:, 1 - core[0]] = other_ref[:, :run, :]
    if not outs:
        return
    pieces = []
    for q in range(6):
        at = slice(q * LANES, (q + 1) * LANES)
        both = [jnp.sum(r[:, run:, at].astype(F32), axis=0) for r in (mine_ref, other_ref)]
        pieces.append(both[0] + both[1])
    first, more = [pieces[4 + b] + pieces[2 + b] + pieces[b] for b in range(2)]
    each = outs[0].shape[1]
    share = 2 * each
    low = core[0] == 0

    def half_of(values):
        return jnp.where(low, values[:, :each], values[:, each:share])

    for out, row in zip(outs[:8], (6, 7, 0, 1, 2, 3, 4, 5)):
        out[...] = half_of(first[row : row + 1, :])
    pair = jnp.where(low, more[0:2, :share], more[2:4, :share])
    outs[8][:, :share] = pair[0:1, :]
    outs[8][:, share:] = pair[1:2, :]


def weave(core, part, rows_of_core, small=0):
    groups, _, features = part.shape
    outs = [jax.ShapeDtypeStruct((groups, 2, rows_of_core, features), BF16)]
    if small:
        outs += [jax.ShapeDtypeStruct((1, small), F32)] * 8
        outs.append(jax.ShapeDtypeStruct((1, 4 * small), F32))
    rows, *more = pl.pallas_call(
        weave_kernel,
        grid_spec=pltpu.PrefetchScalarGridSpec(
            num_scalar_prefetch=1,
            grid=(1,),
            in_specs=[whole(part.shape)] * 2,
            out_specs=[whole(o.shape) for o in outs],
        ),
        out_shape=outs,
        cost_estimate=cost(1, 1),
        compiler_params=params(),
        name="weave",
    )(core, part, swap(part))
    rows = rows.reshape(groups * 2 * rows_of_core, features)
    return (rows, *[m.reshape(-1) for m in more]) if small else rows


def local(
    tokens,
    token_slot,
    seq_lengths,
    query_weight,
    query_bias,
    key_weight,
    value_weight,
    value_bias,
    out_weight,
    out_bias,
    first_gain,
    first_shift,
    up_weight,
    up_bias,
    down_weight,
    down_bias,
    second_gain,
    second_shift,
    cotangent,
):
    groups = lax.axis_size("dp")
    row_count, features = tokens.shape
    run_rows = row_count // groups
    half_run = run_rows // 2
    half = row_count // 2
    mine = lax.axis_index("tensor")
    core = mine.reshape(1)
    near, far = near_groups(groups)

    def part_of(values):
        return lax.dynamic_slice_in_dim(
            values.reshape(groups, run_rows, features), mine * half_run, half_run, 1
        )

    cot_part = part_of(cotangent)
    token_rows = after(exchange(part_of(tokens)), cot_part).reshape(half, features)
    cot_raw = exchange(cot_part).reshape(half, features)

    qkv_weights = [query_weight, key_weight, value_weight]
    out_other, up_other, down_other = swap(out_weight), swap(up_weight), swap(down_weight)
    vectors = [out_bias, first_gain, first_shift, down_bias, second_gain, second_shift]
    bias_other = swap(up_bias)
    vectors = [v.reshape(1, -1) for v in vectors + [up_bias, bias_other]]
    qkv_other = [swap(w) for w in qkv_weights]
    token_got = after(swap(token_rows), (out_other, up_other, down_other, qkv_other, bias_other))

    inputs, query_rows, key_rows, value_rows = intake(
        core, token_slot, run_rows, token_rows, token_got, qkv_weights,
        (query_bias.reshape(1, -1), value_bias.reshape(1, -1)),
    )
    mixed_mine, mixed_theirs, logsum = attention_forward(seq_lengths, core, query_rows, key_rows, value_rows)
    cot_rows = after(cot_raw, mixed_mine)
    mixed_other = swap(mixed_theirs)
    (
        output_low, hidden_low, second_low, act_mine, act_other, inner_mine, inner_other, first_grad,
        first_low, mixed_grad_mine, mixed_grad_other, sums, up_sums,
    ) = row_pass(
        core, inputs, mixed_mine, mixed_other, token_slot, run_rows, cot_rows, swap(cot_rows), vectors,
        out_weight, out_other, up_weight, up_other, down_weight, down_other,
    )
    mixed_grad_got = swap(mixed_grad_other)

    width = query_weight.shape[1]
    ff_width = up_weight.shape[1]
    output_got = swap(output_low)
    second_low, hidden_low, first_low, act_other, inner_other = after(
        (second_low, hidden_low, first_low, act_other, inner_other), output_got
    )
    second_got, act_got = swap(second_low), swap(act_other)
    hidden_got, inner_got = swap(hidden_low), swap(inner_other)
    first_got = swap(first_low)
    returned = route(core, token_slot, output_low, output_got, groups)
    kept, sent = [], []
    left = gradients([((second_low, 0), (second_got, 0), act_mine, act_got)], groups, near == 4)
    right = [
        ((hidden_low, 0), (hidden_got, 0), inner_mine, inner_got),
        ((first_low, 0), (first_got, 0), mixed_mine, mixed_theirs),
    ]
    right = gradients(right, groups, 2 * (near == 4))
    if near == 4:
        kept, sent = [left[0], right[0]], [left[1], right[1]]
    else:
        kept, sent = [left[0][None], right[0][None]], []
    mixed_grad_mine, mixed_grad_got = after(
        (mixed_grad_mine, mixed_grad_got), (returned, kept, sent)
    )
    returned = exchange(returned)
    got = [lax.ppermute(v, "dp", pairs(groups, n + 1)) for n, v in enumerate(sent)]
    qkv_mine, qkv_theirs, qv_sums = attention_backward(
        seq_lengths, core, query_rows, key_rows, value_rows, (mixed_mine, mixed_theirs), logsum,
        mixed_grad_mine, mixed_grad_got,
    )
    other_grad = swap(qkv_theirs)
    qkv_terms = gradients([((inputs, 0), (inputs, 1), qkv_mine, qkv_theirs)], groups)
    got, returned = after((got, returned), qkv_terms)
    both = [k.astype(F32) + g.astype(F32) for k, g in zip(kept, got)]
    sent = [b[1].astype(BF16) for b in both]
    kept = [b[0] for b in both] if got else [k[0] for k in kept]
    first_grad = after(first_grad, (qkv_terms, sent, kept))
    qkv_got = near_sends(qkv_terms[1:], groups)
    got = [lax.ppermute(v, "dp", pairs(groups, 2 - n)) for n, v in enumerate(sent)]
    input_low = input_rows(
        first_grad, qkv_mine, other_grad, qkv_weights + qkv_other
    )
    given = route(core, token_slot, input_low, swap(input_low), groups, (sums, up_sums, qv_sums))
    got = after(got, given)
    if got:
        kept = [k + g.astype(F32) for k, g in zip(kept, got)]
    ffn_terms = far_halves(jnp.concatenate(kept, axis=2), groups, 0)
    payload, given = given, exchange(given)
    layer_out = weave(core, after(returned, payload), half_run)
    ffn_sum = far_step(ffn_terms, groups, 0, (given, layer_out))
    qkv_got = after(qkv_got, ffn_sum)
    for bit in range(1, far.bit_length() - 1):
        ffn_sum = far_step(ffn_sum, groups, bit, qkv_got)
    qkv_sum = far_direct(sum_of(qkv_terms[0], qkv_got), groups, ffn_sum)
    (
        input_gradient, query_bias_sum, value_bias_sum, out_bias_sum, first_gain_sum,
        first_shift_sum, down_bias_sum, second_gain_sum, second_shift_sum, up_bias_sum,
    ) = weave(core, given, half_run, features // groups // 2)
    return (
        layer_out,
        input_gradient,
        qkv_sum[:, :width],
        query_bias_sum,
        qkv_sum[:, width : 2 * width],
        qkv_sum[:, 2 * width :],
        value_bias_sum,
        ffn_sum[:, 2 * ff_width :].T,
        out_bias_sum,
        first_gain_sum,
        first_shift_sum,
        ffn_sum[:, ff_width : 2 * ff_width],
        up_bias_sum,
        ffn_sum[:, :ff_width].T,
        down_bias_sum,
        second_gain_sum,
        second_shift_sum,
    )


def solution(mesh):
    rows = P("dp", None)
    in_specs = (
        rows,
        rows,
        rows,
        P(None, "tensor"),
        P("tensor"),
        P(None, "tensor"),
        P(None, "tensor"),
        P("tensor"),
        P("tensor", None),
        P(),
        P(),
        P(),
        P(None, "tensor"),
        P("tensor"),
        P("tensor", None),
        P(),
        P(),
        P(),
        rows,
    )
    spread = P(("dp", "tensor"))
    out_specs = (
        rows,
        rows,
        P("dp", "tensor"),
        spread,
        P("dp", "tensor"),
        P("dp", "tensor"),
        spread,
        P("tensor", "dp"),
        spread,
        spread,
        spread,
        P("dp", "tensor"),
        spread,
        P("tensor", "dp"),
        spread,
        spread,
        spread,
    )
    return jax.shard_map(local, mesh=mesh, in_specs=in_specs, out_specs=out_specs, check_vma=False)
```

profile of v0, /device:TPU:0, one launch (start us, length us, event | category | flops | bytes accessed | tf_op | source)
XLA Modules:
  0.0 247.9 jit_solution(18231046583299982153)
XLA Ops:
  3.0 8.4 %all-to-all-start = ((bf16[16,32,768]{2,1,0:T(8,128)(2,1)}), bf16[16,32,768]{2,1,0:T(8,128)(2,1)S(1)}, u32[]{:S(2)}, u32[]{:S(2)}) async-start(bf16[16,32,768]{2,1,0:T(8,128)(2,1)} %constant_dynamic-slice_fusion.2), calls=%async_computation | async-start | bytes 1572864 | tf_op jit(solution)/shard_map/all_to_all | solution.py:936
  12.2 2.1 constant_dynamic-slice_fusion.1
  14.2 17.0 %all-to-all-done = bf16[16,32,768]{2,1,0:T(8,128)(2,1)S(1)} async-done(((bf16[16,32,768]{2,1,0:T(8,128)(2,1)}), bf16[16,32,768]{2,1,0:T(8,128)(2,1)S(1)}, u32[]{:S(2)}, u32[]{:S(2)}) %all-to-all-start) | async-done | bytes 786464 | tf_op jit(solution)/shard_map/all_to_all | solution.py:936
  32.6 4.9 %all-to-all-start.1 = ((bf16[16,32,768]{2,1,0:T(8,128)(2,1)}), bf16[16,32,768]{2,1,0:T(8,128)(2,1)S(1)}, u32[]{:S(2)}, u32[]{:S(2)}) async-start(bf16[16,32,768]{2,1,0:T(8,128)(2,1)} %constant_dynamic-slice_fusion.1), calls=%async_computation.1 | async-start | bytes 1572864 | tf_op jit(solution)/shard_map/all_to_all | solution.py:936
  38.7 9.0 %intake.1 = (bf16[1024,768]{1,0:T(8,128)(2,1)}, bf16[1024,384]{1,0:T(8,128)(2,1)}, bf16[1024,384]{1,0:T(8,128)(2,1)}, bf16[1024,384]{1,0:T(8,128)(2,1)}) custom-call(s32[1]{0:T(128)} %bitcast.core.refs_0_, s32[1,1024]{1,0:T(1,128)} %refs_2_.5, bf16[512,768]{1,0:T(8,128)(2,1)} %bitcast.63, bf16[512,768]{1,0:T(8,128)(2,1)} %collective-permute-done.other_ref, ...), custom_call_target="tpu_custom_call" | custom-call | flops 3422552064 | bytes 6291456 | tf_op jit(solution)/shard_map/intake/pallas_call | solution.py:394
  47.7 14.7 %attend.1 = (bf16[512,384]{1,0:T(8,128)(2,1)}, bf16[512,384]{1,0:T(8,128)(2,1)}, f32[8,1024]{1,0:T(8,128)}) custom-call(s32[1,4]{1,0:T(1,128)} %lengths.3, s32[1]{0:T(128)} %bitcast.core.refs_0_, bf16[1024,384]{1,0:T(8,128)(2,1)} %get-tuple-element.86.q_ref, bf16[1024,384]{1,0:T(8,128)(2,1)} %get-tuple-element.87.k_ref, ...), custom_call_target="tpu_custom_call" | custom-call | flops 6442450944 | bytes 3145728 | tf_op jit(solution)/shard_map/attend/pallas_call | solution.py:169
  68.8 25.5 %row_pass.1 = (bf16[512,768]{1,0:T(8,128)(2,1)}, bf16[512,768]{1,0:T(8,128)(2,1)}, bf16[512,768]{1,0:T(8,128)(2,1)}, bf16[512,1536]{1,0:T(8,128)(2,1)}, bf16[512...) custom-call(s32[1]{0:T(128)} %bitcast.core.refs_0_, ...), custom_call_target="tpu_custom_call" | custom-call | flops 12683575296 | bytes 30670848 | tf_op jit(solution)/shard_map/row_pass/pallas_call | solution.py:629
  94.4 2.4 collective-permute-done.10.refs_4_
  98.9 3.3 %route.2 = bf16[16,32,768]{2,1,0:T(8,128)(2,1)} custom-call(s32[1]{0:T(128)} %bitcast.core.refs_0_, s32[1,1024]{1,0:T(1,128)} %refs_2_.5, s32[1,1024]{1,0:T(1,128)} %refs_2_.5, bf16[512,768]{1,0:T(8,128)(2,1)} %get-tuple-element.97.refs_3_, bf16[512,768]{1,0:T(8,128)(2,1)} %copy-done.26), custom_call_target="tpu_custom_call" | custom-call | flops 805306368 | bytes 2359296 | tf_op jit(solution)/shard_map/route/pallas_call | solution.py:919
  102.2 5.2 %all-to-all-start.2 = ((bf16[16,32,768]{2,1,0:T(8,128)(2,1)}), bf16[16,32,768]{2,1,0:T(8,128)(2,1)}, u32[]{:S(2)}, u32[]{:S(2)}) async-start(bf16[16,32,768]{2,1,0:T(8,128)(2,1)} %route.2), calls=%async_computation.2 | async-start | bytes 1572864 | tf_op jit(solution)/shard_map/all_to_all | solution.py:936
  108.7 8.7 %gradients.4 = (bf16[2,4,48,1920]{3,2,1,0:T(8,128)(2,1)}, bf16[2,4,48,1920]{3,2,1,0:T(8,128)(2,1)}) custom-call(s32[1]{0:T(128)} %bitcast.1.me, bf16[512,768]{1,0:T(8,128)(2,1)} %get-tuple-element.102.refs_0_, bf16[512,768]{1,0:T(8,128)(2,1)} %collective-permute-done.14.refs_1_, bf16[512,1536]{1,0:T(8,128)(2,1)} %get-tuple-element.103.refs_2_, ...), custom_call_target="tpu_custom_call" | custom-call | flops 3019898880 | bytes 9043968 | tf_op jit(solution)/shard_map/gradients/pallas_call | solution.py:777
  117.4 1.8 collective-permute-start.17
  120.4 6.4 %gradients.3 = (bf16[2,4,48,1536]{3,2,1,0:T(8,128)(2,1)}, bf16[2,4,48,1536]{3,2,1,0:T(8,128)(2,1)}) custom-call(s32[1]{0:T(128)} %bitcast.1.me, bf16[512,768]{1,0:T(8,128)(2,1)} %get-tuple-element.98.refs_0_, bf16[512,768]{1,0:T(8,128)(2,1)} %collective-permute-done.11.refs_1_, bf16[512,1536]{1,0:T(8,128)(2,1)} %get-tuple-element.99.refs_2_, ...), custom_call_target="tpu_custom_call" | custom-call | flops 2415919104 | bytes 7864320 | tf_op jit(solution)/shard_map/gradients/pallas_call | solution.py:777
  129.0 21.6 %attend_back.1 = (bf16[512,1152]{1,0:T(8,128)(2,1)}, bf16[512,1152]{1,0:T(8,128)(2,1)}, f32[8,384]{1,0:T(8,128)}) custom-call(s32[1,4]{1,0:T(1,128)} %lengths.3, s32[1]{0:T(128)} %bitcast.core.refs_0_, bf16[1024,384]{1,0:T(8,128)(2,1)} %get-tuple-element.86.q_ref, bf16[512,384]{1,0:T(8,128)(2,1)} %get-tuple-element.111.do_mine, bf16[512,384]{1,0:T(8,128)(2,1)} %copy-done.29, ...), custom_call_target="tpu_custom_call" | custom-call | flops 16106127360 | bytes 6291456 | tf_op jit(solution)/shard_map/attend_back/pallas_call | solution.py:312
  150.7 6.2 %gradients.5 = (bf16[4,48,1152]{2,1,0:T(8,128)(2,1)}, bf16[4,48,1152]{2,1,0:T(8,128)(2,1)}, bf16[4,48,1152]{2,1,0:T(8,128)(2,1)}, bf16[4,48,1152]{2,1,0:T(8,128)(2,1)}) custom-call(s32[1]{0:T(128)} %bitcast.1.me, bf16[1024,768]{1,0:T(8,128)(2,1)} %get-tuple-element.85.x_ref.refs_0_.refs_1_, bf16[1024,768]{1,0:T(8,128)(2,1)} %get-tuple-element.85.x_ref.refs_0_.refs_1_, ...), custom_call_target="tpu_custom_call" | custom-call | flops 1811939328 | bytes 6684672 | tf_op jit(solution)/shard_map/gradients/pallas_call | solution.py:777
  157.9 2.2 convert_add_fusion
  161.7 1.8 convert_add_fusion.1
  164.8 5.9 %input_rows.1.refs_3_ = bf16[512,768]{1,0:T(8,128)(2,1)} custom-call(f32[512,768]{1,0:T(8,128)} %get-tuple-element.124.first_ref, bf16[512,1152]{1,0:T(8,128)(2,1)} %get-tuple-element.114.refs_2_.mine_ref, bf16[512,1152]{1,0:T(8,128)(2,1)} %collective-permute-done.19.other_ref, bf16[768,384]{1,0:T(8,128)(2,1)} %refs_0_.1, bf16[768,384]{1,0:T(8,128)(2,1)} %refs_1_.4, ...), custom_call_target="tpu_custom_call" | custom-call | flops 1811939328 | bytes 6684672 | tf_op jit(solution)/shard_map/input_rows/pallas_call | solution.py:851
  173.4 3.4 %route.3 = bf16[16,40,768]{2,1,0:T(8,128)(2,1)} custom-call(s32[1]{0:T(128)} %bitcast.core.refs_0_, s32[1,1024]{1,0:T(1,128)} %refs_2_.5, s32[1,1024]{1,0:T(1,128)} %refs_2_.5, bf16[512,768]{1,0:T(8,128)(2,1)} %input_rows.1.refs_3_, bf16[512,768]{1,0:T(8,128)(2,1)} %collective-permute-done.20.refs_4_, f32[8,768]{1,0:T(8,128)} %get-tuple-element.125.refs_5_, ...), custom_call_target="tpu_custom_call" | custom-call | flops 805306368 | bytes 2359296 | tf_op jit(solution)/shard_map/route/pallas_call | solution.py:919
  176.8 4.3 %all-to-all-start.3 = ((bf16[16,40,768]{2,1,0:T(8,128)(2,1)}), bf16[16,40,768]{2,1,0:T(8,128)(2,1)}, u32[]{:S(2)}, u32[]{:S(2)}) async-start(bf16[16,40,768]{2,1,0:T(8,128)(2,1)} %route.3), calls=%async_computation.3 | async-start | bytes 1966080 | tf_op jit(solution)/shard_map/all_to_all | solution.py:936
  181.1 8.9 %collective-permute-done.26 = bf16[4,48,1536]{2,1,0:T(8,128)(2,1)} collective-permute-done((bf16[4,48,1536]{2,1,0:T(8,128)(2,1)S(1)}, bf16[4,48,1536]{2,1,0:T(8,128)(2,1)}, u32[]{:S(2)}, u32[]{:S(2)}) %collective-permute-start.26) | collective-permute-done | bytes 589856 | tf_op jit(solution)/shard_map/ppermute | solution.py:1089
  190.9 1.6 convert_add_fusion.3
  194.9 2.0 collective-permute-start.23
  199.4 2.6 %weave.2 = bf16[16,2,32,768]{3,2,1,0:T(8,128)(2,1)} custom-call(s32[1]{0:T(128)} %bitcast.core.refs_0_, bf16[16,32,768]{2,1,0:T(8,128)(2,1)} %all-to-all-done.2.mine_ref, bf16[16,32,768]{2,1,0:T(8,128)(2,1)} %copy-done.8), custom_call_target="tpu_custom_call" | custom-call | flops 1 | bytes 1 | tf_op jit(solution)/shard_map/weave/pallas_call | solution.py:971
  202.0 13.2 %collective-permute-done.28 = bf16[2,48,3456]{2,1,0:T(8,128)(2,1)} collective-permute-done((bf16[2,48,3456]{2,1,0:T(8,128)(2,1)}, bf16[2,48,3456]{2,1,0:T(8,128)(2,1)}, u32[]{:S(2)}, u32[]{:S(2)}) %collective-permute-start.28) | collective-permute-done | bytes 663584 | tf_op jit(solution)/shard_map/ppermute | solution.py:807
  216.5 2.5 collective-permute-start.32
  218.9 2.5 collective-permute-done.24
  221.4 1.5 convert_add_fusion.4
  223.9 2.8 %collective-permute-start.30 = (bf16[48,1152]{1,0:T(8,128)(2,1)S(1)}, bf16[48,1152]{1,0:T(8,128)(2,1)S(1)}, u32[]{:S(2)}, u32[]{:S(2)}) collective-permute-start(bf16[48,1152]{1,0:T(8,128)(2,1)S(1)} %get-tuple-element.150), channel_id=1, source_target_pairs={{0,16},{2,18},{4,20},{6,22},{8,24},{10,26},{12,28},{14,30},{16,0},... | collective-permute-start | bytes 331784 | tf_op jit(solution)/shard_map/ppermute | solution.py:819
  227.4 12.6 %collective-permute-done.32 = bf16[1,48,3456]{2,1,0:T(8,128)(2,1)S(1)} collective-permute-done((bf16[1,48,3456]{2,1,0:T(8,128)(2,1)S(1)}, bf16[1,48,3456]{2,1,0:T(8,128)(2,1)S(1)}, u32[]{:S(2)}, u32[]{:S(2)}) %collective-permute-start.32) | collective-permute-done | bytes 331808 | tf_op jit(solution)/shard_map/ppermute | solution.py:807
  240.1 2.3 collective-permute-done.30
  245.0 2.8 %weave.3 = (bf16[16,2,32,768]{3,2,1,0:T(8,128)(2,1)}, f32[1,24]{1,0:T(1,128)}, f32[1,24]{1,0:T(1,128)}, f32[1,24]{1,0:T(1,128)}, f32[1,24]{1,0:T(1,128)}, /*inde...) custom-call(s32[1]{0:T(128)} %bitcast.core.refs_0_, ...), custom_call_target="tpu_custom_call" | custom-call | flops 1 | bytes 1 | tf_op jit(solution)/shard_map/weave/pallas_call | solution.py:971
  (144 shorter events, 36.9 us)
Async XLA Ops:
  0.7 38.0 %collective-permute-start.2 = (bf16[768,1536]{1,0:T(8,128)(2,1)}, bf16[768,1536]{1,0:T(8,128)(2,1)}, u32[]{:S(2)}, u32[]{:S(2)}) collective-permute-start(bf16[768,1536]{1,0:T(8,128)(2,1)} %up_mine.1), channel_id=1, source_target_pairs={{0,1},{1,0},{2,3},{3,2},{4,5},{5,4},{6,7},{7,6},{8,9},{9,8},{10,11... | collective-permute-start | bytes 7077896 | tf_op jit(solution)/shard_map/ppermute | solution.py:28
  1.2 37.5 %collective-permute-start.3 = (bf16[1536,768]{1,0:T(8,128)(2,1)}, bf16[1536,768]{1,0:T(8,128)(2,1)}, u32[]{:S(2)}, u32[]{:S(2)}) collective-permute-start(bf16[1536,768]{1,0:T(8,128)(2,1)} %down_mine.1), channel_id=1, source_target_pairs={{0,1},{1,0},{2,3},{3,2},{4,5},{5,4},{6,7},{7,6},{8,9},{9,8},{10,11... | collective-permute-start | bytes 7077896 | tf_op jit(solution)/shard_map/ppermute | solution.py:28
  3.0 28.2 %all-to-all-start = ((bf16[16,32,768]{2,1,0:T(8,128)(2,1)}), bf16[16,32,768]{2,1,0:T(8,128)(2,1)S(1)}, u32[]{:S(2)}, u32[]{:S(2)}) async-start(bf16[16,32,768]{2,1,0:T(8,128)(2,1)} %constant_dynamic-slice_fusion.2), calls=%async_computation | async-start | bytes 1572864 | tf_op jit(solution)/shard_map/all_to_all | solution.py:936
  11.5 19.8 %collective-permute-start.1 = (bf16[384,768]{1,0:T(8,128)(2,1)}, bf16[384,768]{1,0:T(8,128)(2,1)}, u32[]{:S(2)}, u32[]{:S(2)}) collective-permute-start(bf16[384,768]{1,0:T(8,128)(2,1)} %out_mine.1), channel_id=1, source_target_pairs={{0,1},{1,0},{2,3},{3,2},{4,5},{5,4},{6,7},{7,6},{8,9},{9,8},{10,11... | collective-permute-start | bytes 1769480 | tf_op jit(solution)/shard_map/ppermute | solution.py:28
  11.6 20.2 %collective-permute-start.4 = (bf16[768,384]{1,0:T(8,128)(2,1)S(1)}, bf16[768,384]{1,0:T(8,128)(2,1)S(1)}, u32[]{:S(2)}, u32[]{:S(2)}) collective-permute-start(bf16[768,384]{1,0:T(8,128)(2,1)S(1)} %copy-done.9), channel_id=1, source_target_pairs={{0,1},{1,0},{2,3},{3,2},{4,5},{5,4},{6,7},{7,6},{8,9},{9,8},{10,11... | collective-permute-start | bytes 1769480 | tf_op jit(solution)/shard_map/ppermute | solution.py:28
  12.1 19.2 %collective-permute-start.7 = (f32[1536]{0:T(1024)S(1)}, f32[1536]{0:T(1024)S(1)}, u32[]{:S(2)}, u32[]{:S(2)}) collective-permute-start(f32[1536]{0:T(1024)S(1)} %copy-done.15), channel_id=1, source_target_pairs={{0,1},{1,0},{2,3},{3,2},{4,5},{5,4},{6,7},{7,6},{8,9},{9,8},{10,11... | collective-permute-start | bytes 18440 | tf_op jit(solution)/shard_map/ppermute | solution.py:28
  31.2 7.4 %collective-permute-start = (bf16[512,768]{1,0:T(8,128)(2,1)S(1)}, bf16[512,768]{1,0:T(8,128)(2,1)}, u32[]{:S(2)}, u32[]{:S(2)}) collective-permute-start(bf16[512,768]{1,0:T(8,128)(2,1)S(1)} %bitcast.62), channel_id=1, source_target_pairs={{0,1},{1,0},{2,3},{3,2},{4,5},{5,4},{6,7},{7,6},{8,9},{9,8},{10,11... | collective-permute-start | bytes 2359304 | tf_op jit(solution)/shard_map/ppermute | solution.py:28
  31.3 7.4 %collective-permute-start.5 = (bf16[768,384]{1,0:T(8,128)(2,1)S(1)}, bf16[768,384]{1,0:T(8,128)(2,1)}, u32[]{:S(2)}, u32[]{:S(2)}) collective-permute-start(bf16[768,384]{1,0:T(8,128)(2,1)S(1)} %copy-done.10), channel_id=1, source_target_pairs={{0,1},{1,0},{2,3},{3,2},{4,5},{5,4},{6,7},{7,6},{8,9},{9,8},{10,11... | collective-permute-start | bytes 1769480 | tf_op jit(solution)/shard_map/ppermute | solution.py:28
  31.8 6.9 %collective-permute-start.6 = (bf16[768,384]{1,0:T(8,128)(2,1)S(1)}, bf16[768,384]{1,0:T(8,128)(2,1)S(1)}, u32[]{:S(2)}, u32[]{:S(2)}) collective-permute-start(bf16[768,384]{1,0:T(8,128)(2,1)S(1)} %copy-done.11), channel_id=1, source_target_pairs={{0,1},{1,0},{2,3},{3,2},{4,5},{5,4},{6,7},{7,6},{8,9},{9,8},{10,11... | collective-permute-start | bytes 1769480 | tf_op jit(solution)/shard_map/ppermute | solution.py:28
  32.6 29.9 %all-to-all-start.1 = ((bf16[16,32,768]{2,1,0:T(8,128)(2,1)}), bf16[16,32,768]{2,1,0:T(8,128)(2,1)S(1)}, u32[]{:S(2)}, u32[]{:S(2)}) async-start(bf16[16,32,768]{2,1,0:T(8,128)(2,1)} %constant_dynamic-slice_fusion.1), calls=%async_computation.1 | async-start | bytes 1572864 | tf_op jit(solution)/shard_map/all_to_all | solution.py:936
  97.7 9.8 %collective-permute-start.15 = (bf16[512,1536]{1,0:T(8,128)(2,1)}, bf16[512,1536]{1,0:T(8,128)(2,1)S(1)}, u32[]{:S(2)}, u32[]{:S(2)}) collective-permute-start(bf16[512,1536]{1,0:T(8,128)(2,1)} %get-tuple-element.104), channel_id=1, source_target_pairs={{0,1},{1,0},{2,3},{3,2},{4,5},{5,4},{6,7},{7,6},{8,9},{9,8},{10,11... | collective-permute-start | bytes 4718600 | tf_op jit(solution)/shard_map/ppermute | solution.py:28
  97.9 21.3 %collective-permute-start.12 = (bf16[512,1536]{1,0:T(8,128)(2,1)}, bf16[512,1536]{1,0:T(8,128)(2,1)S(1)}, u32[]{:S(2)}, u32[]{:S(2)}) collective-permute-start(bf16[512,1536]{1,0:T(8,128)(2,1)} %get-tuple-element.100), channel_id=1, source_target_pairs={{0,1},{1,0},{2,3},{3,2},{4,5},{5,4},{6,7},{7,6},{8,9},{9,8},{10,11... | collective-permute-start | bytes 4718600 | tf_op jit(solution)/shard_map/ppermute | solution.py:28
  98.3 9.1 %collective-permute-start.14 = (bf16[512,768]{1,0:T(8,128)(2,1)}, bf16[512,768]{1,0:T(8,128)(2,1)}, u32[]{:S(2)}, u32[]{:S(2)}) collective-permute-start(bf16[512,768]{1,0:T(8,128)(2,1)} %get-tuple-element.102.refs_0_), channel_id=1, source_target_pairs={{0,1},{1,0},{2,3},{3,2},{4,5},{5,4},{6,7},{7,6},{8,9},{9,8},{10,11... | collective-permute-start | bytes 2359304 | tf_op jit(solution)/shard_map/ppermute | solution.py:28
  98.4 9.2 %collective-permute-start.16 = (bf16[512,768]{1,0:T(8,128)(2,1)}, bf16[512,768]{1,0:T(8,128)(2,1)}, u32[]{:S(2)}, u32[]{:S(2)}) collective-permute-start(bf16[512,768]{1,0:T(8,128)(2,1)} %get-tuple-element.105.refs_4_), channel_id=1, source_target_pairs={{0,1},{1,0},{2,3},{3,2},{4,5},{5,4},{6,7},{7,6},{8,9},{9,8},{10,11... | collective-permute-start | bytes 2359304 | tf_op jit(solution)/shard_map/ppermute | solution.py:28
  98.8 20.5 %collective-permute-start.11 = (bf16[512,768]{1,0:T(8,128)(2,1)}, bf16[512,768]{1,0:T(8,128)(2,1)}, u32[]{:S(2)}, u32[]{:S(2)}) collective-permute-start(bf16[512,768]{1,0:T(8,128)(2,1)} %get-tuple-element.98.refs_0_), channel_id=1, source_target_pairs={{0,1},{1,0},{2,3},{3,2},{4,5},{5,4},{6,7},{7,6},{8,9},{9,8},{10,11... | collective-permute-start | bytes 2359304 | tf_op jit(solution)/shard_map/ppermute | solution.py:28
  102.2 54.7 %all-to-all-start.2 = ((bf16[16,32,768]{2,1,0:T(8,128)(2,1)}), bf16[16,32,768]{2,1,0:T(8,128)(2,1)}, u32[]{:S(2)}, u32[]{:S(2)}) async-start(bf16[16,32,768]{2,1,0:T(8,128)(2,1)} %route.2), calls=%async_computation.2 | async-start | bytes 1572864 | tf_op jit(solution)/shard_map/all_to_all | solution.py:936
  107.4 20.8 %collective-permute-start.18 = (bf16[512,384]{1,0:T(8,128)(2,1)S(1)}, bf16[512,384]{1,0:T(8,128)(2,1)S(1)}, u32[]{:S(2)}, u32[]{:S(2)}) collective-permute-start(bf16[512,384]{1,0:T(8,128)(2,1)S(1)} %copy-done.28), channel_id=1, source_target_pairs={{0,1},{1,0},{2,3},{3,2},{4,5},{5,4},{6,7},{7,6},{8,9},{9,8},{10,11... | collective-permute-start | bytes 1179656 | tf_op jit(solution)/shard_map/ppermute | solution.py:28
  117.4 39.5 %collective-permute-start.17 = (bf16[2,4,48,1920]{3,2,1,0:T(8,128)(2,1)}, bf16[2,4,48,1920]{3,2,1,0:T(8,128)(2,1)}, u32[]{:S(2)}, u32[]{:S(2)}) collective-permute-start(bf16[2,4,48,1920]{3,2,1,0:T(8,128)(2,1)} %get-tuple-element.106), channel_id=1, source_target_pairs={{0,4},{2,6},{4,0},{6,2},{8,12},{10,14},{12,8},{14,10},{16,20},{18,... | collective-permute-start | bytes 4423688 | tf_op jit(solution)/shard_map/ppermute | solution.py:1076
  126.8 30.1 %collective-permute-start.13 = (bf16[2,4,48,1536]{3,2,1,0:T(8,128)(2,1)}, bf16[2,4,48,1536]{3,2,1,0:T(8,128)(2,1)S(1)}, u32[]{:S(2)}, u32[]{:S(2)}) collective-permute-start(bf16[2,4,48,1536]{3,2,1,0:T(8,128)(2,1)} %get-tuple-element.101), channel_id=1, source_target_pairs={{0,2},{2,0},{4,6},{6,4},{8,10},{10,8},{12,14},{14,12},{16,18},{18,... | collective-permute-start | bytes 3538952 | tf_op jit(solution)/shard_map/ppermute | solution.py:1076
  150.6 14.1 %collective-permute-start.19 = (bf16[512,1152]{1,0:T(8,128)(2,1)}, bf16[512,1152]{1,0:T(8,128)(2,1)}, u32[]{:S(2)}, u32[]{:S(2)}) collective-permute-start(bf16[512,1152]{1,0:T(8,128)(2,1)} %get-tuple-element.115.refs_3_), channel_id=1, source_target_pairs={{0,1},{1,0},{2,3},{3,2},{4,5},{5,4},{6,7},{7,6},{8,9},{9,8},{10,11... | collective-permute-start | bytes 3538952 | tf_op jit(solution)/shard_map/ppermute | solution.py:28
  171.2 19.7 %collective-permute-start.27 = (bf16[4,48,1920]{2,1,0:T(8,128)(2,1)}, bf16[4,48,1920]{2,1,0:T(8,128)(2,1)}, u32[]{:S(2)}, u32[]{:S(2)}) collective-permute-start(bf16[4,48,1920]{2,1,0:T(8,128)(2,1)} %fusion), channel_id=1, source_target_pairs={{0,2},{2,0},{4,6},{6,4},{8,10},{10,8},{12,14},{14,12},{16,18},{18,... | collective-permute-start | bytes 2211848 | tf_op jit(solution)/shard_map/ppermute | solution.py:1089
  171.2 18.8 %collective-permute-start.26 = (bf16[4,48,1536]{2,1,0:T(8,128)(2,1)S(1)}, bf16[4,48,1536]{2,1,0:T(8,128)(2,1)}, u32[]{:S(2)}, u32[]{:S(2)}) collective-permute-start(bf16[4,48,1536]{2,1,0:T(8,128)(2,1)S(1)} %fusion.2), channel_id=1, source_target_pairs={{0,4},{2,6},{4,0},{6,2},{8,12},{10,14},{12,8},{14,10},{16,20},{18,... | collective-permute-start | bytes 1769480 | tf_op jit(solution)/shard_map/ppermute | solution.py:1089
  176.8 38.4 %all-to-all-start.3 = ((bf16[16,40,768]{2,1,0:T(8,128)(2,1)}), bf16[16,40,768]{2,1,0:T(8,128)(2,1)}, u32[]{:S(2)}, u32[]{:S(2)}) async-start(bf16[16,40,768]{2,1,0:T(8,128)(2,1)} %route.3), calls=%async_computation.3 | async-start | bytes 1966080 | tf_op jit(solution)/shard_map/all_to_all | solution.py:936
  194.9 20.3 %collective-permute-start.28 = (bf16[2,48,3456]{2,1,0:T(8,128)(2,1)}, bf16[2,48,3456]{2,1,0:T(8,128)(2,1)}, u32[]{:S(2)}, u32[]{:S(2)}) collective-permute-start(bf16[2,48,3456]{2,1,0:T(8,128)(2,1)} %fusion.1), channel_id=1, source_target_pairs={{0,8},{2,10},{4,12},{6,14},{8,0},{10,2},{12,4},{14,6},{16,24},{18,... | collective-permute-start | bytes 1990664 | tf_op jit(solution)/shard_map/ppermute | solution.py:807
  194.9 24.0 %collective-permute-start.23 = (bf16[4,48,1152]{2,1,0:T(8,128)(2,1)}, bf16[4,48,1152]{2,1,0:T(8,128)(2,1)}, u32[]{:S(2)}, u32[]{:S(2)}) collective-permute-start(bf16[4,48,1152]{2,1,0:T(8,128)(2,1)} %get-tuple-element.117), channel_id=1, source_target_pairs={{0,2},{2,0},{4,6},{6,4},{8,10},{10,8},{12,14},{14,12},{16,18},{18,... | collective-permute-start | bytes 1327112 | tf_op jit(solution)/shard_map/ppermute | solution.py:824
  196.9 24.5 %collective-permute-start.24 = (bf16[4,48,1152]{2,1,0:T(8,128)(2,1)}, bf16[4,48,1152]{2,1,0:T(8,128)(2,1)}, u32[]{:S(2)}, u32[]{:S(2)}) collective-permute-start(bf16[4,48,1152]{2,1,0:T(8,128)(2,1)} %get-tuple-element.118), channel_id=1, source_target_pairs={{0,4},{2,6},{4,0},{6,2},{8,12},{10,14},{12,8},{14,10},{16,20},{18,... | collective-permute-start | bytes 1327112 | tf_op jit(solution)/shard_map/ppermute | solution.py:824
  197.5 24.0 %collective-permute-start.25 = (bf16[4,48,1152]{2,1,0:T(8,128)(2,1)}, bf16[4,48,1152]{2,1,0:T(8,128)(2,1)}, u32[]{:S(2)}, u32[]{:S(2)}) collective-permute-start(bf16[4,48,1152]{2,1,0:T(8,128)(2,1)} %get-tuple-element.119), channel_id=1, source_target_pairs={{0,6},{2,4},{4,2},{6,0},{8,14},{10,12},{12,10},{14,8},{16,22},{18,... | collective-permute-start | bytes 1327112 | tf_op jit(solution)/shard_map/ppermute | solution.py:824
  216.5 23.5 %collective-permute-start.32 = (bf16[1,48,3456]{2,1,0:T(8,128)(2,1)S(1)}, bf16[1,48,3456]{2,1,0:T(8,128)(2,1)S(1)}, u32[]{:S(2)}, u32[]{:S(2)}) collective-permute-start(bf16[1,48,3456]{2,1,0:T(8,128)(2,1)S(1)} %dynamic-slice_convert_fusion), channel_id=1, source_target_pairs={{0,16},{2,18},{4,20},{6,22},{8,24},{10,26},{12,28},{14,30},{16,0},... | collective-permute-start | bytes 995336 | tf_op jit(solution)/shard_map/ppermute | solution.py:807
  223.0 17.1 %collective-permute-start.29 = (bf16[48,1152]{1,0:T(8,128)(2,1)S(1)}, bf16[48,1152]{1,0:T(8,128)(2,1)S(1)}, u32[]{:S(2)}, u32[]{:S(2)}) collective-permute-start(bf16[48,1152]{1,0:T(8,128)(2,1)S(1)} %get-tuple-element.151), channel_id=1, source_target_pairs={{0,8},{2,10},{4,12},{6,14},{8,0},{10,2},{12,4},{14,6},{16,24},{18,... | collective-permute-start | bytes 331784 | tf_op jit(solution)/shard_map/ppermute | solution.py:819
  223.9 18.4 %collective-permute-start.30 = (bf16[48,1152]{1,0:T(8,128)(2,1)S(1)}, bf16[48,1152]{1,0:T(8,128)(2,1)S(1)}, u32[]{:S(2)}, u32[]{:S(2)}) collective-permute-start(bf16[48,1152]{1,0:T(8,128)(2,1)S(1)} %get-tuple-element.150), channel_id=1, source_target_pairs={{0,16},{2,18},{4,20},{6,22},{8,24},{10,26},{12,28},{14,30},{16,0},... | collective-permute-start | bytes 331784 | tf_op jit(solution)/shard_map/ppermute | solution.py:819
  226.7 15.6 %collective-permute-start.31 = (bf16[48,1152]{1,0:T(8,128)(2,1)S(1)}, bf16[48,1152]{1,0:T(8,128)(2,1)S(1)}, u32[]{:S(2)}, u32[]{:S(2)}) collective-permute-start(bf16[48,1152]{1,0:T(8,128)(2,1)S(1)} %get-tuple-element.149), channel_id=1, source_target_pairs={{0,24},{2,26},{4,28},{6,30},{8,16},{10,18},{12,20},{14,22},{16,8},... | collective-permute-start | bytes 331784 | tf_op jit(solution)/shard_map/ppermute | solution.py:819
  227.4 16.6 %collective-permute-start.22 = (bf16[16,40,768]{2,1,0:T(8,128)(2,1)}, bf16[16,40,768]{2,1,0:T(8,128)(2,1)S(1)}, u32[]{:S(2)}, u32[]{:S(2)}) collective-permute-start(bf16[16,40,768]{2,1,0:T(8,128)(2,1)} %all-to-all-done.3.mine_ref), channel_id=1, source_target_pairs={{0,1},{1,0},{2,3},{3,2},{4,5},{5,4},{6,7},{7,6},{8,9},{9,8},{10,11... | collective-permute-start | bytes 2949128 | tf_op jit(solution)/shard_map/ppermute | solution.py:28
  (36 other events, 310.5 us)
where the time goes:
time: 250 us; the launch traced here: 248 us
  Pallas kernels  110 us (44%)
  waiting for transfers between devices  61.2 us (24%)
  starting transfers between devices  41.8 us (17%)
  local copies, waits for them, and re-layouts  23.8 us (10%)
  other arithmetic  9.83 us (4%)
    ppermute x2, waiting for transfers between devices, far_step(): got = after(lax.ppermute(sent, 'dp', pairs(groups, near << bit)), first)  25.7 us
    pallas_call x1, Pallas kernels, row_pass(): pl.pallas_call(functools.partial(rows_kernel, run_rows), grid_spec=pltpu....  25.5 us
    all_to_all x4, starting transfers between devices, exchange(): return lax.all_to_all(values, 'dp', split_axis=0, concat_axis=0, tiled=True)  22.8 us
    pallas_call x1, Pallas kernels, attention_backward(): pl.pallas_call(backward_kernel, grid_spec=pltpu.PrefetchScalarGridSpec(nu...  21.6 us
    pallas_call x3, Pallas kernels, gradients(): pl.pallas_call(functools.partial(gradient_kernel, chunks, near, share, ha...  21.3 us
    all_to_all x4, waiting for transfers between devices, exchange(): return lax.all_to_all(values, 'dp', split_axis=0, concat_axis=0, tiled=True)  17 us
    pallas_call x1, Pallas kernels, attention_forward(): pl.pallas_call(forward_kernel, grid_spec=pltpu.PrefetchScalarGridSpec(num...  14.7 us
    unnamed x62, local copies, waits for them, and re-layouts  9.99 us
  transfers between devices with their start and end apart: 37, of which 9 were waited for; matrix products, arithmetic and copies ran while one was open for 10% of the time, Pallas kernels for 31%

commit v1 on v0

--- a/solution.py
+++ b/solution.py
@@ -834,16 +834,17 @@
 def input_kernel(first_ref, mine_ref, other_ref, *refs):
     weights, out_ref = refs[:-1], refs[-1]
     total = first_ref[...]
-    for n, rows in enumerate((mine_ref, other_ref)):
-        wide = jnp.concatenate([weight[...] for weight in weights[3 * n : 3 * n + 3]], axis=1)
-        total = total + nt(rows[...], wide)
+    width = weights[0].shape[1]
+    for n, weight in enumerate(weights):
+        rows = (mine_ref, other_ref)[n // 3]
+        total = total + nt(rows[:, n % 3 * width : (n % 3 + 1) * width], weight[...])
     out_ref[...] = total.astype(BF16)
 
 
 def input_rows(first_grad, mine_rows, other_rows, weights):
     half, features = first_grad.shape
     wide = other_rows.shape[1]
-    count = 256
+    count = 512
 
     def tile(n):
         return pl.BlockSpec((count, n), lambda i: (i, 0))
@@ -1030,11 +1031,17 @@
     bias_other = swap(up_bias)
     vectors = [v.reshape(1, -1) for v in vectors + [up_bias, bias_other]]
     qkv_other = [swap(w) for w in qkv_weights]
-    token_got = after(swap(token_rows), (out_other, up_other, down_other, qkv_other, bias_other))
+    biases = [query_bias.reshape(1, -1), value_bias.reshape(1, -1)]
+    early = (out_other, up_other, down_other, qkv_other)
+    token_rows, vectors, biases, early = lax.optimization_barrier(
+        (token_rows, vectors, biases, early)
+    )
+    out_other, up_other, down_other, qkv_other = early
+    token_got = swap(token_rows)
 
     inputs, query_rows, key_rows, value_rows = intake(
         core, token_slot, run_rows, token_rows, token_got, qkv_weights,
-        (query_bias.reshape(1, -1), value_bias.reshape(1, -1)),
+        biases,
     )
     mixed_mine, mixed_theirs, logsum = attention_forward(seq_lengths, core, query_rows, key_rows, value_rows)
     cot_rows = after(cot_raw, mixed_mine)

time: 250 us -> 249 us (level)
  waiting for transfers between devices: 61.2 us -> 55 us
  starting transfers between devices: 41.8 us -> 46.6 us
    all_to_all x4, waiting for transfers between devices: 17 us -> 9.2 us  [exchange(): return lax.all_to_all(values, 'dp', split_axis=0, concat_axis=0, tiled=True)]
    ppermute x21, waiting for transfers between devices: 3.93 us -> 8.04 us  [swap(): return lax.ppermute(values, 'tensor', SWAP)]
    all_to_all x4, starting transfers between devices: 22.8 us -> 25.5 us  [exchange(): return lax.all_to_all(values, 'dp', split_axis=0, concat_axis=0, tiled=True)]
  transfers between devices with their start and end apart: 37 -> 37, of which waited for: 9 -> 11; matrix products, arithmetic and copies ran while one was open for 10% -> 10% of each run, Pallas kernels for 31% -> 30%
where the time goes in v1:
time: 249 us; the launch traced here: 248 us
  Pallas kernels  110 us (44%)
  waiting for transfers between devices  55 us (22%)
  starting transfers between devices  46.6 us (19%)
  local copies, waits for them, and re-layouts  24.7 us (10%)
  other arithmetic  9.83 us (4%)
    all_to_all x4, starting transfers between devices, exchange(): return lax.all_to_all(values, 'dp', split_axis=0, concat_axis=0, tiled=True)  25.5 us
    pallas_call x1, Pallas kernels, row_pass(): pl.pallas_call(functools.partial(rows_kernel, run_rows), grid_spec=pltpu....  25.4 us
    ppermute x2, waiting for transfers between devices, far_step(): got = after(lax.ppermute(sent, 'dp', pairs(groups, near << bit)), first)  25 us
    pallas_call x1, Pallas kernels, attention_backward(): pl.pallas_call(backward_kernel, grid_spec=pltpu.PrefetchScalarGridSpec(nu...  21.6 us
    pallas_call x3, Pallas kernels, gradients(): pl.pallas_call(functools.partial(gradient_kernel, chunks, near, share, ha...  21.3 us
    pallas_call x1, Pallas kernels, attention_forward(): pl.pallas_call(forward_kernel, grid_spec=pltpu.PrefetchScalarGridSpec(num...  14.6 us
    unnamed x62, local copies, waits for them, and re-layouts  10.9 us
    ppermute x2, waiting for transfers between devices, local(): lax.ppermute(v, 'dp', pairs(groups, 2 - n))  9.25 us
  transfers between devices with their start and end apart: 37, of which 11 were waited for; matrix products, arithmetic and copies ran while one was open for 10% of the time, Pallas kernels for 30%

profile of v1, /device:TPU:0, one launch (start us, length us, event | category | flops | bytes accessed | tf_op | source)
XLA Modules:
  0.0 247.7 jit_solution(9090113897979646891)
XLA Ops:
  3.1 8.3 %all-to-all-start = ((bf16[16,32,768]{2,1,0:T(8,128)(2,1)}), bf16[16,32,768]{2,1,0:T(8,128)(2,1)S(1)}, u32[]{:S(2)}, u32[]{:S(2)}) async-start(bf16[16,32,768]{2,1,0:T(8,128)(2,1)} %constant_dynamic-slice_fusion.2), calls=%async_computation | async-start | bytes 1572864 | tf_op jit(solution)/shard_map/all_to_all | solution.py:937
  19.3 2.1 constant_dynamic-slice_fusion.1
  22.0 9.2 %all-to-all-done = bf16[16,32,768]{2,1,0:T(8,128)(2,1)S(1)} async-done(((bf16[16,32,768]{2,1,0:T(8,128)(2,1)}), bf16[16,32,768]{2,1,0:T(8,128)(2,1)S(1)}, u32[]{:S(2)}, u32[]{:S(2)}) %all-to-all-start) | async-done | bytes 786464 | tf_op jit(solution)/shard_map/all_to_all | solution.py:937
  32.1 4.9 %all-to-all-start.1 = ((bf16[16,32,768]{2,1,0:T(8,128)(2,1)}), bf16[16,32,768]{2,1,0:T(8,128)(2,1)S(1)}, u32[]{:S(2)}, u32[]{:S(2)}) async-start(bf16[16,32,768]{2,1,0:T(8,128)(2,1)} %constant_dynamic-slice_fusion.1), calls=%async_computation.1 | async-start | bytes 1572864 | tf_op jit(solution)/shard_map/all_to_all | solution.py:937
  37.9 8.8 %intake.1 = (bf16[1024,768]{1,0:T(8,128)(2,1)}, bf16[1024,384]{1,0:T(8,128)(2,1)}, bf16[1024,384]{1,0:T(8,128)(2,1)}, bf16[1024,384]{1,0:T(8,128)(2,1)}) custom-call(s32[1]{0:T(128)} %bitcast.core.refs_0_, s32[1,1024]{1,0:T(1,128)} %refs_2_.5, bf16[512,768]{1,0:T(8,128)(2,1)} %bitcast.61, bf16[512,768]{1,0:T(8,128)(2,1)} %copy-done.27, ...), custom_call_target="tpu_custom_call" | custom-call | flops 3422552064 | bytes 6291456 | tf_op jit(solution)/shard_map/intake/pallas_call | solution.py:394
  46.6 14.6 %attend.1 = (bf16[512,384]{1,0:T(8,128)(2,1)}, bf16[512,384]{1,0:T(8,128)(2,1)}, f32[8,1024]{1,0:T(8,128)}) custom-call(s32[1,4]{1,0:T(1,128)} %lengths.3, s32[1]{0:T(128)} %bitcast.core.refs_0_, bf16[1024,384]{1,0:T(8,128)(2,1)} %get-tuple-element.104.q_ref, bf16[1024,384]{1,0:T(8,128)(2,1)} %get-tuple-element.105.k_ref, ...), custom_call_target="tpu_custom_call" | custom-call | flops 6442450944 | bytes 3145728 | tf_op jit(solution)/shard_map/attend/pallas_call | solution.py:169
  61.8 2.5 %collective-permute-done.8.mixed_other = bf16[512,384]{1,0:T(8,128)(2,1)S(1)} collective-permute-done((bf16[512,384]{1,0:T(8,128)(2,1)}, bf16[512,384]{1,0:T(8,128)(2,1)S(1)}, u32[]{:S(2)}, u32[]{:S(2)}) %collective-permute-start.8) | collective-permute-done | bytes 393248 | tf_op jit(solution)/shard_map/ppermute | solution.py:28
  65.4 25.4 %row_pass.1 = (bf16[512,768]{1,0:T(8,128)(2,1)}, bf16[512,768]{1,0:T(8,128)(2,1)}, bf16[512,768]{1,0:T(8,128)(2,1)}, bf16[512,1536]{1,0:T(8,128)(2,1)}, bf16[512...) custom-call(s32[1]{0:T(128)} %bitcast.core.refs_0_, ...), custom_call_target="tpu_custom_call" | custom-call | flops 12683575296 | bytes 30670848 | tf_op jit(solution)/shard_map/row_pass/pallas_call | solution.py:629
  91.0 2.4 collective-permute-done.10.refs_4_
  95.5 3.3 %route.2 = bf16[16,32,768]{2,1,0:T(8,128)(2,1)} custom-call(s32[1]{0:T(128)} %bitcast.core.refs_0_, s32[1,1024]{1,0:T(1,128)} %refs_2_.5, s32[1,1024]{1,0:T(1,128)} %refs_2_.5, bf16[512,768]{1,0:T(8,128)(2,1)} %get-tuple-element.126.refs_3_, bf16[512,768]{1,0:T(8,128)(2,1)} %copy-done.25), custom_call_target="tpu_custom_call" | custom-call | flops 805306368 | bytes 2359296 | tf_op jit(solution)/shard_map/route/pallas_call | solution.py:920
  98.8 7.0 %all-to-all-start.2 = ((bf16[16,32,768]{2,1,0:T(8,128)(2,1)}), bf16[16,32,768]{2,1,0:T(8,128)(2,1)}, u32[]{:S(2)}, u32[]{:S(2)}) async-start(bf16[16,32,768]{2,1,0:T(8,128)(2,1)} %route.2), calls=%async_computation.2 | async-start | bytes 1572864 | tf_op jit(solution)/shard_map/all_to_all | solution.py:937
  107.1 8.7 %gradients.4 = (bf16[2,4,48,1920]{3,2,1,0:T(8,128)(2,1)}, bf16[2,4,48,1920]{3,2,1,0:T(8,128)(2,1)}) custom-call(s32[1]{0:T(128)} %bitcast.1.me, bf16[512,768]{1,0:T(8,128)(2,1)} %get-tuple-element.131.refs_0_, bf16[512,768]{1,0:T(8,128)(2,1)} %collective-permute-done.14.refs_1_, bf16[512,1536]{1,0:T(8,128)(2,1)} %get-tuple-element.132.refs_2_, ...), custom_call_target="tpu_custom_call" | custom-call | flops 3019898880 | bytes 9043968 | tf_op jit(solution)/shard_map/gradients/pallas_call | solution.py:777
  115.7 1.8 collective-permute-start.17
  118.8 6.4 %gradients.3 = (bf16[2,4,48,1536]{3,2,1,0:T(8,128)(2,1)}, bf16[2,4,48,1536]{3,2,1,0:T(8,128)(2,1)}) custom-call(s32[1]{0:T(128)} %bitcast.1.me, bf16[512,768]{1,0:T(8,128)(2,1)} %get-tuple-element.127.refs_0_, bf16[512,768]{1,0:T(8,128)(2,1)} %collective-permute-done.11.refs_1_, bf16[512,1536]{1,0:T(8,128)(2,1)} %get-tuple-element.128.refs_2_, ...), custom_call_target="tpu_custom_call" | custom-call | flops 2415919104 | bytes 7864320 | tf_op jit(solution)/shard_map/gradients/pallas_call | solution.py:777
  127.3 21.6 %attend_back.1 = (bf16[512,1152]{1,0:T(8,128)(2,1)}, bf16[512,1152]{1,0:T(8,128)(2,1)}, f32[8,384]{1,0:T(8,128)}) custom-call(s32[1,4]{1,0:T(1,128)} %lengths.3, s32[1]{0:T(128)} %bitcast.core.refs_0_, bf16[1024,384]{1,0:T(8,128)(2,1)} %get-tuple-element.104.q_ref, bf16[512,384]{1,0:T(8,128)(2,1)} %get-tuple-element.140.do_mine, ...), custom_call_target="tpu_custom_call" | custom-call | flops 16106127360 | bytes 6291456 | tf_op jit(solution)/shard_map/attend_back/pallas_call | solution.py:312
  149.0 6.2 %gradients.5 = (bf16[4,48,1152]{2,1,0:T(8,128)(2,1)}, bf16[4,48,1152]{2,1,0:T(8,128)(2,1)}, bf16[4,48,1152]{2,1,0:T(8,128)(2,1)}, bf16[4,48,1152]{2,1,0:T(8,128)(2,1)}) custom-call(s32[1]{0:T(128)} %bitcast.1.me, bf16[1024,768]{1,0:T(8,128)(2,1)} %get-tuple-element.103.x_ref.refs_0_.refs_1_, bf16[1024,768]{1,0:T(8,128)(2,1)} %get-tuple-element.103.x_ref.refs_0_.refs_1_, ...), custom_call_target="tpu_custom_call" | custom-call | flops 1811939328 | bytes 6684672 | tf_op jit(solution)/shard_map/gradients/pallas_call | solution.py:777
  156.3 2.2 convert_add_fusion
  160.0 1.8 convert_add_fusion.1
  163.1 6.6 %input_rows.1.refs_3_ = bf16[512,768]{1,0:T(8,128)(2,1)} custom-call(f32[512,768]{1,0:T(8,128)} %get-tuple-element.153.first_ref, bf16[512,1152]{1,0:T(8,128)(2,1)} %get-tuple-element.143.refs_2_.mine_ref, bf16[512,1152]{1,0:T(8,128)(2,1)} %collective-permute-done.19.other_ref, bf16[768,384]{1,0:T(8,128)(2,1)} %refs_0_.1, bf16[768,384]{1,0:T(8,128)(2,1)} %refs_1_.4, ...), custom_call_target="tpu_custom_call" | custom-call | flops 1811939328 | bytes 6684672 | tf_op jit(solution)/shard_map/input_rows/pallas_call | solution.py:852
  171.0 1.5 collective-permute-done.20.refs_4_
  172.5 3.4 %route.3 = bf16[16,40,768]{2,1,0:T(8,128)(2,1)} custom-call(s32[1]{0:T(128)} %bitcast.core.refs_0_, s32[1,1024]{1,0:T(1,128)} %refs_2_.5, s32[1,1024]{1,0:T(1,128)} %refs_2_.5, bf16[512,768]{1,0:T(8,128)(2,1)} %input_rows.1.refs_3_, bf16[512,768]{1,0:T(8,128)(2,1)} %collective-permute-done.20.refs_4_, f32[8,768]{1,0:T(8,128)} %get-tuple-element.157.refs_5_, ...), custom_call_target="tpu_custom_call" | custom-call | flops 805306368 | bytes 2359296 | tf_op jit(solution)/shard_map/route/pallas_call | solution.py:920
  175.8 5.4 %all-to-all-start.3 = ((bf16[16,40,768]{2,1,0:T(8,128)(2,1)}), bf16[16,40,768]{2,1,0:T(8,128)(2,1)}, u32[]{:S(2)}, u32[]{:S(2)}) async-start(bf16[16,40,768]{2,1,0:T(8,128)(2,1)} %route.3), calls=%async_computation.3 | async-start | bytes 1966080 | tf_op jit(solution)/shard_map/all_to_all | solution.py:937
  181.2 9.2 %collective-permute-done.26 = bf16[4,48,1536]{2,1,0:T(8,128)(2,1)} collective-permute-done((bf16[4,48,1536]{2,1,0:T(8,128)(2,1)S(1)}, bf16[4,48,1536]{2,1,0:T(8,128)(2,1)}, u32[]{:S(2)}, u32[]{:S(2)}) %collective-permute-start.26) | collective-permute-done | bytes 589856 | tf_op jit(solution)/shard_map/ppermute | solution.py:1096
  190.4 1.6 convert_add_fusion.3
  196.5 2.5 %collective-permute-start.25 = (bf16[4,48,1152]{2,1,0:T(8,128)(2,1)}, bf16[4,48,1152]{2,1,0:T(8,128)(2,1)}, u32[]{:S(2)}, u32[]{:S(2)}) collective-permute-start(bf16[4,48,1152]{2,1,0:T(8,128)(2,1)} %get-tuple-element.148), channel_id=1, source_target_pairs={{0,6},{2,4},{4,2},{6,0},{8,14},{10,12},{12,10},{14,8},{16,22},{18,... | collective-permute-start | bytes 1327112 | tf_op jit(solution)/shard_map/ppermute | solution.py:824
  200.0 2.6 %weave.2 = bf16[16,2,32,768]{3,2,1,0:T(8,128)(2,1)} custom-call(s32[1]{0:T(128)} %bitcast.core.refs_0_, bf16[16,32,768]{2,1,0:T(8,128)(2,1)} %all-to-all-done.2.mine_ref, bf16[16,32,768]{2,1,0:T(8,128)(2,1)} %copy-done.8), custom_call_target="tpu_custom_call" | custom-call | flops 1 | bytes 1 | tf_op jit(solution)/shard_map/weave/pallas_call | solution.py:972
  202.6 12.1 %collective-permute-done.28 = bf16[2,48,3456]{2,1,0:T(8,128)(2,1)} collective-permute-done((bf16[2,48,3456]{2,1,0:T(8,128)(2,1)}, bf16[2,48,3456]{2,1,0:T(8,128)(2,1)}, u32[]{:S(2)}, u32[]{:S(2)}) %collective-permute-start.28) | collective-permute-done | bytes 663584 | tf_op jit(solution)/shard_map/ppermute | solution.py:807
  216.0 3.3 %collective-permute-start.32 = (bf16[1,48,3456]{2,1,0:T(8,128)(2,1)S(1)}, bf16[1,48,3456]{2,1,0:T(8,128)(2,1)S(1)}, u32[]{:S(2)}, u32[]{:S(2)}) collective-permute-start(bf16[1,48,3456]{2,1,0:T(8,128)(2,1)S(1)} %dynamic-slice_convert_fusion), channel_id=1, source_target_pairs={{0,16},{2,18},{4,20},{6,22},{8,24},{10,26},{12,28},{14,30},{16,0},... | collective-permute-start | bytes 995336 | tf_op jit(solution)/shard_map/ppermute | solution.py:807
  223.5 3.4 %collective-permute-start.30 = (bf16[48,1152]{1,0:T(8,128)(2,1)S(1)}, bf16[48,1152]{1,0:T(8,128)(2,1)S(1)}, u32[]{:S(2)}, u32[]{:S(2)}) collective-permute-start(bf16[48,1152]{1,0:T(8,128)(2,1)S(1)} %get-tuple-element.182), channel_id=1, source_target_pairs={{0,16},{2,18},{4,20},{6,22},{8,24},{10,26},{12,28},{14,30},{16,0},... | collective-permute-start | bytes 331784 | tf_op jit(solution)/shard_map/ppermute | solution.py:819
  226.9 12.9 %collective-permute-done.32 = bf16[1,48,3456]{2,1,0:T(8,128)(2,1)S(1)} collective-permute-done((bf16[1,48,3456]{2,1,0:T(8,128)(2,1)S(1)}, bf16[1,48,3456]{2,1,0:T(8,128)(2,1)S(1)}, u32[]{:S(2)}, u32[]{:S(2)}) %collective-permute-start.32) | collective-permute-done | bytes 331808 | tf_op jit(solution)/shard_map/ppermute | solution.py:807
  239.9 2.3 collective-permute-done.30
  244.8 2.8 %weave.3 = (bf16[16,2,32,768]{3,2,1,0:T(8,128)(2,1)}, f32[1,24]{1,0:T(1,128)}, f32[1,24]{1,0:T(1,128)}, f32[1,24]{1,0:T(1,128)}, f32[1,24]{1,0:T(1,128)}, /*inde...) custom-call(s32[1]{0:T(128)} %bitcast.core.refs_0_, ...), custom_call_target="tpu_custom_call" | custom-call | flops 1 | bytes 1 | tf_op jit(solution)/shard_map/weave/pallas_call | solution.py:972
  (144 shorter events, 39.8 us)
Async XLA Ops:
  0.7 30.5 %collective-permute-start.2 = (bf16[768,1536]{1,0:T(8,128)(2,1)}, bf16[768,1536]{1,0:T(8,128)(2,1)}, u32[]{:S(2)}, u32[]{:S(2)}) collective-permute-start(bf16[768,1536]{1,0:T(8,128)(2,1)} %up_mine.1), channel_id=1, source_target_pairs={{0,1},{1,0},{2,3},{3,2},{4,5},{5,4},{6,7},{7,6},{8,9},{9,8},{10,11... | collective-permute-start | bytes 7077896 | tf_op jit(solution)/shard_map/ppermute | solution.py:28
  1.2 30.0 %collective-permute-start.3 = (bf16[1536,768]{1,0:T(8,128)(2,1)}, bf16[1536,768]{1,0:T(8,128)(2,1)}, u32[]{:S(2)}, u32[]{:S(2)}) collective-permute-start(bf16[1536,768]{1,0:T(8,128)(2,1)} %down_mine.1), channel_id=1, source_target_pairs={{0,1},{1,0},{2,3},{3,2},{4,5},{5,4},{6,7},{7,6},{8,9},{9,8},{10,11... | collective-permute-start | bytes 7077896 | tf_op jit(solution)/shard_map/ppermute | solution.py:28
  3.1 28.1 %all-to-all-start = ((bf16[16,32,768]{2,1,0:T(8,128)(2,1)}), bf16[16,32,768]{2,1,0:T(8,128)(2,1)S(1)}, u32[]{:S(2)}, u32[]{:S(2)}) async-start(bf16[16,32,768]{2,1,0:T(8,128)(2,1)} %constant_dynamic-slice_fusion.2), calls=%async_computation | async-start | bytes 1572864 | tf_op jit(solution)/shard_map/all_to_all | solution.py:937
  12.0 19.2 %collective-permute-start.4 = (bf16[768,384]{1,0:T(8,128)(2,1)S(1)}, bf16[768,384]{1,0:T(8,128)(2,1)S(1)}, u32[]{:S(2)}, u32[]{:S(2)}) collective-permute-start(bf16[768,384]{1,0:T(8,128)(2,1)S(1)} %copy-done.9), channel_id=1, source_target_pairs={{0,1},{1,0},{2,3},{3,2},{4,5},{5,4},{6,7},{7,6},{8,9},{9,8},{10,11... | collective-permute-start | bytes 1769480 | tf_op jit(solution)/shard_map/ppermute | solution.py:28
  13.5 17.7 %collective-permute-start.5 = (bf16[768,384]{1,0:T(8,128)(2,1)S(1)}, bf16[768,384]{1,0:T(8,128)(2,1)}, u32[]{:S(2)}, u32[]{:S(2)}) collective-permute-start(bf16[768,384]{1,0:T(8,128)(2,1)S(1)} %copy-done.10), channel_id=1, source_target_pairs={{0,1},{1,0},{2,3},{3,2},{4,5},{5,4},{6,7},{7,6},{8,9},{9,8},{10,11... | collective-permute-start | bytes 1769480 | tf_op jit(solution)/shard_map/ppermute | solution.py:28
  13.9 17.4 %collective-permute-start.6 = (bf16[768,384]{1,0:T(8,128)(2,1)S(1)}, bf16[768,384]{1,0:T(8,128)(2,1)}, u32[]{:S(2)}, u32[]{:S(2)}) collective-permute-start(bf16[768,384]{1,0:T(8,128)(2,1)S(1)} %copy-done.11), channel_id=1, source_target_pairs={{0,1},{1,0},{2,3},{3,2},{4,5},{5,4},{6,7},{7,6},{8,9},{9,8},{10,11... | collective-permute-start | bytes 1769480 | tf_op jit(solution)/shard_map/ppermute | solution.py:28
  31.2 5.7 %collective-permute-start.7 = (bf16[512,768]{1,0:T(8,128)(2,1)S(1)}, bf16[512,768]{1,0:T(8,128)(2,1)S(1)}, u32[]{:S(2)}, u32[]{:S(2)}) collective-permute-start(bf16[512,768]{1,0:T(8,128)(2,1)S(1)} %bitcast.60), channel_id=1, source_target_pairs={{0,1},{1,0},{2,3},{3,2},{4,5},{5,4},{6,7},{7,6},{8,9},{9,8},{10,11... | collective-permute-start | bytes 2359304 | tf_op jit(solution)/shard_map/ppermute | solution.py:28
  32.1 29.2 %all-to-all-start.1 = ((bf16[16,32,768]{2,1,0:T(8,128)(2,1)}), bf16[16,32,768]{2,1,0:T(8,128)(2,1)S(1)}, u32[]{:S(2)}, u32[]{:S(2)}) async-start(bf16[16,32,768]{2,1,0:T(8,128)(2,1)} %constant_dynamic-slice_fusion.1), calls=%async_computation.1 | async-start | bytes 1572864 | tf_op jit(solution)/shard_map/all_to_all | solution.py:937
  61.2 3.1 %collective-permute-start.9 = (bf16[512,768]{1,0:T(8,128)(2,1)S(1)}, bf16[512,768]{1,0:T(8,128)(2,1)S(1)}, u32[]{:S(2)}, u32[]{:S(2)}) collective-permute-start(bf16[512,768]{1,0:T(8,128)(2,1)S(1)} %bitcast.62), channel_id=1, source_target_pairs={{0,1},{1,0},{2,3},{3,2},{4,5},{5,4},{6,7},{7,6},{8,9},{9,8},{10,11... | collective-permute-start | bytes 2359304 | tf_op jit(solution)/shard_map/ppermute | solution.py:28
  94.3 11.6 %collective-permute-start.15 = (bf16[512,1536]{1,0:T(8,128)(2,1)}, bf16[512,1536]{1,0:T(8,128)(2,1)S(1)}, u32[]{:S(2)}, u32[]{:S(2)}) collective-permute-start(bf16[512,1536]{1,0:T(8,128)(2,1)} %get-tuple-element.133), channel_id=1, source_target_pairs={{0,1},{1,0},{2,3},{3,2},{4,5},{5,4},{6,7},{7,6},{8,9},{9,8},{10,11... | collective-permute-start | bytes 4718600 | tf_op jit(solution)/shard_map/ppermute | solution.py:28
  94.4 23.1 %collective-permute-start.12 = (bf16[512,1536]{1,0:T(8,128)(2,1)}, bf16[512,1536]{1,0:T(8,128)(2,1)S(1)}, u32[]{:S(2)}, u32[]{:S(2)}) collective-permute-start(bf16[512,1536]{1,0:T(8,128)(2,1)} %get-tuple-element.129), channel_id=1, source_target_pairs={{0,1},{1,0},{2,3},{3,2},{4,5},{5,4},{6,7},{7,6},{8,9},{9,8},{10,11... | collective-permute-start | bytes 4718600 | tf_op jit(solution)/shard_map/ppermute | solution.py:28
  94.8 10.9 %collective-permute-start.14 = (bf16[512,768]{1,0:T(8,128)(2,1)}, bf16[512,768]{1,0:T(8,128)(2,1)}, u32[]{:S(2)}, u32[]{:S(2)}) collective-permute-start(bf16[512,768]{1,0:T(8,128)(2,1)} %get-tuple-element.131.refs_0_), channel_id=1, source_target_pairs={{0,1},{1,0},{2,3},{3,2},{4,5},{5,4},{6,7},{7,6},{8,9},{9,8},{10,11... | collective-permute-start | bytes 2359304 | tf_op jit(solution)/shard_map/ppermute | solution.py:28
  94.9 11.0 %collective-permute-start.16 = (bf16[512,768]{1,0:T(8,128)(2,1)}, bf16[512,768]{1,0:T(8,128)(2,1)}, u32[]{:S(2)}, u32[]{:S(2)}) collective-permute-start(bf16[512,768]{1,0:T(8,128)(2,1)} %get-tuple-element.134.refs_4_), channel_id=1, source_target_pairs={{0,1},{1,0},{2,3},{3,2},{4,5},{5,4},{6,7},{7,6},{8,9},{9,8},{10,11... | collective-permute-start | bytes 2359304 | tf_op jit(solution)/shard_map/ppermute | solution.py:28
  95.3 22.3 %collective-permute-start.11 = (bf16[512,768]{1,0:T(8,128)(2,1)}, bf16[512,768]{1,0:T(8,128)(2,1)}, u32[]{:S(2)}, u32[]{:S(2)}) collective-permute-start(bf16[512,768]{1,0:T(8,128)(2,1)} %get-tuple-element.127.refs_0_), channel_id=1, source_target_pairs={{0,1},{1,0},{2,3},{3,2},{4,5},{5,4},{6,7},{7,6},{8,9},{9,8},{10,11... | collective-permute-start | bytes 2359304 | tf_op jit(solution)/shard_map/ppermute | solution.py:28
  98.8 56.5 %all-to-all-start.2 = ((bf16[16,32,768]{2,1,0:T(8,128)(2,1)}), bf16[16,32,768]{2,1,0:T(8,128)(2,1)}, u32[]{:S(2)}, u32[]{:S(2)}) async-start(bf16[16,32,768]{2,1,0:T(8,128)(2,1)} %route.2), calls=%async_computation.2 | async-start | bytes 1572864 | tf_op jit(solution)/shard_map/all_to_all | solution.py:937
  105.8 20.8 %collective-permute-start.18 = (bf16[512,384]{1,0:T(8,128)(2,1)S(1)}, bf16[512,384]{1,0:T(8,128)(2,1)S(1)}, u32[]{:S(2)}, u32[]{:S(2)}) collective-permute-start(bf16[512,384]{1,0:T(8,128)(2,1)S(1)} %copy-done.28), channel_id=1, source_target_pairs={{0,1},{1,0},{2,3},{3,2},{4,5},{5,4},{6,7},{7,6},{8,9},{9,8},{10,11... | collective-permute-start | bytes 1179656 | tf_op jit(solution)/shard_map/ppermute | solution.py:28
  115.7 39.5 %collective-permute-start.17 = (bf16[2,4,48,1920]{3,2,1,0:T(8,128)(2,1)}, bf16[2,4,48,1920]{3,2,1,0:T(8,128)(2,1)}, u32[]{:S(2)}, u32[]{:S(2)}) collective-permute-start(bf16[2,4,48,1920]{3,2,1,0:T(8,128)(2,1)} %get-tuple-element.135), channel_id=1, source_target_pairs={{0,4},{2,6},{4,0},{6,2},{8,12},{10,14},{12,8},{14,10},{16,20},{18,... | collective-permute-start | bytes 4423688 | tf_op jit(solution)/shard_map/ppermute | solution.py:1083
  125.1 30.1 %collective-permute-start.13 = (bf16[2,4,48,1536]{3,2,1,0:T(8,128)(2,1)}, bf16[2,4,48,1536]{3,2,1,0:T(8,128)(2,1)S(1)}, u32[]{:S(2)}, u32[]{:S(2)}) collective-permute-start(bf16[2,4,48,1536]{3,2,1,0:T(8,128)(2,1)} %get-tuple-element.130), channel_id=1, source_target_pairs={{0,2},{2,0},{4,6},{6,4},{8,10},{10,8},{12,14},{14,12},{16,18},{18,... | collective-permute-start | bytes 3538952 | tf_op jit(solution)/shard_map/ppermute | solution.py:1083
  149.0 14.1 %collective-permute-start.19 = (bf16[512,1152]{1,0:T(8,128)(2,1)}, bf16[512,1152]{1,0:T(8,128)(2,1)}, u32[]{:S(2)}, u32[]{:S(2)}) collective-permute-start(bf16[512,1152]{1,0:T(8,128)(2,1)} %get-tuple-element.144.refs_3_), channel_id=1, source_target_pairs={{0,1},{1,0},{2,3},{3,2},{4,5},{5,4},{6,7},{7,6},{8,9},{9,8},{10,11... | collective-permute-start | bytes 3538952 | tf_op jit(solution)/shard_map/ppermute | solution.py:28
  170.2 20.2 %collective-permute-start.27 = (bf16[4,48,1920]{2,1,0:T(8,128)(2,1)}, bf16[4,48,1920]{2,1,0:T(8,128)(2,1)}, u32[]{:S(2)}, u32[]{:S(2)}) collective-permute-start(bf16[4,48,1920]{2,1,0:T(8,128)(2,1)} %fusion), channel_id=1, source_target_pairs={{0,2},{2,0},{4,6},{6,4},{8,10},{10,8},{12,14},{14,12},{16,18},{18,... | collective-permute-start | bytes 2211848 | tf_op jit(solution)/shard_map/ppermute | solution.py:1096
  170.2 20.2 %collective-permute-start.26 = (bf16[4,48,1536]{2,1,0:T(8,128)(2,1)S(1)}, bf16[4,48,1536]{2,1,0:T(8,128)(2,1)}, u32[]{:S(2)}, u32[]{:S(2)}) collective-permute-start(bf16[4,48,1536]{2,1,0:T(8,128)(2,1)S(1)} %fusion.2), channel_id=1, source_target_pairs={{0,4},{2,6},{4,0},{6,2},{8,12},{10,14},{12,8},{14,10},{16,20},{18,... | collective-permute-start | bytes 1769480 | tf_op jit(solution)/shard_map/ppermute | solution.py:1096
  175.8 38.9 %all-to-all-start.3 = ((bf16[16,40,768]{2,1,0:T(8,128)(2,1)}), bf16[16,40,768]{2,1,0:T(8,128)(2,1)}, u32[]{:S(2)}, u32[]{:S(2)}) async-start(bf16[16,40,768]{2,1,0:T(8,128)(2,1)} %route.3), calls=%async_computation.3 | async-start | bytes 1966080 | tf_op jit(solution)/shard_map/all_to_all | solution.py:937
  193.3 5.8 %collective-permute-start.21 = (bf16[16,32,768]{2,1,0:T(8,128)(2,1)}, bf16[16,32,768]{2,1,0:T(8,128)(2,1)S(1)}, u32[]{:S(2)}, u32[]{:S(2)}) collective-permute-start(bf16[16,32,768]{2,1,0:T(8,128)(2,1)} %all-to-all-done.2.mine_ref), channel_id=1, source_target_pairs={{0,1},{1,0},{2,3},{3,2},{4,5},{5,4},{6,7},{7,6},{8,9},{9,8},{10,11... | collective-permute-start | bytes 2359304 | tf_op jit(solution)/shard_map/ppermute | solution.py:28
  194.5 20.3 %collective-permute-start.28 = (bf16[2,48,3456]{2,1,0:T(8,128)(2,1)}, bf16[2,48,3456]{2,1,0:T(8,128)(2,1)}, u32[]{:S(2)}, u32[]{:S(2)}) collective-permute-start(bf16[2,48,3456]{2,1,0:T(8,128)(2,1)} %fusion.1), channel_id=1, source_target_pairs={{0,8},{2,10},{4,12},{6,14},{8,0},{10,2},{12,4},{14,6},{16,24},{18,... | collective-permute-start | bytes 1990664 | tf_op jit(solution)/shard_map/ppermute | solution.py:807
  195.6 23.8 %collective-permute-start.23 = (bf16[4,48,1152]{2,1,0:T(8,128)(2,1)}, bf16[4,48,1152]{2,1,0:T(8,128)(2,1)}, u32[]{:S(2)}, u32[]{:S(2)}) collective-permute-start(bf16[4,48,1152]{2,1,0:T(8,128)(2,1)} %get-tuple-element.146), channel_id=1, source_target_pairs={{0,2},{2,0},{4,6},{6,4},{8,10},{10,8},{12,14},{14,12},{16,18},{18,... | collective-permute-start | bytes 1327112 | tf_op jit(solution)/shard_map/ppermute | solution.py:824
  196.0 23.3 %collective-permute-start.24 = (bf16[4,48,1152]{2,1,0:T(8,128)(2,1)}, bf16[4,48,1152]{2,1,0:T(8,128)(2,1)}, u32[]{:S(2)}, u32[]{:S(2)}) collective-permute-start(bf16[4,48,1152]{2,1,0:T(8,128)(2,1)} %get-tuple-element.147), channel_id=1, source_target_pairs={{0,4},{2,6},{4,0},{6,2},{8,12},{10,14},{12,8},{14,10},{16,20},{18,... | collective-permute-start | bytes 1327112 | tf_op jit(solution)/shard_map/ppermute | solution.py:824
  196.5 24.0 %collective-permute-start.25 = (bf16[4,48,1152]{2,1,0:T(8,128)(2,1)}, bf16[4,48,1152]{2,1,0:T(8,128)(2,1)}, u32[]{:S(2)}, u32[]{:S(2)}) collective-permute-start(bf16[4,48,1152]{2,1,0:T(8,128)(2,1)} %get-tuple-element.148), channel_id=1, source_target_pairs={{0,6},{2,4},{4,2},{6,0},{8,14},{10,12},{12,10},{14,8},{16,22},{18,... | collective-permute-start | bytes 1327112 | tf_op jit(solution)/shard_map/ppermute | solution.py:824
  216.0 23.8 %collective-permute-start.32 = (bf16[1,48,3456]{2,1,0:T(8,128)(2,1)S(1)}, bf16[1,48,3456]{2,1,0:T(8,128)(2,1)S(1)}, u32[]{:S(2)}, u32[]{:S(2)}) collective-permute-start(bf16[1,48,3456]{2,1,0:T(8,128)(2,1)S(1)} %dynamic-slice_convert_fusion), channel_id=1, source_target_pairs={{0,16},{2,18},{4,20},{6,22},{8,24},{10,26},{12,28},{14,30},{16,0},... | collective-permute-start | bytes 995336 | tf_op jit(solution)/shard_map/ppermute | solution.py:807
  222.1 17.8 %collective-permute-start.29 = (bf16[48,1152]{1,0:T(8,128)(2,1)S(1)}, bf16[48,1152]{1,0:T(8,128)(2,1)S(1)}, u32[]{:S(2)}, u32[]{:S(2)}) collective-permute-start(bf16[48,1152]{1,0:T(8,128)(2,1)S(1)} %get-tuple-element.183), channel_id=1, source_target_pairs={{0,8},{2,10},{4,12},{6,14},{8,0},{10,2},{12,4},{14,6},{16,24},{18,... | collective-permute-start | bytes 331784 | tf_op jit(solution)/shard_map/ppermute | solution.py:819
  223.5 18.7 %collective-permute-start.30 = (bf16[48,1152]{1,0:T(8,128)(2,1)S(1)}, bf16[48,1152]{1,0:T(8,128)(2,1)S(1)}, u32[]{:S(2)}, u32[]{:S(2)}) collective-permute-start(bf16[48,1152]{1,0:T(8,128)(2,1)S(1)} %get-tuple-element.182), channel_id=1, source_target_pairs={{0,16},{2,18},{4,20},{6,22},{8,24},{10,26},{12,28},{14,30},{16,0},... | collective-permute-start | bytes 331784 | tf_op jit(solution)/shard_map/ppermute | solution.py:819
  226.9 15.3 %collective-permute-start.31 = (bf16[48,1152]{1,0:T(8,128)(2,1)S(1)}, bf16[48,1152]{1,0:T(8,128)(2,1)S(1)}, u32[]{:S(2)}, u32[]{:S(2)}) collective-permute-start(bf16[48,1152]{1,0:T(8,128)(2,1)S(1)} %get-tuple-element.181), channel_id=1, source_target_pairs={{0,24},{2,26},{4,28},{6,30},{8,16},{10,18},{12,20},{14,22},{16,8},... | collective-permute-start | bytes 331784 | tf_op jit(solution)/shard_map/ppermute | solution.py:819
  226.9 16.9 %collective-permute-start.22 = (bf16[16,40,768]{2,1,0:T(8,128)(2,1)}, bf16[16,40,768]{2,1,0:T(8,128)(2,1)S(1)}, u32[]{:S(2)}, u32[]{:S(2)}) collective-permute-start(bf16[16,40,768]{2,1,0:T(8,128)(2,1)} %all-to-all-done.3.mine_ref), channel_id=1, source_target_pairs={{0,1},{1,0},{2,3},{3,2},{4,5},{5,4},{6,7},{7,6},{8,9},{9,8},{10,11... | collective-permute-start | bytes 2949128 | tf_op jit(solution)/shard_map/ppermute | solution.py:28
  (36 other events, 219.1 us)

commit v2 on v1

--- a/solution.py
+++ b/solution.py
@@ -1088,10 +1088,9 @@
     other_grad = swap(qkv_theirs)
     qkv_terms = gradients([((inputs, 0), (inputs, 1), qkv_mine, qkv_theirs)], groups)
     got, returned = after((got, returned), qkv_terms)
-    both = [k.astype(F32) + g.astype(F32) for k, g in zip(kept, got)]
-    sent = [b[1].astype(BF16) for b in both]
-    kept = [b[0] for b in both] if got else [k[0] for k in kept]
-    first_grad = after(first_grad, (qkv_terms, sent, kept))
+    sent = [(k[1].astype(F32) + g[1].astype(F32)).astype(BF16) for k, g in zip(kept, got)]
+    first_grad = after(first_grad, (qkv_terms, sent))
+    kept, first_got = [k[0].astype(F32) for k in kept], got
     qkv_got = near_sends(qkv_terms[1:], groups)
     got = [lax.ppermute(v, "dp", pairs(groups, 2 - n)) for n, v in enumerate(sent)]
     input_low = input_rows(
@@ -1100,7 +1099,7 @@
     given = route(core, token_slot, input_low, swap(input_low), groups, (sums, up_sums, qv_sums))
     got = after(got, given)
     if got:
-        kept = [k + g.astype(F32) for k, g in zip(kept, got)]
+        kept = [k + f[0].astype(F32) + g.astype(F32) for k, f, g in zip(kept, first_got, got)]
     ffn_terms = far_halves(jnp.concatenate(kept, axis=2), groups, 0)
     payload, given = given, exchange(given)
     layer_out = weave(core, after(returned, payload), half_run)

time: 249 us -> 244 us (0.980)
  Pallas kernels: 110 us -> 101 us
  local copies, waits for them, and re-layouts: 24.7 us -> 18.1 us
  waiting for transfers between devices: 55 us -> 61.2 us
  starting transfers between devices: 46.6 us -> 51.5 us
    all_to_all x4, starting transfers between devices: 25.5 us -> 31.3 us  [exchange(): return lax.all_to_all(values, 'dp', split_axis=0, concat_axis=0, tiled=True)]
    pallas_call x1, Pallas kernels: 14.6 us -> 9.65 us  [attention_forward(): pl.pallas_call(forward_kernel, grid_spec=pltpu.PrefetchScalarGridSpec(num...]
    pallas_call x1, Pallas kernels: 21.6 us -> 17.1 us  [attention_backward(): pl.pallas_call(backward_kernel, grid_spec=pltpu.PrefetchScalarGridSpec(nu...]
    unnamed x62 -> x58, local copies, waits for them, and re-layouts: 10.9 us -> 6.53 us
    convert_element_type x0 -> x2, other arithmetic: none -> 4.27 us  [local(): (k[1].astype(F32) + g[1].astype(F32)).astype(BF16)]
    add x4 -> x2, other arithmetic: 6.79 us -> 3.03 us  [local(): k + f[0].astype(F32) + g.astype(F32)]
    ppermute x2, starting transfers between devices: 4.38 us -> 1.17 us  [far_step(): got = after(lax.ppermute(sent, 'dp', pairs(groups, near << bit)), first)]
    ppermute x2, waiting for transfers between devices: 0.01 us -> 2.72 us  [local(): lax.ppermute(v, 'dp', pairs(groups, n + 1))]
  transfers between devices with their start and end apart: 37 -> 37, of which waited for: 11 -> 13; matrix products, arithmetic and copies ran while one was open for 10% -> 9% of each run, Pallas kernels for 30% -> 27%
where the time goes in v2:
time: 244 us; the launch traced here: 243 us
  Pallas kernels  101 us (41%)
  waiting for transfers between devices  61.2 us (25%)
  starting transfers between devices  51.5 us (21%)
  local copies, waits for them, and re-layouts  18.1 us (7%)
  other arithmetic  10.3 us (4%)
    all_to_all x4, starting transfers between devices, exchange(): return lax.all_to_all(values, 'dp', split_axis=0, concat_axis=0, tiled=True)  31.3 us
    ppermute x2, waiting for transfers between devices, far_step(): got = after(lax.ppermute(sent, 'dp', pairs(groups, near << bit)), first)  27.5 us
    pallas_call x1, Pallas kernels, row_pass(): pl.pallas_call(functools.partial(rows_kernel, run_rows), grid_spec=pltpu....  25.4 us
    pallas_call x3, Pallas kernels, gradients(): pl.pallas_call(functools.partial(gradient_kernel, chunks, near, share, ha...  21.4 us
    pallas_call x1, Pallas kernels, attention_backward(): pl.pallas_call(backward_kernel, grid_spec=pltpu.PrefetchScalarGridSpec(nu...  17.1 us
    ppermute x2, waiting for transfers between devices, local(): lax.ppermute(v, 'dp', pairs(groups, 2 - n))  10.8 us
    pallas_call x1, Pallas kernels, attention_forward(): pl.pallas_call(forward_kernel, grid_spec=pltpu.PrefetchScalarGridSpec(num...  9.65 us
    all_to_all x4, waiting for transfers between devices, exchange(): return lax.all_to_all(values, 'dp', split_axis=0, concat_axis=0, tiled=True)  9.5 us
  transfers between devices with their start and end apart: 37, of which 13 were waited for; matrix products, arithmetic and copies ran while one was open for 9% of the time, Pallas kernels for 27%

profile of v2, /device:TPU:0, one launch (start us, length us, event | category | flops | bytes accessed | tf_op | source)
XLA Modules:
  0.0 243.2 jit_solution(12001295279761302460)
XLA Ops:
  3.1 8.3 %all-to-all-start = ((bf16[16,32,768]{2,1,0:T(8,128)(2,1)}), bf16[16,32,768]{2,1,0:T(8,128)(2,1)S(1)}, u32[]{:S(2)}, u32[]{:S(2)}) async-start(bf16[16,32,768]{2,1,0:T(8,128)(2,1)} %constant_dynamic-slice_fusion.2), calls=%async_computation | async-start | bytes 1572864 | tf_op jit(solution)/shard_map/all_to_all | solution.py:937
  19.3 2.1 constant_dynamic-slice_fusion.1
  22.0 9.2 %all-to-all-done = bf16[16,32,768]{2,1,0:T(8,128)(2,1)S(1)} async-done(((bf16[16,32,768]{2,1,0:T(8,128)(2,1)}), bf16[16,32,768]{2,1,0:T(8,128)(2,1)S(1)}, u32[]{:S(2)}, u32[]{:S(2)}) %all-to-all-start) | async-done | bytes 786464 | tf_op jit(solution)/shard_map/all_to_all | solution.py:937
  32.0 4.9 %all-to-all-start.1 = ((bf16[16,32,768]{2,1,0:T(8,128)(2,1)}), bf16[16,32,768]{2,1,0:T(8,128)(2,1)S(1)}, u32[]{:S(2)}, u32[]{:S(2)}) async-start(bf16[16,32,768]{2,1,0:T(8,128)(2,1)} %constant_dynamic-slice_fusion.1), calls=%async_computation.1 | async-start | bytes 1572864 | tf_op jit(solution)/shard_map/all_to_all | solution.py:937
  37.9 8.8 %intake.1 = (bf16[1024,768]{1,0:T(8,128)(2,1)}, bf16[1024,384]{1,0:T(8,128)(2,1)}, bf16[1024,384]{1,0:T(8,128)(2,1)}, bf16[1024,384]{1,0:T(8,128)(2,1)}) custom-call(s32[1]{0:T(128)} %bitcast.core.refs_0_, s32[1,1024]{1,0:T(1,128)} %refs_2_.5, bf16[512,768]{1,0:T(8,128)(2,1)} %bitcast.57, bf16[512,768]{1,0:T(8,128)(2,1)} %copy-done.26, ...), custom_call_target="tpu_custom_call" | custom-call | flops 3422552064 | bytes 6291456 | tf_op jit(solution)/shard_map/intake/pallas_call | solution.py:394
  46.7 9.7 %attend.1 = (bf16[512,384]{1,0:T(8,128)(2,1)}, bf16[512,384]{1,0:T(8,128)(2,1)}, f32[8,1024]{1,0:T(8,128)}) custom-call(s32[1,4]{1,0:T(1,128)} %lengths.3, s32[1]{0:T(128)} %bitcast.core.refs_0_, bf16[1024,384]{1,0:T(8,128)(2,1)} %get-tuple-element.104.q_ref, bf16[1024,384]{1,0:T(8,128)(2,1)} %get-tuple-element.105.k_ref, ...), custom_call_target="tpu_custom_call" | custom-call | flops 6442450944 | bytes 3145728 | tf_op jit(solution)/shard_map/attend/pallas_call | solution.py:169
  57.2 2.2 collective-permute-done.8.mixed_other
  60.4 25.4 %row_pass.1 = (bf16[512,768]{1,0:T(8,128)(2,1)}, bf16[512,768]{1,0:T(8,128)(2,1)}, bf16[512,768]{1,0:T(8,128)(2,1)}, bf16[512,1536]{1,0:T(8,128)(2,1)}, bf16[512...) custom-call(s32[1]{0:T(128)} %bitcast.core.refs_0_, ...), custom_call_target="tpu_custom_call" | custom-call | flops 12683575296 | bytes 30670848 | tf_op jit(solution)/shard_map/row_pass/pallas_call | solution.py:629
  86.2 2.2 collective-permute-done.10.refs_4_
  89.8 3.3 %route.2 = bf16[16,32,768]{2,1,0:T(8,128)(2,1)} custom-call(s32[1]{0:T(128)} %bitcast.core.refs_0_, s32[1,1024]{1,0:T(1,128)} %refs_2_.5, s32[1,1024]{1,0:T(1,128)} %refs_2_.5, bf16[512,768]{1,0:T(8,128)(2,1)} %get-tuple-element.126.refs_3_, bf16[512,768]{1,0:T(8,128)(2,1)} %copy-done.24), custom_call_target="tpu_custom_call" | custom-call | flops 805306368 | bytes 2359296 | tf_op jit(solution)/shard_map/route/pallas_call | solution.py:920
  93.1 11.7 %all-to-all-start.2 = ((bf16[16,32,768]{2,1,0:T(8,128)(2,1)}), bf16[16,32,768]{2,1,0:T(8,128)(2,1)S(1)}, u32[]{:S(2)}, u32[]{:S(2)}) async-start(bf16[16,32,768]{2,1,0:T(8,128)(2,1)} %route.2), calls=%async_computation.2 | async-start | bytes 1572864 | tf_op jit(solution)/shard_map/all_to_all | solution.py:937
  105.0 8.7 %gradients.4 = (bf16[2,4,48,1920]{3,2,1,0:T(8,128)(2,1)}, bf16[2,4,48,1920]{3,2,1,0:T(8,128)(2,1)}) custom-call(s32[1]{0:T(128)} %bitcast.1.me, bf16[512,768]{1,0:T(8,128)(2,1)} %get-tuple-element.131.refs_0_, bf16[512,768]{1,0:T(8,128)(2,1)} %collective-permute-done.14.refs_1_, bf16[512,1536]{1,0:T(8,128)(2,1)} %get-tuple-element.132.refs_2_, ...), custom_call_target="tpu_custom_call" | custom-call | flops 3019898880 | bytes 9043968 | tf_op jit(solution)/shard_map/gradients/pallas_call | solution.py:777
  113.6 1.9 collective-permute-start.17
  116.9 6.4 %gradients.3 = (bf16[2,4,48,1536]{3,2,1,0:T(8,128)(2,1)}, bf16[2,4,48,1536]{3,2,1,0:T(8,128)(2,1)}) custom-call(s32[1]{0:T(128)} %bitcast.1.me, bf16[512,768]{1,0:T(8,128)(2,1)} %get-tuple-element.127.refs_0_, bf16[512,768]{1,0:T(8,128)(2,1)} %copy-done.23, bf16[512,1536]{1,0:T(8,128)(2,1)} %get-tuple-element.128.refs_2_, bf16[512,1536]{1,0:T(8,128)(2,1)} %copy-done.22), custom_call_target="tpu_custom_call" | custom-call | flops 2415919104 | bytes 7864320 | tf_op jit(solution)/shard_map/gradients/pallas_call | solution.py:777
  125.5 17.1 %attend_back.1 = (bf16[512,1152]{1,0:T(8,128)(2,1)}, bf16[512,1152]{1,0:T(8,128)(2,1)}, f32[8,384]{1,0:T(8,128)}) custom-call(s32[1,4]{1,0:T(1,128)} %lengths.3, s32[1]{0:T(128)} %bitcast.core.refs_0_, bf16[1024,384]{1,0:T(8,128)(2,1)} %get-tuple-element.104.q_ref, bf16[512,384]{1,0:T(8,128)(2,1)} %get-tuple-element.140.do_mine, ...), custom_call_target="tpu_custom_call" | custom-call | flops 16106127360 | bytes 6291456 | tf_op jit(solution)/shard_map/attend_back/pallas_call | solution.py:312
  142.7 6.3 %gradients.5 = (bf16[4,48,1152]{2,1,0:T(8,128)(2,1)}, bf16[4,48,1152]{2,1,0:T(8,128)(2,1)}, bf16[4,48,1152]{2,1,0:T(8,128)(2,1)}, bf16[4,48,1152]{2,1,0:T(8,128)(2,1)}) custom-call(s32[1]{0:T(128)} %bitcast.1.me, bf16[1024,768]{1,0:T(8,128)(2,1)} %get-tuple-element.103.x_ref.refs_0_.refs_1_, bf16[1024,768]{1,0:T(8,128)(2,1)} %get-tuple-element.103.x_ref.refs_0_.refs_1_, ...), custom_call_target="tpu_custom_call" | custom-call | flops 1811939328 | bytes 6684672 | tf_op jit(solution)/shard_map/gradients/pallas_call | solution.py:777
  149.0 2.7 %collective-permute-done.13 = bf16[2,4,48,1536]{3,2,1,0:T(8,128)(2,1)} collective-permute-done((bf16[2,4,48,1536]{3,2,1,0:T(8,128)(2,1)}, bf16[2,4,48,1536]{3,2,1,0:T(8,128)(2,1)}, u32[]{:S(2)}, u32[]{:S(2)}) %collective-permute-start.13) | collective-permute-done | bytes 1179680 | tf_op jit(solution)/shard_map/ppermute | solution.py:1083
  151.7 2.2 fusion
  153.9 2.0 fusion.2
  156.0 6.6 %input_rows.1.refs_3_ = bf16[512,768]{1,0:T(8,128)(2,1)} custom-call(f32[512,768]{1,0:T(8,128)} %get-tuple-element.153.first_ref, bf16[512,1152]{1,0:T(8,128)(2,1)} %get-tuple-element.143.refs_2_.mine_ref, bf16[512,1152]{1,0:T(8,128)(2,1)} %collective-permute-done.19.other_ref, bf16[768,384]{1,0:T(8,128)(2,1)} %refs_0_.1, bf16[768,384]{1,0:T(8,128)(2,1)} %refs_1_.4, ...), custom_call_target="tpu_custom_call" | custom-call | flops 1811939328 | bytes 6684672 | tf_op jit(solution)/shard_map/input_rows/pallas_call | solution.py:852
  162.6 3.2 %collective-permute-start.27 = (bf16[4,48,1920]{2,1,0:T(8,128)(2,1)}, bf16[4,48,1920]{2,1,0:T(8,128)(2,1)}, u32[]{:S(2)}, u32[]{:S(2)}) collective-permute-start(bf16[4,48,1920]{2,1,0:T(8,128)(2,1)} %fusion), channel_id=1, source_target_pairs={{0,2},{2,0},{4,6},{6,4},{8,10},{10,8},{12,14},{14,12},{16,18},{18,... | collective-permute-start | bytes 2211848 | tf_op jit(solution)/shard_map/ppermute | solution.py:1095
  165.8 3.4 %route.3 = bf16[16,40,768]{2,1,0:T(8,128)(2,1)} custom-call(s32[1]{0:T(128)} %bitcast.core.refs_0_, s32[1,1024]{1,0:T(1,128)} %refs_2_.5, s32[1,1024]{1,0:T(1,128)} %refs_2_.5, bf16[512,768]{1,0:T(8,128)(2,1)} %input_rows.1.refs_3_, bf16[512,768]{1,0:T(8,128)(2,1)} %collective-permute-done.20.refs_4_, f32[8,768]{1,0:T(8,128)} %get-tuple-element.157.refs_5_, ...), custom_call_target="tpu_custom_call" | custom-call | flops 805306368 | bytes 2359296 | tf_op jit(solution)/shard_map/route/pallas_call | solution.py:920
  169.2 6.4 %all-to-all-start.3 = ((bf16[16,40,768]{2,1,0:T(8,128)(2,1)}), bf16[16,40,768]{2,1,0:T(8,128)(2,1)}, u32[]{:S(2)}, u32[]{:S(2)}) async-start(bf16[16,40,768]{2,1,0:T(8,128)(2,1)} %route.3), calls=%async_computation.3 | async-start | bytes 1966080 | tf_op jit(solution)/shard_map/all_to_all | solution.py:937
  175.6 10.8 %collective-permute-done.26 = bf16[4,48,1536]{2,1,0:T(8,128)(2,1)} collective-permute-done((bf16[4,48,1536]{2,1,0:T(8,128)(2,1)}, bf16[4,48,1536]{2,1,0:T(8,128)(2,1)}, u32[]{:S(2)}, u32[]{:S(2)}) %collective-permute-start.26) | collective-permute-done | bytes 589856 | tf_op jit(solution)/shard_map/ppermute | solution.py:1095
  191.7 2.3 collective-permute-start.25
  194.1 2.6 %weave.2 = bf16[16,2,32,768]{3,2,1,0:T(8,128)(2,1)} custom-call(s32[1]{0:T(128)} %bitcast.core.refs_0_, bf16[16,32,768]{2,1,0:T(8,128)(2,1)} %copy-done.2, bf16[16,32,768]{2,1,0:T(8,128)(2,1)} %collective-permute-done.21.other_ref), custom_call_target="tpu_custom_call" | custom-call | flops 1 | bytes 1 | tf_op jit(solution)/shard_map/weave/pallas_call | solution.py:972
  196.7 14.1 %collective-permute-done.28 = bf16[2,48,3456]{2,1,0:T(8,128)(2,1)} collective-permute-done((bf16[2,48,3456]{2,1,0:T(8,128)(2,1)}, bf16[2,48,3456]{2,1,0:T(8,128)(2,1)}, u32[]{:S(2)}, u32[]{:S(2)}) %collective-permute-start.28) | collective-permute-done | bytes 663584 | tf_op jit(solution)/shard_map/ppermute | solution.py:807
  213.3 2.3 collective-permute-done.24
  218.2 3.6 %collective-permute-start.30 = (bf16[48,1152]{1,0:T(8,128)(2,1)S(1)}, bf16[48,1152]{1,0:T(8,128)(2,1)S(1)}, u32[]{:S(2)}, u32[]{:S(2)}) collective-permute-start(bf16[48,1152]{1,0:T(8,128)(2,1)S(1)} %get-tuple-element.182), channel_id=1, source_target_pairs={{0,16},{2,18},{4,20},{6,22},{8,24},{10,26},{12,28},{14,30},{16,0},... | collective-permute-start | bytes 331784 | tf_op jit(solution)/shard_map/ppermute | solution.py:819
  221.8 13.4 %collective-permute-done.32 = bf16[1,48,3456]{2,1,0:T(8,128)(2,1)S(1)} collective-permute-done((bf16[1,48,3456]{2,1,0:T(8,128)(2,1)S(1)}, bf16[1,48,3456]{2,1,0:T(8,128)(2,1)S(1)}, u32[]{:S(2)}, u32[]{:S(2)}) %collective-permute-start.32) | collective-permute-done | bytes 331808 | tf_op jit(solution)/shard_map/ppermute | solution.py:807
  235.3 2.3 collective-permute-done.30
  240.3 2.8 %weave.3 = (bf16[16,2,32,768]{3,2,1,0:T(8,128)(2,1)}, f32[1,24]{1,0:T(1,128)}, f32[1,24]{1,0:T(1,128)}, f32[1,24]{1,0:T(1,128)}, f32[1,24]{1,0:T(1,128)}, /*inde...) custom-call(s32[1]{0:T(128)} %bitcast.core.refs_0_, ...), custom_call_target="tpu_custom_call" | custom-call | flops 1 | bytes 1 | tf_op jit(solution)/shard_map/weave/pallas_call | solution.py:972
  (138 shorter events, 33.3 us)
Async XLA Ops:
  0.7 30.5 %collective-permute-start.2 = (bf16[768,1536]{1,0:T(8,128)(2,1)}, bf16[768,1536]{1,0:T(8,128)(2,1)}, u32[]{:S(2)}, u32[]{:S(2)}) collective-permute-start(bf16[768,1536]{1,0:T(8,128)(2,1)} %up_mine.1), channel_id=1, source_target_pairs={{0,1},{1,0},{2,3},{3,2},{4,5},{5,4},{6,7},{7,6},{8,9},{9,8},{10,11... | collective-permute-start | bytes 7077896 | tf_op jit(solution)/shard_map/ppermute | solution.py:28
  1.2 30.0 %collective-permute-start.3 = (bf16[1536,768]{1,0:T(8,128)(2,1)}, bf16[1536,768]{1,0:T(8,128)(2,1)}, u32[]{:S(2)}, u32[]{:S(2)}) collective-permute-start(bf16[1536,768]{1,0:T(8,128)(2,1)} %down_mine.1), channel_id=1, source_target_pairs={{0,1},{1,0},{2,3},{3,2},{4,5},{5,4},{6,7},{7,6},{8,9},{9,8},{10,11... | collective-permute-start | bytes 7077896 | tf_op jit(solution)/shard_map/ppermute | solution.py:28
  3.1 28.1 %all-to-all-start = ((bf16[16,32,768]{2,1,0:T(8,128)(2,1)}), bf16[16,32,768]{2,1,0:T(8,128)(2,1)S(1)}, u32[]{:S(2)}, u32[]{:S(2)}) async-start(bf16[16,32,768]{2,1,0:T(8,128)(2,1)} %constant_dynamic-slice_fusion.2), calls=%async_computation | async-start | bytes 1572864 | tf_op jit(solution)/shard_map/all_to_all | solution.py:937
  12.0 19.2 %collective-permute-start.4 = (bf16[768,384]{1,0:T(8,128)(2,1)S(1)}, bf16[768,384]{1,0:T(8,128)(2,1)S(1)}, u32[]{:S(2)}, u32[]{:S(2)}) collective-permute-start(bf16[768,384]{1,0:T(8,128)(2,1)S(1)} %copy-done.8), channel_id=1, source_target_pairs={{0,1},{1,0},{2,3},{3,2},{4,5},{5,4},{6,7},{7,6},{8,9},{9,8},{10,11... | collective-permute-start | bytes 1769480 | tf_op jit(solution)/shard_map/ppermute | solution.py:28
  13.5 17.7 %collective-permute-start.5 = (bf16[768,384]{1,0:T(8,128)(2,1)S(1)}, bf16[768,384]{1,0:T(8,128)(2,1)}, u32[]{:S(2)}, u32[]{:S(2)}) collective-permute-start(bf16[768,384]{1,0:T(8,128)(2,1)S(1)} %copy-done.9), channel_id=1, source_target_pairs={{0,1},{1,0},{2,3},{3,2},{4,5},{5,4},{6,7},{7,6},{8,9},{9,8},{10,11... | collective-permute-start | bytes 1769480 | tf_op jit(solution)/shard_map/ppermute | solution.py:28
  13.9 17.4 %collective-permute-start.6 = (bf16[768,384]{1,0:T(8,128)(2,1)S(1)}, bf16[768,384]{1,0:T(8,128)(2,1)}, u32[]{:S(2)}, u32[]{:S(2)}) collective-permute-start(bf16[768,384]{1,0:T(8,128)(2,1)S(1)} %copy-done.10), channel_id=1, source_target_pairs={{0,1},{1,0},{2,3},{3,2},{4,5},{5,4},{6,7},{7,6},{8,9},{9,8},{10,11... | collective-permute-start | bytes 1769480 | tf_op jit(solution)/shard_map/ppermute | solution.py:28
  31.2 5.7 %collective-permute-start.7 = (bf16[512,768]{1,0:T(8,128)(2,1)S(1)}, bf16[512,768]{1,0:T(8,128)(2,1)S(1)}, u32[]{:S(2)}, u32[]{:S(2)}) collective-permute-start(bf16[512,768]{1,0:T(8,128)(2,1)S(1)} %bitcast.56), channel_id=1, source_target_pairs={{0,1},{1,0},{2,3},{3,2},{4,5},{5,4},{6,7},{7,6},{8,9},{9,8},{10,11... | collective-permute-start | bytes 2359304 | tf_op jit(solution)/shard_map/ppermute | solution.py:28
  32.0 24.6 %all-to-all-start.1 = ((bf16[16,32,768]{2,1,0:T(8,128)(2,1)}), bf16[16,32,768]{2,1,0:T(8,128)(2,1)S(1)}, u32[]{:S(2)}, u32[]{:S(2)}) async-start(bf16[16,32,768]{2,1,0:T(8,128)(2,1)} %constant_dynamic-slice_fusion.1), calls=%async_computation.1 | async-start | bytes 1572864 | tf_op jit(solution)/shard_map/all_to_all | solution.py:937
  88.4 16.5 %collective-permute-start.15 = (bf16[512,1536]{1,0:T(8,128)(2,1)}, bf16[512,1536]{1,0:T(8,128)(2,1)}, u32[]{:S(2)}, u32[]{:S(2)}) collective-permute-start(bf16[512,1536]{1,0:T(8,128)(2,1)} %get-tuple-element.133), channel_id=1, source_target_pairs={{0,1},{1,0},{2,3},{3,2},{4,5},{5,4},{6,7},{7,6},{8,9},{9,8},{10,11... | collective-permute-start | bytes 4718600 | tf_op jit(solution)/shard_map/ppermute | solution.py:28
  88.7 26.8 %collective-permute-start.12 = (bf16[512,1536]{1,0:T(8,128)(2,1)}, bf16[512,1536]{1,0:T(8,128)(2,1)S(1)}, u32[]{:S(2)}, u32[]{:S(2)}) collective-permute-start(bf16[512,1536]{1,0:T(8,128)(2,1)} %get-tuple-element.129), channel_id=1, source_target_pairs={{0,1},{1,0},{2,3},{3,2},{4,5},{5,4},{6,7},{7,6},{8,9},{9,8},{10,11... | collective-permute-start | bytes 4718600 | tf_op jit(solution)/shard_map/ppermute | solution.py:28
  88.9 15.9 %collective-permute-start.14 = (bf16[512,768]{1,0:T(8,128)(2,1)}, bf16[512,768]{1,0:T(8,128)(2,1)}, u32[]{:S(2)}, u32[]{:S(2)}) collective-permute-start(bf16[512,768]{1,0:T(8,128)(2,1)} %get-tuple-element.131.refs_0_), channel_id=1, source_target_pairs={{0,1},{1,0},{2,3},{3,2},{4,5},{5,4},{6,7},{7,6},{8,9},{9,8},{10,11... | collective-permute-start | bytes 2359304 | tf_op jit(solution)/shard_map/ppermute | solution.py:28
  89.3 15.7 %collective-permute-start.16 = (bf16[512,768]{1,0:T(8,128)(2,1)}, bf16[512,768]{1,0:T(8,128)(2,1)}, u32[]{:S(2)}, u32[]{:S(2)}) collective-permute-start(bf16[512,768]{1,0:T(8,128)(2,1)} %get-tuple-element.134.refs_4_), channel_id=1, source_target_pairs={{0,1},{1,0},{2,3},{3,2},{4,5},{5,4},{6,7},{7,6},{8,9},{9,8},{10,11... | collective-permute-start | bytes 2359304 | tf_op jit(solution)/shard_map/ppermute | solution.py:28
  89.4 26.1 %collective-permute-start.11 = (bf16[512,768]{1,0:T(8,128)(2,1)}, bf16[512,768]{1,0:T(8,128)(2,1)S(1)}, u32[]{:S(2)}, u32[]{:S(2)}) collective-permute-start(bf16[512,768]{1,0:T(8,128)(2,1)} %get-tuple-element.127.refs_0_), channel_id=1, source_target_pairs={{0,1},{1,0},{2,3},{3,2},{4,5},{5,4},{6,7},{7,6},{8,9},{9,8},{10,11... | collective-permute-start | bytes 2359304 | tf_op jit(solution)/shard_map/ppermute | solution.py:28
  93.1 55.9 %all-to-all-start.2 = ((bf16[16,32,768]{2,1,0:T(8,128)(2,1)}), bf16[16,32,768]{2,1,0:T(8,128)(2,1)S(1)}, u32[]{:S(2)}, u32[]{:S(2)}) async-start(bf16[16,32,768]{2,1,0:T(8,128)(2,1)} %route.2), calls=%async_computation.2 | async-start | bytes 1572864 | tf_op jit(solution)/shard_map/all_to_all | solution.py:937
  104.8 20.0 %collective-permute-start.18 = (bf16[512,384]{1,0:T(8,128)(2,1)}, bf16[512,384]{1,0:T(8,128)(2,1)S(1)}, u32[]{:S(2)}, u32[]{:S(2)}) collective-permute-start(bf16[512,384]{1,0:T(8,128)(2,1)} %get-tuple-element.137), channel_id=1, source_target_pairs={{0,1},{1,0},{2,3},{3,2},{4,5},{5,4},{6,7},{7,6},{8,9},{9,8},{10,11... | collective-permute-start | bytes 1179656 | tf_op jit(solution)/shard_map/ppermute | solution.py:28
  113.6 38.1 %collective-permute-start.17 = (bf16[2,4,48,1920]{3,2,1,0:T(8,128)(2,1)}, bf16[2,4,48,1920]{3,2,1,0:T(8,128)(2,1)}, u32[]{:S(2)}, u32[]{:S(2)}) collective-permute-start(bf16[2,4,48,1920]{3,2,1,0:T(8,128)(2,1)} %get-tuple-element.135), channel_id=1, source_target_pairs={{0,4},{2,6},{4,0},{6,2},{8,12},{10,14},{12,8},{14,10},{16,20},{18,... | collective-permute-start | bytes 4423688 | tf_op jit(solution)/shard_map/ppermute | solution.py:1083
  123.3 28.4 %collective-permute-start.13 = (bf16[2,4,48,1536]{3,2,1,0:T(8,128)(2,1)}, bf16[2,4,48,1536]{3,2,1,0:T(8,128)(2,1)}, u32[]{:S(2)}, u32[]{:S(2)}) collective-permute-start(bf16[2,4,48,1536]{3,2,1,0:T(8,128)(2,1)} %get-tuple-element.130), channel_id=1, source_target_pairs={{0,2},{2,0},{4,6},{6,4},{8,10},{10,8},{12,14},{14,12},{16,18},{18,... | collective-permute-start | bytes 3538952 | tf_op jit(solution)/shard_map/ppermute | solution.py:1083
  142.6 13.4 %collective-permute-start.19 = (bf16[512,1152]{1,0:T(8,128)(2,1)}, bf16[512,1152]{1,0:T(8,128)(2,1)}, u32[]{:S(2)}, u32[]{:S(2)}) collective-permute-start(bf16[512,1152]{1,0:T(8,128)(2,1)} %get-tuple-element.144.refs_3_), channel_id=1, source_target_pairs={{0,1},{1,0},{2,3},{3,2},{4,5},{5,4},{6,7},{7,6},{8,9},{9,8},{10,11... | collective-permute-start | bytes 3538952 | tf_op jit(solution)/shard_map/ppermute | solution.py:28
  162.6 3.2 %collective-permute-start.20 = (bf16[512,768]{1,0:T(8,128)(2,1)}, bf16[512,768]{1,0:T(8,128)(2,1)}, u32[]{:S(2)}, u32[]{:S(2)}) collective-permute-start(bf16[512,768]{1,0:T(8,128)(2,1)} %input_rows.1.refs_3_), channel_id=1, source_target_pairs={{0,1},{1,0},{2,3},{3,2},{4,5},{5,4},{6,7},{7,6},{8,9},{9,8},{10,11... | collective-permute-start | bytes 2359304 | tf_op jit(solution)/shard_map/ppermute | solution.py:28
  162.6 23.8 %collective-permute-start.27 = (bf16[4,48,1920]{2,1,0:T(8,128)(2,1)}, bf16[4,48,1920]{2,1,0:T(8,128)(2,1)}, u32[]{:S(2)}, u32[]{:S(2)}) collective-permute-start(bf16[4,48,1920]{2,1,0:T(8,128)(2,1)} %fusion), channel_id=1, source_target_pairs={{0,2},{2,0},{4,6},{6,4},{8,10},{10,8},{12,14},{14,12},{16,18},{18,... | collective-permute-start | bytes 2211848 | tf_op jit(solution)/shard_map/ppermute | solution.py:1095
  165.8 20.5 %collective-permute-start.26 = (bf16[4,48,1536]{2,1,0:T(8,128)(2,1)}, bf16[4,48,1536]{2,1,0:T(8,128)(2,1)}, u32[]{:S(2)}, u32[]{:S(2)}) collective-permute-start(bf16[4,48,1536]{2,1,0:T(8,128)(2,1)} %fusion.2), channel_id=1, source_target_pairs={{0,4},{2,6},{4,0},{6,2},{8,12},{10,14},{12,8},{14,10},{16,20},{18,... | collective-permute-start | bytes 1769480 | tf_op jit(solution)/shard_map/ppermute | solution.py:1095
  169.2 41.7 %all-to-all-start.3 = ((bf16[16,40,768]{2,1,0:T(8,128)(2,1)}), bf16[16,40,768]{2,1,0:T(8,128)(2,1)}, u32[]{:S(2)}, u32[]{:S(2)}) async-start(bf16[16,40,768]{2,1,0:T(8,128)(2,1)} %route.3), calls=%async_computation.3 | async-start | bytes 1966080 | tf_op jit(solution)/shard_map/all_to_all | solution.py:937
  189.4 4.7 %collective-permute-start.21 = (bf16[16,32,768]{2,1,0:T(8,128)(2,1)S(1)}, bf16[16,32,768]{2,1,0:T(8,128)(2,1)}, u32[]{:S(2)}, u32[]{:S(2)}) collective-permute-start(bf16[16,32,768]{2,1,0:T(8,128)(2,1)S(1)} %all-to-all-done.2.mine_ref), channel_id=1, source_target_pairs={{0,1},{1,0},{2,3},{3,2},{4,5},{5,4},{6,7},{7,6},{8,9},{9,8},{10,11... | collective-permute-start | bytes 2359304 | tf_op jit(solution)/shard_map/ppermute | solution.py:28
  190.6 20.3 %collective-permute-start.28 = (bf16[2,48,3456]{2,1,0:T(8,128)(2,1)}, bf16[2,48,3456]{2,1,0:T(8,128)(2,1)}, u32[]{:S(2)}, u32[]{:S(2)}) collective-permute-start(bf16[2,48,3456]{2,1,0:T(8,128)(2,1)} %fusion.1), channel_id=1, source_target_pairs={{0,8},{2,10},{4,12},{6,14},{8,0},{10,2},{12,4},{14,6},{16,24},{18,... | collective-permute-start | bytes 1990664 | tf_op jit(solution)/shard_map/ppermute | solution.py:807
  190.6 22.7 %collective-permute-start.23 = (bf16[4,48,1152]{2,1,0:T(8,128)(2,1)}, bf16[4,48,1152]{2,1,0:T(8,128)(2,1)}, u32[]{:S(2)}, u32[]{:S(2)}) collective-permute-start(bf16[4,48,1152]{2,1,0:T(8,128)(2,1)} %get-tuple-element.146), channel_id=1, source_target_pairs={{0,2},{2,0},{4,6},{6,4},{8,10},{10,8},{12,14},{14,12},{16,18},{18,... | collective-permute-start | bytes 1327112 | tf_op jit(solution)/shard_map/ppermute | solution.py:824
  190.6 25.0 %collective-permute-start.24 = (bf16[4,48,1152]{2,1,0:T(8,128)(2,1)}, bf16[4,48,1152]{2,1,0:T(8,128)(2,1)}, u32[]{:S(2)}, u32[]{:S(2)}) collective-permute-start(bf16[4,48,1152]{2,1,0:T(8,128)(2,1)} %get-tuple-element.147), channel_id=1, source_target_pairs={{0,4},{2,6},{4,0},{6,2},{8,12},{10,14},{12,8},{14,10},{16,20},{18,... | collective-permute-start | bytes 1327112 | tf_op jit(solution)/shard_map/ppermute | solution.py:824
  191.7 23.8 %collective-permute-start.25 = (bf16[4,48,1152]{2,1,0:T(8,128)(2,1)}, bf16[4,48,1152]{2,1,0:T(8,128)(2,1)}, u32[]{:S(2)}, u32[]{:S(2)}) collective-permute-start(bf16[4,48,1152]{2,1,0:T(8,128)(2,1)} %get-tuple-element.148), channel_id=1, source_target_pairs={{0,6},{2,4},{4,2},{6,0},{8,14},{10,12},{12,10},{14,8},{16,22},{18,... | collective-permute-start | bytes 1327112 | tf_op jit(solution)/shard_map/ppermute | solution.py:824
  212.2 23.1 %collective-permute-start.32 = (bf16[1,48,3456]{2,1,0:T(8,128)(2,1)S(1)}, bf16[1,48,3456]{2,1,0:T(8,128)(2,1)S(1)}, u32[]{:S(2)}, u32[]{:S(2)}) collective-permute-start(bf16[1,48,3456]{2,1,0:T(8,128)(2,1)S(1)} %dynamic-slice_convert_fusion), channel_id=1, source_target_pairs={{0,16},{2,18},{4,20},{6,22},{8,24},{10,26},{12,28},{14,30},{16,0},... | collective-permute-start | bytes 995336 | tf_op jit(solution)/shard_map/ppermute | solution.py:807
  217.1 18.2 %collective-permute-start.29 = (bf16[48,1152]{1,0:T(8,128)(2,1)S(1)}, bf16[48,1152]{1,0:T(8,128)(2,1)S(1)}, u32[]{:S(2)}, u32[]{:S(2)}) collective-permute-start(bf16[48,1152]{1,0:T(8,128)(2,1)S(1)} %get-tuple-element.183), channel_id=1, source_target_pairs={{0,8},{2,10},{4,12},{6,14},{8,0},{10,2},{12,4},{14,6},{16,24},{18,... | collective-permute-start | bytes 331784 | tf_op jit(solution)/shard_map/ppermute | solution.py:819
  218.2 19.4 %collective-permute-start.30 = (bf16[48,1152]{1,0:T(8,128)(2,1)S(1)}, bf16[48,1152]{1,0:T(8,128)(2,1)S(1)}, u32[]{:S(2)}, u32[]{:S(2)}) collective-permute-start(bf16[48,1152]{1,0:T(8,128)(2,1)S(1)} %get-tuple-element.182), channel_id=1, source_target_pairs={{0,16},{2,18},{4,20},{6,22},{8,24},{10,26},{12,28},{14,30},{16,0},... | collective-permute-start | bytes 331784 | tf_op jit(solution)/shard_map/ppermute | solution.py:819
  221.8 15.8 %collective-permute-start.31 = (bf16[48,1152]{1,0:T(8,128)(2,1)S(1)}, bf16[48,1152]{1,0:T(8,128)(2,1)S(1)}, u32[]{:S(2)}, u32[]{:S(2)}) collective-permute-start(bf16[48,1152]{1,0:T(8,128)(2,1)S(1)} %get-tuple-element.181), channel_id=1, source_target_pairs={{0,24},{2,26},{4,28},{6,30},{8,16},{10,18},{12,20},{14,22},{16,8},... | collective-permute-start | bytes 331784 | tf_op jit(solution)/shard_map/ppermute | solution.py:819
  221.8 17.4 %collective-permute-start.22 = (bf16[16,40,768]{2,1,0:T(8,128)(2,1)}, bf16[16,40,768]{2,1,0:T(8,128)(2,1)S(1)}, u32[]{:S(2)}, u32[]{:S(2)}) collective-permute-start(bf16[16,40,768]{2,1,0:T(8,128)(2,1)} %all-to-all-done.3.mine_ref), channel_id=1, source_target_pairs={{0,1},{1,0},{2,3},{3,2},{4,5},{5,4},{6,7},{7,6},{8,9},{9,8},{10,11... | collective-permute-start | bytes 2949128 | tf_op jit(solution)/shard_map/ppermute | solution.py:28
  (34 other events, 255.3 us)

commit v3 on v2

--- a/solution.py
+++ b/solution.py
@@ -801,6 +801,19 @@
     return kept, lax.dynamic_index_in_dim(total, 1 - side, 1, keepdims=False).astype(BF16)
 
 
+def far_halves_of(terms, groups, bit):
+    side = (lax.axis_index("dp") // near_groups(groups)[0] >> bit) & 1
+    halves = []
+    for which in (side, 1 - side):
+        total = 0.0
+        for n, term in enumerate(terms):
+            term = term.reshape(-1, 2, *term.shape[1:])
+            term = lax.dynamic_index_in_dim(term, which, 1, keepdims=False).astype(F32)
+            total = total + term if n else term
+        halves.append(total)
+    return halves[0], halves[1].astype(BF16)
+
+
 def far_step(halves, groups, bit, first=()):
     near, far = near_groups(groups)
     kept, sent = halves
@@ -1098,9 +1111,12 @@
     )
     given = route(core, token_slot, input_low, swap(input_low), groups, (sums, up_sums, qv_sums))
     got = after(got, given)
+    parts = [[k] for k in kept]
     if got:
-        kept = [k + f[0].astype(F32) + g.astype(F32) for k, f, g in zip(kept, first_got, got)]
-    ffn_terms = far_halves(jnp.concatenate(kept, axis=2), groups, 0)
+        parts = [[k, f[0], g] for k, f, g in zip(kept, first_got, got)]
+    ffn_terms = [
+        jnp.concatenate(half, axis=-1) for half in zip(*(far_halves_of(p, groups, 0) for p in parts))
+    ]
     payload, given = given, exchange(given)
     layer_out = weave(core, after(returned, payload), half_run)
     ffn_sum = far_step(ffn_terms, groups, 0, (given, layer_out))

time: 244 us -> 246 us (level)
  waiting for transfers between devices: 61.2 us -> 53 us
  local copies, waits for them, and re-layouts: 18.1 us -> 22.9 us
  starting transfers between devices: 51.5 us -> 55.6 us
    ppermute x2, waiting for transfers between devices: 10.8 us -> 5.07 us  [local(): lax.ppermute(v, 'dp', pairs(groups, 2 - n))]
    slice x0 -> x5, local copies, waits for them, and re-layouts: none -> 3.38 us  [the longest x2 2.27 us: local(): kept, first_got = ([k[0].astype(F32) for k in kept], got)]
    add x2 -> x0, other arithmetic: 3.03 us -> none  [local(): k + f[0].astype(F32) + g.astype(F32)]
    ppermute x2, starting transfers between devices: 1.17 us -> 4.08 us  [far_step(): got = after(lax.ppermute(sent, 'dp', pairs(groups, near << bit)), first)]
    unnamed x58 -> x68, local copies, waits for them, and re-layouts: 6.53 us -> 8.94 us
  transfers between devices with their start and end apart: 37 -> 37, of which waited for: 13 -> 12; matrix products, arithmetic and copies ran while one was open for 9% -> 10% of each run, Pallas kernels for 27% -> 27%
where the time goes in v3:
time: 246 us; the launch traced here: 244 us
  Pallas kernels  101 us (41%)
  starting transfers between devices  55.6 us (23%)
  waiting for transfers between devices  53 us (22%)
  local copies, waits for them, and re-layouts  22.9 us (9%)
  other arithmetic  10.7 us (4%)
    all_to_all x4, starting transfers between devices, exchange(): return lax.all_to_all(values, 'dp', split_axis=0, concat_axis=0, tiled=True)  32 us
    ppermute x2, waiting for transfers between devices, far_step(): got = after(lax.ppermute(sent, 'dp', pairs(groups, near << bit)), first)  27.1 us
    pallas_call x1, Pallas kernels, row_pass(): pl.pallas_call(functools.partial(rows_kernel, run_rows), grid_spec=pltpu....  25.4 us
    pallas_call x3, Pallas kernels, gradients(): pl.pallas_call(functools.partial(gradient_kernel, chunks, near, share, ha...  21.2 us
    pallas_call x1, Pallas kernels, attention_backward(): pl.pallas_call(backward_kernel, grid_spec=pltpu.PrefetchScalarGridSpec(nu...  17.1 us
    pallas_call x1, Pallas kernels, attention_forward(): pl.pallas_call(forward_kernel, grid_spec=pltpu.PrefetchScalarGridSpec(num...  9.63 us
    all_to_all x4, waiting for transfers between devices, exchange(): return lax.all_to_all(values, 'dp', split_axis=0, concat_axis=0, tiled=True)  9.55 us
    unnamed x68, local copies, waits for them, and re-layouts  8.94 us
  transfers between devices with their start and end apart: 37, of which 12 were waited for; matrix products, arithmetic and copies ran while one was open for 10% of the time, Pallas kernels for 27%

profile of v3, /device:TPU:0, one launch (start us, length us, event | category | flops | bytes accessed | tf_op | source)
XLA Modules:
  0.0 244.2 jit_solution(18165983907982218139)
XLA Ops:
  3.1 8.3 %all-to-all-start = ((bf16[16,32,768]{2,1,0:T(8,128)(2,1)}), bf16[16,32,768]{2,1,0:T(8,128)(2,1)S(1)}, u32[]{:S(2)}, u32[]{:S(2)}) async-start(bf16[16,32,768]{2,1,0:T(8,128)(2,1)} %constant_dynamic-slice_fusion.2), calls=%async_computation | async-start | bytes 1572864 | tf_op jit(solution)/shard_map/all_to_all | solution.py:950
  19.3 2.1 constant_dynamic-slice_fusion.1
  22.0 9.2 %all-to-all-done = bf16[16,32,768]{2,1,0:T(8,128)(2,1)S(1)} async-done(((bf16[16,32,768]{2,1,0:T(8,128)(2,1)}), bf16[16,32,768]{2,1,0:T(8,128)(2,1)S(1)}, u32[]{:S(2)}, u32[]{:S(2)}) %all-to-all-start) | async-done | bytes 786464 | tf_op jit(solution)/shard_map/all_to_all | solution.py:950
  32.1 4.9 %all-to-all-start.1 = ((bf16[16,32,768]{2,1,0:T(8,128)(2,1)}), bf16[16,32,768]{2,1,0:T(8,128)(2,1)S(1)}, u32[]{:S(2)}, u32[]{:S(2)}) async-start(bf16[16,32,768]{2,1,0:T(8,128)(2,1)} %constant_dynamic-slice_fusion.1), calls=%async_computation.1 | async-start | bytes 1572864 | tf_op jit(solution)/shard_map/all_to_all | solution.py:950
  37.9 8.8 %intake.1 = (bf16[1024,768]{1,0:T(8,128)(2,1)}, bf16[1024,384]{1,0:T(8,128)(2,1)}, bf16[1024,384]{1,0:T(8,128)(2,1)}, bf16[1024,384]{1,0:T(8,128)(2,1)}) custom-call(s32[1]{0:T(128)} %bitcast.core.refs_0_, s32[1,1024]{1,0:T(1,128)} %refs_2_.5, bf16[512,768]{1,0:T(8,128)(2,1)} %bitcast.106, bf16[512,768]{1,0:T(8,128)(2,1)} %copy-done.30, ...), custom_call_target="tpu_custom_call" | custom-call | flops 3422552064 | bytes 6291456 | tf_op jit(solution)/shard_map/intake/pallas_call | solution.py:394
  46.7 9.6 %attend.1 = (bf16[512,384]{1,0:T(8,128)(2,1)}, bf16[512,384]{1,0:T(8,128)(2,1)}, f32[8,1024]{1,0:T(8,128)}) custom-call(s32[1,4]{1,0:T(1,128)} %lengths.3, s32[1]{0:T(128)} %bitcast.core.refs_0_, bf16[1024,384]{1,0:T(8,128)(2,1)} %get-tuple-element.104.q_ref, bf16[1024,384]{1,0:T(8,128)(2,1)} %get-tuple-element.105.k_ref, ...), custom_call_target="tpu_custom_call" | custom-call | flops 6442450944 | bytes 3145728 | tf_op jit(solution)/shard_map/attend/pallas_call | solution.py:169
  57.2 2.2 collective-permute-done.8.mixed_other
  60.4 25.4 %row_pass.1 = (bf16[512,768]{1,0:T(8,128)(2,1)}, bf16[512,768]{1,0:T(8,128)(2,1)}, bf16[512,768]{1,0:T(8,128)(2,1)}, bf16[512,1536]{1,0:T(8,128)(2,1)}, bf16[512...) custom-call(s32[1]{0:T(128)} %bitcast.core.refs_0_, ...), custom_call_target="tpu_custom_call" | custom-call | flops 12683575296 | bytes 30670848 | tf_op jit(solution)/shard_map/row_pass/pallas_call | solution.py:629
  86.2 2.1 collective-permute-done.10.refs_4_
  89.8 3.3 %route.2 = bf16[16,32,768]{2,1,0:T(8,128)(2,1)} custom-call(s32[1]{0:T(128)} %bitcast.core.refs_0_, s32[1,1024]{1,0:T(1,128)} %refs_2_.5, s32[1,1024]{1,0:T(1,128)} %refs_2_.5, bf16[512,768]{1,0:T(8,128)(2,1)} %get-tuple-element.126.refs_3_, bf16[512,768]{1,0:T(8,128)(2,1)} %copy-done.27), custom_call_target="tpu_custom_call" | custom-call | flops 805306368 | bytes 2359296 | tf_op jit(solution)/shard_map/route/pallas_call | solution.py:933
  93.0 11.8 %all-to-all-start.2 = ((bf16[16,32,768]{2,1,0:T(8,128)(2,1)}), bf16[16,32,768]{2,1,0:T(8,128)(2,1)S(1)}, u32[]{:S(2)}, u32[]{:S(2)}) async-start(bf16[16,32,768]{2,1,0:T(8,128)(2,1)} %route.2), calls=%async_computation.2 | async-start | bytes 1572864 | tf_op jit(solution)/shard_map/all_to_all | solution.py:950
  106.2 8.7 %gradients.4 = (bf16[2,4,48,1920]{3,2,1,0:T(8,128)(2,1)}, bf16[2,4,48,1920]{3,2,1,0:T(8,128)(2,1)}) custom-call(s32[1]{0:T(128)} %bitcast.1.me, bf16[512,768]{1,0:T(8,128)(2,1)} %get-tuple-element.131.refs_0_, bf16[512,768]{1,0:T(8,128)(2,1)} %collective-permute-done.14.refs_1_, bf16[512,1536]{1,0:T(8,128)(2,1)} %get-tuple-element.132.refs_2_, ...), custom_call_target="tpu_custom_call" | custom-call | flops 3019898880 | bytes 9043968 | tf_op jit(solution)/shard_map/gradients/pallas_call | solution.py:777
  117.6 6.4 %gradients.3 = (bf16[2,4,48,1536]{3,2,1,0:T(8,128)(2,1)}, bf16[2,4,48,1536]{3,2,1,0:T(8,128)(2,1)}) custom-call(s32[1]{0:T(128)} %bitcast.1.me, bf16[512,768]{1,0:T(8,128)(2,1)} %get-tuple-element.127.refs_0_, bf16[512,768]{1,0:T(8,128)(2,1)} %copy-done.26, bf16[512,1536]{1,0:T(8,128)(2,1)} %get-tuple-element.128.refs_2_, ...), custom_call_target="tpu_custom_call" | custom-call | flops 2415919104 | bytes 7864320 | tf_op jit(solution)/shard_map/gradients/pallas_call | solution.py:777
  126.3 17.1 %attend_back.1 = (bf16[512,1152]{1,0:T(8,128)(2,1)}, bf16[512,1152]{1,0:T(8,128)(2,1)}, f32[8,384]{1,0:T(8,128)}) custom-call(s32[1,4]{1,0:T(1,128)} %lengths.3, s32[1]{0:T(128)} %bitcast.core.refs_0_, bf16[1024,384]{1,0:T(8,128)(2,1)} %get-tuple-element.104.q_ref, bf16[512,384]{1,0:T(8,128)(2,1)} %get-tuple-element.140.do_mine, ...), custom_call_target="tpu_custom_call" | custom-call | flops 16106127360 | bytes 6291456 | tf_op jit(solution)/shard_map/attend_back/pallas_call | solution.py:312
  143.4 6.2 %gradients.5 = (bf16[4,48,1152]{2,1,0:T(8,128)(2,1)}, bf16[4,48,1152]{2,1,0:T(8,128)(2,1)}, bf16[4,48,1152]{2,1,0:T(8,128)(2,1)}, bf16[4,48,1152]{2,1,0:T(8,128)(2,1)}) custom-call(s32[1]{0:T(128)} %bitcast.1.me, bf16[1024,768]{1,0:T(8,128)(2,1)} %get-tuple-element.103.x_ref.refs_0_.refs_1_, bf16[1024,768]{1,0:T(8,128)(2,1)} %get-tuple-element.103.x_ref.refs_0_.refs_1_, ...), custom_call_target="tpu_custom_call" | custom-call | flops 1811939328 | bytes 6684672 | tf_op jit(solution)/shard_map/gradients/pallas_call | solution.py:777
  149.6 2.8 %collective-permute-done.13 = bf16[2,4,48,1536]{3,2,1,0:T(8,128)(2,1)} collective-permute-done((bf16[2,4,48,1536]{3,2,1,0:T(8,128)(2,1)}, bf16[2,4,48,1536]{3,2,1,0:T(8,128)(2,1)}, u32[]{:S(2)}, u32[]{:S(2)}) %collective-permute-start.13) | collective-permute-done | bytes 1179680 | tf_op jit(solution)/shard_map/ppermute | solution.py:1096
  152.4 2.7 %fusion = bf16[4,48,1920]{2,1,0:T(8,128)(2,1)} fusion(bf16[2,4,48,1920]{3,2,1,0:T(8,128)(2,1)S(1)} %collective-permute-done.17, bf16[2,4,48,1920]{3,2,1,0:T(8,128)(2,1)} %get-tuple-element.139), kind=kLoop, calls=%fused_computation.4 | loop fusion | flops 1474560 | bytes 2211840 | tf_op jit(solution)/shard_map/convert_element_type | solution.py:1104
  155.1 2.0 fusion.5
  157.1 6.6 %input_rows.1.refs_3_ = bf16[512,768]{1,0:T(8,128)(2,1)} custom-call(f32[512,768]{1,0:T(8,128)} %get-tuple-element.153.first_ref, bf16[512,1152]{1,0:T(8,128)(2,1)} %get-tuple-element.143.refs_2_.mine_ref, bf16[512,1152]{1,0:T(8,128)(2,1)} %collective-permute-done.19.other_ref, bf16[768,384]{1,0:T(8,128)(2,1)} %refs_0_.1, bf16[768,384]{1,0:T(8,128)(2,1)} %refs_1_.4, ...), custom_call_target="tpu_custom_call" | custom-call | flops 1811939328 | bytes 6684672 | tf_op jit(solution)/shard_map/input_rows/pallas_call | solution.py:865
  163.8 3.0 %collective-permute-start.27 = (bf16[4,48,1920]{2,1,0:T(8,128)(2,1)}, bf16[4,48,1920]{2,1,0:T(8,128)(2,1)S(1)}, u32[]{:S(2)}, u32[]{:S(2)}) collective-permute-start(bf16[4,48,1920]{2,1,0:T(8,128)(2,1)} %fusion), channel_id=1, source_target_pairs={{0,2},{2,0},{4,6},{6,4},{8,10},{10,8},{12,14},{14,12},{16,18},{18,... | collective-permute-start | bytes 2211848 | tf_op jit(solution)/shard_map/ppermute | solution.py:1108
  167.7 3.4 %route.3 = bf16[16,40,768]{2,1,0:T(8,128)(2,1)} custom-call(s32[1]{0:T(128)} %bitcast.core.refs_0_, s32[1,1024]{1,0:T(1,128)} %refs_2_.5, s32[1,1024]{1,0:T(1,128)} %refs_2_.5, bf16[512,768]{1,0:T(8,128)(2,1)} %input_rows.1.refs_3_, bf16[512,768]{1,0:T(8,128)(2,1)} %copy-done.29, f32[8,768]{1,0:T(8,128)} %get-tuple-element.157.refs_5_, ...), custom_call_target="tpu_custom_call" | custom-call | flops 805306368 | bytes 2359296 | tf_op jit(solution)/shard_map/route/pallas_call | solution.py:933
  171.1 7.0 %all-to-all-start.3 = ((bf16[16,40,768]{2,1,0:T(8,128)(2,1)}), bf16[16,40,768]{2,1,0:T(8,128)(2,1)S(1)}, u32[]{:S(2)}, u32[]{:S(2)}) async-start(bf16[16,40,768]{2,1,0:T(8,128)(2,1)} %route.3), calls=%async_computation.3 | async-start | bytes 1966080 | tf_op jit(solution)/shard_map/all_to_all | solution.py:950
  181.7 5.1 %collective-permute-done.26 = bf16[4,48,1536]{2,1,0:T(8,128)(2,1)} collective-permute-done((bf16[4,48,1536]{2,1,0:T(8,128)(2,1)}, bf16[4,48,1536]{2,1,0:T(8,128)(2,1)}, u32[]{:S(2)}, u32[]{:S(2)}) %collective-permute-start.26) | collective-permute-done | bytes 589856 | tf_op jit(solution)/shard_map/ppermute | solution.py:1108
  191.1 3.2 %collective-permute-start.25 = (bf16[4,48,1152]{2,1,0:T(8,128)(2,1)}, bf16[4,48,1152]{2,1,0:T(8,128)(2,1)}, u32[]{:S(2)}, u32[]{:S(2)}) collective-permute-start(bf16[4,48,1152]{2,1,0:T(8,128)(2,1)} %get-tuple-element.148), channel_id=1, source_target_pairs={{0,6},{2,4},{4,2},{6,0},{8,14},{10,12},{12,10},{14,8},{16,22},{18,... | collective-permute-start | bytes 1327112 | tf_op jit(solution)/shard_map/ppermute | solution.py:837
  194.3 2.6 %weave.2 = bf16[16,2,32,768]{3,2,1,0:T(8,128)(2,1)} custom-call(s32[1]{0:T(128)} %bitcast.core.refs_0_, bf16[16,32,768]{2,1,0:T(8,128)(2,1)} %copy-done.3, bf16[16,32,768]{2,1,0:T(8,128)(2,1)} %collective-permute-done.21.other_ref), custom_call_target="tpu_custom_call" | custom-call | flops 1 | bytes 1 | tf_op jit(solution)/shard_map/weave/pallas_call | solution.py:985
  196.9 13.6 %collective-permute-done.28 = bf16[2,48,3456]{2,1,0:T(8,128)(2,1)} collective-permute-done((bf16[2,48,3456]{2,1,0:T(8,128)(2,1)}, bf16[2,48,3456]{2,1,0:T(8,128)(2,1)}, u32[]{:S(2)}, u32[]{:S(2)}) %collective-permute-start.28) | collective-permute-done | bytes 663584 | tf_op jit(solution)/shard_map/ppermute | solution.py:820
  212.2 3.6 %collective-permute-start.32 = (bf16[1,48,3456]{2,1,0:T(8,128)(2,1)S(1)}, bf16[1,48,3456]{2,1,0:T(8,128)(2,1)S(1)}, u32[]{:S(2)}, u32[]{:S(2)}) collective-permute-start(bf16[1,48,3456]{2,1,0:T(8,128)(2,1)S(1)} %dynamic-slice_convert_fusion), channel_id=1, source_target_pairs={{0,16},{2,18},{4,20},{6,22},{8,24},{10,26},{12,28},{14,30},{16,0},... | collective-permute-start | bytes 995336 | tf_op jit(solution)/shard_map/ppermute | solution.py:820
  217.3 2.5 %collective-permute-start.29 = (bf16[48,1152]{1,0:T(8,128)(2,1)S(1)}, bf16[48,1152]{1,0:T(8,128)(2,1)S(1)}, u32[]{:S(2)}, u32[]{:S(2)}) collective-permute-start(bf16[48,1152]{1,0:T(8,128)(2,1)S(1)} %get-tuple-element.187), channel_id=1, source_target_pairs={{0,8},{2,10},{4,12},{6,14},{8,0},{10,2},{12,4},{14,6},{16,24},{18,... | collective-permute-start | bytes 331784 | tf_op jit(solution)/shard_map/ppermute | solution.py:832
  219.9 2.4 collective-permute-start.30
  222.7 13.5 %collective-permute-done.32 = bf16[1,48,3456]{2,1,0:T(8,128)(2,1)S(1)} collective-permute-done((bf16[1,48,3456]{2,1,0:T(8,128)(2,1)S(1)}, bf16[1,48,3456]{2,1,0:T(8,128)(2,1)S(1)}, u32[]{:S(2)}, u32[]{:S(2)}) %collective-permute-start.32) | collective-permute-done | bytes 331808 | tf_op jit(solution)/shard_map/ppermute | solution.py:820
  236.3 2.3 collective-permute-done.30
  241.2 2.8 %weave.3 = (bf16[16,2,32,768]{3,2,1,0:T(8,128)(2,1)}, f32[1,24]{1,0:T(1,128)}, f32[1,24]{1,0:T(1,128)}, f32[1,24]{1,0:T(1,128)}, f32[1,24]{1,0:T(1,128)}, /*inde...) custom-call(s32[1]{0:T(128)} %bitcast.core.refs_0_, ...), custom_call_target="tpu_custom_call" | custom-call | flops 1 | bytes 1 | tf_op jit(solution)/shard_map/weave/pallas_call | solution.py:985
  (154 shorter events, 37.8 us)
Async XLA Ops:
  0.7 30.5 %collective-permute-start.2 = (bf16[768,1536]{1,0:T(8,128)(2,1)}, bf16[768,1536]{1,0:T(8,128)(2,1)}, u32[]{:S(2)}, u32[]{:S(2)}) collective-permute-start(bf16[768,1536]{1,0:T(8,128)(2,1)} %up_mine.1), channel_id=1, source_target_pairs={{0,1},{1,0},{2,3},{3,2},{4,5},{5,4},{6,7},{7,6},{8,9},{9,8},{10,11... | collective-permute-start | bytes 7077896 | tf_op jit(solution)/shard_map/ppermute | solution.py:28
  1.2 30.0 %collective-permute-start.3 = (bf16[1536,768]{1,0:T(8,128)(2,1)}, bf16[1536,768]{1,0:T(8,128)(2,1)}, u32[]{:S(2)}, u32[]{:S(2)}) collective-permute-start(bf16[1536,768]{1,0:T(8,128)(2,1)} %down_mine.1), channel_id=1, source_target_pairs={{0,1},{1,0},{2,3},{3,2},{4,5},{5,4},{6,7},{7,6},{8,9},{9,8},{10,11... | collective-permute-start | bytes 7077896 | tf_op jit(solution)/shard_map/ppermute | solution.py:28
  3.1 28.1 %all-to-all-start = ((bf16[16,32,768]{2,1,0:T(8,128)(2,1)}), bf16[16,32,768]{2,1,0:T(8,128)(2,1)S(1)}, u32[]{:S(2)}, u32[]{:S(2)}) async-start(bf16[16,32,768]{2,1,0:T(8,128)(2,1)} %constant_dynamic-slice_fusion.2), calls=%async_computation | async-start | bytes 1572864 | tf_op jit(solution)/shard_map/all_to_all | solution.py:950
  12.0 19.2 %collective-permute-start.4 = (bf16[768,384]{1,0:T(8,128)(2,1)S(1)}, bf16[768,384]{1,0:T(8,128)(2,1)S(1)}, u32[]{:S(2)}, u32[]{:S(2)}) collective-permute-start(bf16[768,384]{1,0:T(8,128)(2,1)S(1)} %copy-done.11), channel_id=1, source_target_pairs={{0,1},{1,0},{2,3},{3,2},{4,5},{5,4},{6,7},{7,6},{8,9},{9,8},{10,11... | collective-permute-start | bytes 1769480 | tf_op jit(solution)/shard_map/ppermute | solution.py:28
  13.5 17.7 %collective-permute-start.5 = (bf16[768,384]{1,0:T(8,128)(2,1)S(1)}, bf16[768,384]{1,0:T(8,128)(2,1)}, u32[]{:S(2)}, u32[]{:S(2)}) collective-permute-start(bf16[768,384]{1,0:T(8,128)(2,1)S(1)} %copy-done.12), channel_id=1, source_target_pairs={{0,1},{1,0},{2,3},{3,2},{4,5},{5,4},{6,7},{7,6},{8,9},{9,8},{10,11... | collective-permute-start | bytes 1769480 | tf_op jit(solution)/shard_map/ppermute | solution.py:28
  13.9 17.3 %collective-permute-start.6 = (bf16[768,384]{1,0:T(8,128)(2,1)S(1)}, bf16[768,384]{1,0:T(8,128)(2,1)}, u32[]{:S(2)}, u32[]{:S(2)}) collective-permute-start(bf16[768,384]{1,0:T(8,128)(2,1)S(1)} %copy-done.13), channel_id=1, source_target_pairs={{0,1},{1,0},{2,3},{3,2},{4,5},{5,4},{6,7},{7,6},{8,9},{9,8},{10,11... | collective-permute-start | bytes 1769480 | tf_op jit(solution)/shard_map/ppermute | solution.py:28
  31.2 5.7 %collective-permute-start.7 = (bf16[512,768]{1,0:T(8,128)(2,1)S(1)}, bf16[512,768]{1,0:T(8,128)(2,1)S(1)}, u32[]{:S(2)}, u32[]{:S(2)}) collective-permute-start(bf16[512,768]{1,0:T(8,128)(2,1)S(1)} %bitcast.105), channel_id=1, source_target_pairs={{0,1},{1,0},{2,3},{3,2},{4,5},{5,4},{6,7},{7,6},{8,9},{9,8},{10,11... | collective-permute-start | bytes 2359304 | tf_op jit(solution)/shard_map/ppermute | solution.py:28
  32.1 24.6 %all-to-all-start.1 = ((bf16[16,32,768]{2,1,0:T(8,128)(2,1)}), bf16[16,32,768]{2,1,0:T(8,128)(2,1)S(1)}, u32[]{:S(2)}, u32[]{:S(2)}) async-start(bf16[16,32,768]{2,1,0:T(8,128)(2,1)} %constant_dynamic-slice_fusion.1), calls=%async_computation.1 | async-start | bytes 1572864 | tf_op jit(solution)/shard_map/all_to_all | solution.py:950
  88.4 16.6 %collective-permute-start.15 = (bf16[512,1536]{1,0:T(8,128)(2,1)}, bf16[512,1536]{1,0:T(8,128)(2,1)S(1)}, u32[]{:S(2)}, u32[]{:S(2)}) collective-permute-start(bf16[512,1536]{1,0:T(8,128)(2,1)} %get-tuple-element.133), channel_id=1, source_target_pairs={{0,1},{1,0},{2,3},{3,2},{4,5},{5,4},{6,7},{7,6},{8,9},{9,8},{10,11... | collective-permute-start | bytes 4718600 | tf_op jit(solution)/shard_map/ppermute | solution.py:28
  88.7 28.0 %collective-permute-start.12 = (bf16[512,1536]{1,0:T(8,128)(2,1)}, bf16[512,1536]{1,0:T(8,128)(2,1)}, u32[]{:S(2)}, u32[]{:S(2)}) collective-permute-start(bf16[512,1536]{1,0:T(8,128)(2,1)} %get-tuple-element.129), channel_id=1, source_target_pairs={{0,1},{1,0},{2,3},{3,2},{4,5},{5,4},{6,7},{7,6},{8,9},{9,8},{10,11... | collective-permute-start | bytes 4718600 | tf_op jit(solution)/shard_map/ppermute | solution.py:28
  88.9 16.0 %collective-permute-start.14 = (bf16[512,768]{1,0:T(8,128)(2,1)}, bf16[512,768]{1,0:T(8,128)(2,1)}, u32[]{:S(2)}, u32[]{:S(2)}) collective-permute-start(bf16[512,768]{1,0:T(8,128)(2,1)} %get-tuple-element.131.refs_0_), channel_id=1, source_target_pairs={{0,1},{1,0},{2,3},{3,2},{4,5},{5,4},{6,7},{7,6},{8,9},{9,8},{10,11... | collective-permute-start | bytes 2359304 | tf_op jit(solution)/shard_map/ppermute | solution.py:28
  89.3 15.8 %collective-permute-start.16 = (bf16[512,768]{1,0:T(8,128)(2,1)}, bf16[512,768]{1,0:T(8,128)(2,1)}, u32[]{:S(2)}, u32[]{:S(2)}) collective-permute-start(bf16[512,768]{1,0:T(8,128)(2,1)} %get-tuple-element.134.refs_4_), channel_id=1, source_target_pairs={{0,1},{1,0},{2,3},{3,2},{4,5},{5,4},{6,7},{7,6},{8,9},{9,8},{10,11... | collective-permute-start | bytes 2359304 | tf_op jit(solution)/shard_map/ppermute | solution.py:28
  89.4 27.3 %collective-permute-start.11 = (bf16[512,768]{1,0:T(8,128)(2,1)}, bf16[512,768]{1,0:T(8,128)(2,1)S(1)}, u32[]{:S(2)}, u32[]{:S(2)}) collective-permute-start(bf16[512,768]{1,0:T(8,128)(2,1)} %get-tuple-element.127.refs_0_), channel_id=1, source_target_pairs={{0,1},{1,0},{2,3},{3,2},{4,5},{5,4},{6,7},{7,6},{8,9},{9,8},{10,11... | collective-permute-start | bytes 2359304 | tf_op jit(solution)/shard_map/ppermute | solution.py:28
  93.0 56.5 %all-to-all-start.2 = ((bf16[16,32,768]{2,1,0:T(8,128)(2,1)}), bf16[16,32,768]{2,1,0:T(8,128)(2,1)S(1)}, u32[]{:S(2)}, u32[]{:S(2)}) async-start(bf16[16,32,768]{2,1,0:T(8,128)(2,1)} %route.2), calls=%async_computation.2 | async-start | bytes 1572864 | tf_op jit(solution)/shard_map/all_to_all | solution.py:950
  104.9 20.6 %collective-permute-start.18 = (bf16[512,384]{1,0:T(8,128)(2,1)S(1)}, bf16[512,384]{1,0:T(8,128)(2,1)S(1)}, u32[]{:S(2)}, u32[]{:S(2)}) collective-permute-start(bf16[512,384]{1,0:T(8,128)(2,1)S(1)} %copy-done.31), channel_id=1, source_target_pairs={{0,1},{1,0},{2,3},{3,2},{4,5},{5,4},{6,7},{7,6},{8,9},{9,8},{10,11... | collective-permute-start | bytes 1179656 | tf_op jit(solution)/shard_map/ppermute | solution.py:28
  114.8 37.6 %collective-permute-start.17 = (bf16[2,4,48,1920]{3,2,1,0:T(8,128)(2,1)}, bf16[2,4,48,1920]{3,2,1,0:T(8,128)(2,1)S(1)}, u32[]{:S(2)}, u32[]{:S(2)}) collective-permute-start(bf16[2,4,48,1920]{3,2,1,0:T(8,128)(2,1)} %get-tuple-element.135), channel_id=1, source_target_pairs={{0,4},{2,6},{4,0},{6,2},{8,12},{10,14},{12,8},{14,10},{16,20},{18,... | collective-permute-start | bytes 4423688 | tf_op jit(solution)/shard_map/ppermute | solution.py:1096
  124.0 28.4 %collective-permute-start.13 = (bf16[2,4,48,1536]{3,2,1,0:T(8,128)(2,1)}, bf16[2,4,48,1536]{3,2,1,0:T(8,128)(2,1)}, u32[]{:S(2)}, u32[]{:S(2)}) collective-permute-start(bf16[2,4,48,1536]{3,2,1,0:T(8,128)(2,1)} %get-tuple-element.130), channel_id=1, source_target_pairs={{0,2},{2,0},{4,6},{6,4},{8,10},{10,8},{12,14},{14,12},{16,18},{18,... | collective-permute-start | bytes 3538952 | tf_op jit(solution)/shard_map/ppermute | solution.py:1096
  143.3 13.8 %collective-permute-start.19 = (bf16[512,1152]{1,0:T(8,128)(2,1)}, bf16[512,1152]{1,0:T(8,128)(2,1)}, u32[]{:S(2)}, u32[]{:S(2)}) collective-permute-start(bf16[512,1152]{1,0:T(8,128)(2,1)} %get-tuple-element.144.refs_3_), channel_id=1, source_target_pairs={{0,1},{1,0},{2,3},{3,2},{4,5},{5,4},{6,7},{7,6},{8,9},{9,8},{10,11... | collective-permute-start | bytes 3538952 | tf_op jit(solution)/shard_map/ppermute | solution.py:28
  163.8 3.0 %collective-permute-start.20 = (bf16[512,768]{1,0:T(8,128)(2,1)}, bf16[512,768]{1,0:T(8,128)(2,1)S(1)}, u32[]{:S(2)}, u32[]{:S(2)}) collective-permute-start(bf16[512,768]{1,0:T(8,128)(2,1)} %input_rows.1.refs_3_), channel_id=1, source_target_pairs={{0,1},{1,0},{2,3},{3,2},{4,5},{5,4},{6,7},{7,6},{8,9},{9,8},{10,11... | collective-permute-start | bytes 2359304 | tf_op jit(solution)/shard_map/ppermute | solution.py:28
  163.8 23.0 %collective-permute-start.27 = (bf16[4,48,1920]{2,1,0:T(8,128)(2,1)}, bf16[4,48,1920]{2,1,0:T(8,128)(2,1)S(1)}, u32[]{:S(2)}, u32[]{:S(2)}) collective-permute-start(bf16[4,48,1920]{2,1,0:T(8,128)(2,1)} %fusion), channel_id=1, source_target_pairs={{0,2},{2,0},{4,6},{6,4},{8,10},{10,8},{12,14},{14,12},{16,18},{18,... | collective-permute-start | bytes 2211848 | tf_op jit(solution)/shard_map/ppermute | solution.py:1108
  166.8 20.0 %collective-permute-start.26 = (bf16[4,48,1536]{2,1,0:T(8,128)(2,1)}, bf16[4,48,1536]{2,1,0:T(8,128)(2,1)}, u32[]{:S(2)}, u32[]{:S(2)}) collective-permute-start(bf16[4,48,1536]{2,1,0:T(8,128)(2,1)} %fusion.5), channel_id=1, source_target_pairs={{0,4},{2,6},{4,0},{6,2},{8,12},{10,14},{12,8},{14,10},{16,20},{18,... | collective-permute-start | bytes 1769480 | tf_op jit(solution)/shard_map/ppermute | solution.py:1108
  171.1 39.5 %all-to-all-start.3 = ((bf16[16,40,768]{2,1,0:T(8,128)(2,1)}), bf16[16,40,768]{2,1,0:T(8,128)(2,1)S(1)}, u32[]{:S(2)}, u32[]{:S(2)}) async-start(bf16[16,40,768]{2,1,0:T(8,128)(2,1)} %route.3), calls=%async_computation.3 | async-start | bytes 1966080 | tf_op jit(solution)/shard_map/all_to_all | solution.py:950
  186.8 7.5 %collective-permute-start.21 = (bf16[16,32,768]{2,1,0:T(8,128)(2,1)S(1)}, bf16[16,32,768]{2,1,0:T(8,128)(2,1)}, u32[]{:S(2)}, u32[]{:S(2)}) collective-permute-start(bf16[16,32,768]{2,1,0:T(8,128)(2,1)S(1)} %all-to-all-done.2.mine_ref), channel_id=1, source_target_pairs={{0,1},{1,0},{2,3},{3,2},{4,5},{5,4},{6,7},{7,6},{8,9},{9,8},{10,11... | collective-permute-start | bytes 2359304 | tf_op jit(solution)/shard_map/ppermute | solution.py:28
  190.3 20.2 %collective-permute-start.28 = (bf16[2,48,3456]{2,1,0:T(8,128)(2,1)}, bf16[2,48,3456]{2,1,0:T(8,128)(2,1)}, u32[]{:S(2)}, u32[]{:S(2)}) collective-permute-start(bf16[2,48,3456]{2,1,0:T(8,128)(2,1)} %pad_maximum_fusion), channel_id=1, source_target_pairs={{0,8},{2,10},{4,12},{6,14},{8,0},{10,2},{12,4},{14,6},{16,24},{18,... | collective-permute-start | bytes 1990664 | tf_op jit(solution)/shard_map/ppermute | solution.py:820
  190.8 24.9 %collective-permute-start.23 = (bf16[4,48,1152]{2,1,0:T(8,128)(2,1)}, bf16[4,48,1152]{2,1,0:T(8,128)(2,1)}, u32[]{:S(2)}, u32[]{:S(2)}) collective-permute-start(bf16[4,48,1152]{2,1,0:T(8,128)(2,1)} %get-tuple-element.146), channel_id=1, source_target_pairs={{0,2},{2,0},{4,6},{6,4},{8,10},{10,8},{12,14},{14,12},{16,18},{18,... | collective-permute-start | bytes 1327112 | tf_op jit(solution)/shard_map/ppermute | solution.py:837
  190.8 24.9 %collective-permute-start.24 = (bf16[4,48,1152]{2,1,0:T(8,128)(2,1)}, bf16[4,48,1152]{2,1,0:T(8,128)(2,1)}, u32[]{:S(2)}, u32[]{:S(2)}) collective-permute-start(bf16[4,48,1152]{2,1,0:T(8,128)(2,1)} %get-tuple-element.147), channel_id=1, source_target_pairs={{0,4},{2,6},{4,0},{6,2},{8,12},{10,14},{12,8},{14,10},{16,20},{18,... | collective-permute-start | bytes 1327112 | tf_op jit(solution)/shard_map/ppermute | solution.py:837
  191.1 24.6 %collective-permute-start.25 = (bf16[4,48,1152]{2,1,0:T(8,128)(2,1)}, bf16[4,48,1152]{2,1,0:T(8,128)(2,1)}, u32[]{:S(2)}, u32[]{:S(2)}) collective-permute-start(bf16[4,48,1152]{2,1,0:T(8,128)(2,1)} %get-tuple-element.148), channel_id=1, source_target_pairs={{0,6},{2,4},{4,2},{6,0},{8,14},{10,12},{12,10},{14,8},{16,22},{18,... | collective-permute-start | bytes 1327112 | tf_op jit(solution)/shard_map/ppermute | solution.py:837
  212.2 24.1 %collective-permute-start.32 = (bf16[1,48,3456]{2,1,0:T(8,128)(2,1)S(1)}, bf16[1,48,3456]{2,1,0:T(8,128)(2,1)S(1)}, u32[]{:S(2)}, u32[]{:S(2)}) collective-permute-start(bf16[1,48,3456]{2,1,0:T(8,128)(2,1)S(1)} %dynamic-slice_convert_fusion), channel_id=1, source_target_pairs={{0,16},{2,18},{4,20},{6,22},{8,24},{10,26},{12,28},{14,30},{16,0},... | collective-permute-start | bytes 995336 | tf_op jit(solution)/shard_map/ppermute | solution.py:820
  217.3 19.0 %collective-permute-start.29 = (bf16[48,1152]{1,0:T(8,128)(2,1)S(1)}, bf16[48,1152]{1,0:T(8,128)(2,1)S(1)}, u32[]{:S(2)}, u32[]{:S(2)}) collective-permute-start(bf16[48,1152]{1,0:T(8,128)(2,1)S(1)} %get-tuple-element.187), channel_id=1, source_target_pairs={{0,8},{2,10},{4,12},{6,14},{8,0},{10,2},{12,4},{14,6},{16,24},{18,... | collective-permute-start | bytes 331784 | tf_op jit(solution)/shard_map/ppermute | solution.py:832
  219.9 18.7 %collective-permute-start.30 = (bf16[48,1152]{1,0:T(8,128)(2,1)S(1)}, bf16[48,1152]{1,0:T(8,128)(2,1)S(1)}, u32[]{:S(2)}, u32[]{:S(2)}) collective-permute-start(bf16[48,1152]{1,0:T(8,128)(2,1)S(1)} %get-tuple-element.186), channel_id=1, source_target_pairs={{0,16},{2,18},{4,20},{6,22},{8,24},{10,26},{12,28},{14,30},{16,0},... | collective-permute-start | bytes 331784 | tf_op jit(solution)/shard_map/ppermute | solution.py:832
  222.2 16.4 %collective-permute-start.31 = (bf16[48,1152]{1,0:T(8,128)(2,1)S(1)}, bf16[48,1152]{1,0:T(8,128)(2,1)S(1)}, u32[]{:S(2)}, u32[]{:S(2)}) collective-permute-start(bf16[48,1152]{1,0:T(8,128)(2,1)S(1)} %get-tuple-element.185), channel_id=1, source_target_pairs={{0,24},{2,26},{4,28},{6,30},{8,16},{10,18},{12,20},{14,22},{16,8},... | collective-permute-start | bytes 331784 | tf_op jit(solution)/shard_map/ppermute | solution.py:832
  222.7 17.6 %collective-permute-start.22 = (bf16[16,40,768]{2,1,0:T(8,128)(2,1)S(1)}, bf16[16,40,768]{2,1,0:T(8,128)(2,1)S(1)}, u32[]{:S(2)}, u32[]{:S(2)}) collective-permute-start(bf16[16,40,768]{2,1,0:T(8,128)(2,1)S(1)} %all-to-all-done.3.mine_ref), channel_id=1, source_target_pairs={{0,1},{1,0},{2,3},{3,2},{4,5},{5,4},{6,7},{7,6},{8,9},{9,8},{10,11... | collective-permute-start | bytes 2949128 | tf_op jit(solution)/shard_map/ppermute | solution.py:28
  (40 other events, 277.2 us)
